TPU v7x, 256 devices: a whole 4x4x8 slice. The times are simulated.
256 devices in a mesh: claim: 64 (over y_hi, x, z), feat: 4 (over y_lo, core).
Axes of the slice: x: 4, y: 4 (y_hi: 2, y_lo: 2; y = y_hi * 2 + y_lo), z: 8, core: 2. Of those that a mesh axis runs over, the one named last changes fastest.
Arguments:
- block_tiles: bfloat16 [64, 4, 128, 128, 128], P('claim', 'feat'), may hold values from 0.049804688 to 1
- block_scale: float32 [64, 4, 128], P('claim', 'feat'), may hold values from 1 to 12, as said below
- row_index: int32 [64, 4, 128], P('claim', 'feat'), may hold values from 0 to 63
- col_index: int32 [64, 4, 128], P('claim', 'feat'), may hold values from 0 to 31
- start_basis: float32 [16384, 64], P('feat'), may hold values from -6 to 6
Outputs:
- claim_basis: float32 [524288, 64], P(('claim', 'feat'))
- feature_basis: float32 [16384, 64], P(('feat', 'claim'))
- bidiagonal: float32 [4, 64, 64], replicated
Inputs may be any that keep to these rules, and one draw needn't show every extreme that they name: `row_index`: row block within the device's 64 row blocks of claims; a few row blocks hold most stored blocks. `col_index`: column block within the device's 32 column blocks. `block_scale`: positive block scales.
All inputs are finite; a program needn't handle non-finite values.
Results may differ from a plain program's by a relative error of at most 0.012.
Values may be sent and summed in bfloat16 or wider, within the bound.
A program may use at most 64 MiB of HBM per device.

v0:
```python
import jax
import jax.numpy as jnp
from jax import lax
from jax.sharding import PartitionSpec as P

BLK_ROWS = 64


HIGH = lax.Precision.HIGHEST


def forward_local(block_tiles, block_scale, row_index, col_index, operand):
    edge = block_tiles.shape[-1]
    width = operand.shape[-1]
    picked = operand.reshape(-1, edge, width)[col_index]
    products = jnp.einsum("bij,bjk->bik", block_tiles, picked, preferred_element_type=jnp.float32)
    products = products * block_scale[:, None, None]
    selector = (row_index[None, :] == jnp.arange(BLK_ROWS, dtype=jnp.int32)[:, None]).astype(
        jnp.float32
    )
    summed = jnp.einsum("rb,bik->rik", selector, products, precision=HIGH)
    return summed.reshape(BLK_ROWS * edge, width)


def backward_local(block_tiles, block_scale, row_index, col_index, operand, col_count):
    edge = block_tiles.shape[-1]
    width = operand.shape[-1]
    picked = operand.reshape(-1, edge, width)[row_index]
    products = jnp.einsum("bij,bik->bjk", block_tiles, picked, preferred_element_type=jnp.float32)
    products = products * block_scale[:, None, None]
    selector = (col_index[None, :] == jnp.arange(col_count, dtype=jnp.int32)[:, None]).astype(
        jnp.float32
    )
    summed = jnp.einsum("cb,bjk->cjk", selector, products, precision=HIGH)
    return summed.reshape(col_count * edge, width)


def degree_local(block_tiles, block_scale, row_index, col_index, col_count):
    row_sums = jnp.sum(block_tiles, axis=2, dtype=jnp.float32) * block_scale[:, None]
    col_sums = jnp.sum(block_tiles, axis=1, dtype=jnp.float32) * block_scale[:, None]
    row_select = (row_index[None, :] == jnp.arange(BLK_ROWS, dtype=jnp.int32)[:, None]).astype(
        jnp.float32
    )
    col_select = (col_index[None, :] == jnp.arange(col_count, dtype=jnp.int32)[:, None]).astype(
        jnp.float32
    )
    row_part = jnp.einsum("rb,bi->ri", row_select, row_sums, precision=HIGH).reshape(-1)
    col_part = jnp.einsum("cb,bi->ci", col_select, col_sums, precision=HIGH).reshape(-1)
    return (row_part, col_part)


def gram_of(block):
    return jnp.dot(block.T, block, precision=HIGH)


def orthonormal(block, gram_total):
    factor = jnp.linalg.cholesky(gram_total)
    basis = lax.linalg.triangular_solve(
        factor, block, left_side=False, lower=True, transpose_a=True
    )
    return (basis, factor.T)


def per_device(block_tiles, block_scale, row_index, col_index, start_basis):
    tiles_here = block_tiles.reshape(block_tiles.shape[2:])
    scale_here = block_scale.reshape(-1)
    rows_here = row_index.reshape(-1)
    cols_here = col_index.reshape(-1)
    edge = tiles_here.shape[-1]
    col_count = start_basis.shape[0] // edge
    claim_count = lax.axis_size("claim")
    own_cols = start_basis.shape[0] // claim_count
    own_first = lax.axis_index("claim") * own_cols
    row_part, col_part = degree_local(tiles_here, scale_here, rows_here, cols_here, col_count)
    col_total = lax.psum(col_part, "claim")
    col_scale = lax.rsqrt(col_total + 1.0)
    row_total = lax.psum_scatter(row_part, "feat", scatter_dimension=0, tiled=True)
    start_total = lax.psum(gram_of(start_basis), "feat")
    first_basis, _ = orthonormal(start_basis, start_total)
    first_operand = (col_scale[:, None] * first_basis).astype(jnp.bfloat16)
    first_partial = forward_local(tiles_here, scale_here, rows_here, cols_here, first_operand)
    first_sums = lax.psum_scatter(first_partial, "feat", scatter_dimension=0, tiled=True)
    row_scale = lax.rsqrt(row_total + 1.0)

    def row_orthonormal(block):
        total = lax.psum(gram_of(block), ("claim", "feat"))
        return orthonormal(block, total)

    def backward_partial(basis):
        operand = (row_scale[:, None] * basis).astype(jnp.bfloat16)
        gathered = lax.all_gather(operand, "feat", axis=0, tiled=True)
        return backward_local(tiles_here, scale_here, rows_here, cols_here, gathered, col_count)

    def column_update(partial_value, previous, coupling):
        summed = lax.psum(partial_value, "claim")
        update = col_scale[:, None] * summed - jnp.dot(previous, coupling.T, precision=HIGH)
        total = lax.psum(gram_of(update), "feat")
        return orthonormal(update, total)

    u_first, b_first = row_orthonormal(row_scale[:, None] * first_sums)
    v_second, a_second = column_update(backward_partial(u_first), first_basis, b_first)
    scaled = (col_scale[:, None] * v_second).astype(jnp.bfloat16)
    second_partial = forward_local(tiles_here, scale_here, rows_here, cols_here, scaled)
    second_sums = lax.psum_scatter(second_partial, "feat", scatter_dimension=0, tiled=True)
    p_second = row_scale[:, None] * second_sums - jnp.dot(u_first, a_second.T, precision=HIGH)
    u_second, b_second = row_orthonormal(p_second)
    v_third, a_third = column_update(backward_partial(u_second), v_second, b_second)
    v_output = lax.dynamic_slice_in_dim(v_third, own_first, own_cols, 0)
    bidiagonal = jnp.stack([b_first, a_second, b_second, a_third])
    return (u_second, v_output, bidiagonal)


def solution(mesh):
    placed = (
        P("claim", "feat", None, None, None),
        P("claim", "feat", None),
        P("claim", "feat", None),
        P("claim", "feat", None),
        P("feat", None),
    )
    return jax.shard_map(
        per_device,
        mesh=mesh,
        in_specs=placed,
        out_specs=(P(("claim", "feat"), None), P(("feat", "claim"), None), P()),
        check_vma=False,
    )
```

profile of v0, /device:TPU:64, one launch (start us, length us, event | category | flops | bytes accessed | tf_op | source)
XLA Modules:
  0.0 2187.2 jit_solution(12832989908346976326)
XLA Ops:
  9.4 3.4 convert_reduce_fusion.1
  13.1 12.1 all-reduce.1
  25.2 5.8 cholesky.89
  32.4 4.9 custom-call.11
  38.6 353.9 %psum.56 = f32[4096]{0:T(1024)S(1)} all-reduce(f32[4096]{0:T(1024)S(1)} %convolution_bitcast_fusion.6), channel_id=1, replica_groups=mesh['claim'=64,'feat'=4] {'claim'}, use_global_device_ids=true, to_apply=%region_3.0 | all-reduce | flops 4096 | bytes 32768 | tf_op jit(solution)/shard_map/psum | solution.py:75
  394.8 5.8 multiply_bitcast_fusion.3
  400.6 4.2 fusion.14
  408.7 27.8 %reduce-scatter.3.cloned.1.call-done = f32[2048,64]{0,1:T(8,128)} async-done(((f32[8192,64]{0,1:T(8,128)}), f32[2048,64]{0,1:T(8,128)}) %reduce-scatter.3.cloned.1.call-update) | async-done | bytes 524304 | tf_op jit(solution)/shard_map/reduce_scatter | solution.py:82
  438.3 76.1 %psum.58 = f32[64,64]{0,1:T(8,128)S(1)} all-reduce(f32[64,64]{0,1:T(8,128)S(1)} %fusion.27), channel_id=1, replica_groups=mesh['claim'=64,'feat'=4] {'claim','feat'}, use_global_device_ids=true, to_apply=%region_8.11 | all-reduce | flops 4096 | bytes 32768 | tf_op jit(solution)/shard_map/psum | solution.py:86
  514.5 5.8 cholesky.100
  521.7 4.9 custom-call.12
  529.5 20.7 all-gather.3.cloned.1.call-done
  553.8 4.0 multiply_bitcast_fusion.2
  557.9 3.9 fusion.12
  563.5 693.6 %all-reduce.5.cloned.1.call-done = f32[4096,64]{0,1:T(8,128)} async-done(((f32[4096,64]{0,1:T(8,128)}), f32[4096,64]{0,1:T(8,128)}) %all-reduce.5.cloned.1.call-update) | async-done | bytes 1048592 | tf_op jit(solution)/shard_map/psum | solution.py:95
  1257.2 2.9 convolution_subtract_fusion.1
  1261.1 11.0 psum.60
  1272.2 5.8 cholesky.111
  1279.3 4.9 custom-call.13
  1287.6 5.8 multiply_bitcast_fusion.1
  1293.4 4.2 fusion.10
  1300.2 29.6 %reduce-scatter.5.cloned.1.call-done = f32[2048,64]{0,1:T(8,128)} async-done(((f32[8192,64]{0,1:T(8,128)}), f32[2048,64]{0,1:T(8,128)}) %reduce-scatter.5.cloned.1.call-update) | async-done | bytes 524304 | tf_op jit(solution)/shard_map/reduce_scatter | solution.py:104
  1332.7 76.3 %psum.61 = f32[64,64]{0,1:T(8,128)S(1)} all-reduce(f32[64,64]{0,1:T(8,128)S(1)} %fusion.98), channel_id=1, replica_groups=mesh['claim'=64,'feat'=4] {'claim','feat'}, use_global_device_ids=true, to_apply=%region_12.16 | all-reduce | flops 4096 | bytes 32768 | tf_op jit(solution)/shard_map/psum | solution.py:86
  1409.1 5.8 cholesky.122
  1416.3 4.9 custom-call.14
  1422.8 20.9 all-gather.5.cloned.1.call-done
  1447.3 4.0 multiply_bitcast_fusion
  1451.4 3.9 fusion.8
  1457.0 693.7 %all-reduce.7.cloned.1.call-done = f32[4096,64]{0,1:T(8,128)} async-done(((f32[4096,64]{0,1:T(8,128)}), f32[4096,64]{0,1:T(8,128)}) %all-reduce.7.cloned.1.call-update) | async-done | bytes 1048592 | tf_op jit(solution)/shard_map/psum | solution.py:95
  2154.6 10.8 psum.63
  2165.5 5.8 cholesky.133
  2172.6 4.9 custom-call.15
  (86 shorter events, 49.5 us)
Async XLA Ops:
  7.2 1.2 copy-start
  7.2 5.6 copy-start.2
  7.2 5.6 copy-start.3
  7.2 31.2 %copy-start.4 = (s32[1,1,128]{2,1,0:T(1,128)S(1)}, s32[1,1,128]{2,1,0:T(1,128)}, u32[]{:S(2)}) copy-start(s32[1,1,128]{2,1,0:T(1,128)} %param.13) | copy-start | bytes 1540
  7.2 429.3 %reduce-scatter.3.cloned.1.call-start = ((), (), s32[]{:S(2)}) async-start(), calls=%async_computation.2 | async-start | bytes 2621440 | tf_op jit(solution)/shard_map/reduce_scatter | solution.py:82
  404.8 2.6 copy-start.5
  407.4 142.8 %all-gather.3.cloned.1.call-start = ((), (), s32[]{:S(2)}) async-start(), calls=%async_computation.3 | async-start | bytes 1310720 | tf_op jit(solution)/shard_map/all_gather | solution.py:91
  529.2 728.0 %all-reduce.5.cloned.1.call-start = ((), (), s32[]{:S(2)}) async-start(), calls=%async_computation.4 | async-start | bytes 2097152 | tf_op jit(solution)/shard_map/psum | solution.py:95
  563.5 766.3 %reduce-scatter.5.cloned.1.call-start = ((), (), s32[]{:S(2)}) async-start(), calls=%async_computation.5 | async-start | bytes 2621440 | tf_op jit(solution)/shard_map/reduce_scatter | solution.py:104
  1297.6 32.2 %copy-start.1 = (f32[2048,64]{0,1:T(8,128)S(1)}, f32[2048,64]{0,1:T(8,128)}, u32[]{:S(2)}) copy-start(f32[2048,64]{0,1:T(8,128)} %get-tuple-element.28) | copy-start | bytes 1572868
  1300.1 143.5 %all-gather.5.cloned.1.call-start = ((), (), s32[]{:S(2)}) async-start(), calls=%async_computation.6 | async-start | bytes 1310720 | tf_op jit(solution)/shard_map/all_gather | solution.py:91
  1422.7 727.9 %all-reduce.7.cloned.1.call-start = ((), (), s32[]{:S(2)}) async-start(), calls=%async_computation.7 | async-start | bytes 2097152 | tf_op jit(solution)/shard_map/psum | solution.py:95
Sparse Core Ops, SparseCore 0:
  407.5 28.9 reduce-scatter.2
  529.3 20.7 all-gather.2
  563.6 693.5 all-reduce.4
  1300.3 29.4 reduce-scatter.4
  1422.9 20.7 all-gather.4
  1457.1 693.4 all-reduce.6
where the time goes:
time: 2200 us; the launch traced here: 2190 us
  waiting for transfers between devices  1490 us (68%)
  blocking collectives  540 us (25%)
  other arithmetic  64.1 us (3%)
  matrix products  57 us (3%)
  local copies, waits for them, and re-layouts  23.7 us (1%)
    psum x2, waiting for transfers between devices, column_update(): summed = lax.psum(partial_value, 'claim')  1390 us
    psum x1, blocking collectives, per_device(): col_total = lax.psum(col_part, 'claim')  354 us
    psum x2, blocking collectives, row_orthonormal(): total = lax.psum(gram_of(block), ('claim', 'feat'))  152 us
  transfers between devices with their start and end apart: 6, of which 6 were waited for; matrix products, arithmetic and copies ran while one was open for 0% of the time, Pallas kernels for 0%

commit v1 on v0

--- a/solution.py
+++ b/solution.py
@@ -1,12 +1,16 @@
 import jax
 import jax.numpy as jnp
 from jax import lax
+from jax.sharding import Mesh
 from jax.sharding import PartitionSpec as P
 
 BLK_ROWS = 64
 
+HIGH = lax.Precision.HIGHEST
 
-HIGH = lax.Precision.HIGHEST
+FINE = ("yh", "x", "z", "yl", "c")
+CLAIM = ("yh", "x", "z")
+FEAT = ("yl", "c")
 
 
 def forward_local(block_tiles, block_scale, row_index, col_index, operand):
@@ -61,67 +65,88 @@
     return (basis, factor.T)
 
 
+def claim_sum(value):
+    part = lax.psum_scatter(value, "z", scatter_dimension=0, tiled=True)
+    part = lax.psum(part, ("yh", "x"))
+    return lax.all_gather(part, "z", axis=0, tiled=True)
+
+
+def all_sum(value):
+    value = lax.psum(value, FEAT)
+    value = lax.psum(value, "z")
+    return lax.psum(value, ("yh", "x"))
+
+
+def claim_scatter(value):
+    size_z = lax.axis_size("z")
+    size_o = lax.axis_size("yh") * lax.axis_size("x")
+    rows = value.shape[0] // (size_z * size_o)
+    blocks = value.reshape(size_o, size_z, rows, -1).transpose(1, 0, 2, 3).reshape(value.shape)
+    part = lax.psum_scatter(blocks, "z", scatter_dimension=0, tiled=True)
+    return lax.psum_scatter(part, ("yh", "x"), scatter_dimension=0, tiled=True)
+
+
 def per_device(block_tiles, block_scale, row_index, col_index, start_basis):
-    tiles_here = block_tiles.reshape(block_tiles.shape[2:])
+    tiles_here = block_tiles.reshape(block_tiles.shape[-3:])
     scale_here = block_scale.reshape(-1)
     rows_here = row_index.reshape(-1)
     cols_here = col_index.reshape(-1)
     edge = tiles_here.shape[-1]
     col_count = start_basis.shape[0] // edge
-    claim_count = lax.axis_size("claim")
+    claim_count = lax.axis_size(CLAIM)
     own_cols = start_basis.shape[0] // claim_count
-    own_first = lax.axis_index("claim") * own_cols
+    own_first = lax.axis_index(CLAIM) * own_cols
     row_part, col_part = degree_local(tiles_here, scale_here, rows_here, cols_here, col_count)
-    col_total = lax.psum(col_part, "claim")
+    col_total = claim_sum(col_part)
     col_scale = lax.rsqrt(col_total + 1.0)
-    row_total = lax.psum_scatter(row_part, "feat", scatter_dimension=0, tiled=True)
-    start_total = lax.psum(gram_of(start_basis), "feat")
+    row_total = lax.psum_scatter(row_part, FEAT, scatter_dimension=0, tiled=True)
+    start_total = lax.psum(gram_of(start_basis), FEAT)
     first_basis, _ = orthonormal(start_basis, start_total)
     first_operand = (col_scale[:, None] * first_basis).astype(jnp.bfloat16)
     first_partial = forward_local(tiles_here, scale_here, rows_here, cols_here, first_operand)
-    first_sums = lax.psum_scatter(first_partial, "feat", scatter_dimension=0, tiled=True)
+    first_sums = lax.psum_scatter(first_partial, FEAT, scatter_dimension=0, tiled=True)
     row_scale = lax.rsqrt(row_total + 1.0)
 
     def row_orthonormal(block):
-        total = lax.psum(gram_of(block), ("claim", "feat"))
-        return orthonormal(block, total)
+        return orthonormal(block, all_sum(gram_of(block)))
 
     def backward_partial(basis):
         operand = (row_scale[:, None] * basis).astype(jnp.bfloat16)
-        gathered = lax.all_gather(operand, "feat", axis=0, tiled=True)
+        gathered = lax.all_gather(operand, FEAT, axis=0, tiled=True)
         return backward_local(tiles_here, scale_here, rows_here, cols_here, gathered, col_count)
 
-    def column_update(partial_value, previous, coupling):
-        summed = lax.psum(partial_value, "claim")
-        update = col_scale[:, None] * summed - jnp.dot(previous, coupling.T, precision=HIGH)
-        total = lax.psum(gram_of(update), "feat")
-        return orthonormal(update, total)
-
     u_first, b_first = row_orthonormal(row_scale[:, None] * first_sums)
-    v_second, a_second = column_update(backward_partial(u_first), first_basis, b_first)
+    summed = claim_sum(backward_partial(u_first))
+    update = col_scale[:, None] * summed - jnp.dot(first_basis, b_first.T, precision=HIGH)
+    v_second, a_second = orthonormal(update, lax.psum(gram_of(update), FEAT))
     scaled = (col_scale[:, None] * v_second).astype(jnp.bfloat16)
     second_partial = forward_local(tiles_here, scale_here, rows_here, cols_here, scaled)
-    second_sums = lax.psum_scatter(second_partial, "feat", scatter_dimension=0, tiled=True)
+    second_sums = lax.psum_scatter(second_partial, FEAT, scatter_dimension=0, tiled=True)
     p_second = row_scale[:, None] * second_sums - jnp.dot(u_first, a_second.T, precision=HIGH)
     u_second, b_second = row_orthonormal(p_second)
-    v_third, a_third = column_update(backward_partial(u_second), v_second, b_second)
-    v_output = lax.dynamic_slice_in_dim(v_third, own_first, own_cols, 0)
+    own_sums = claim_scatter(backward_partial(u_second))
+    own_scale = lax.dynamic_slice_in_dim(col_scale, own_first, own_cols, 0)
+    own_second = lax.dynamic_slice_in_dim(v_second, own_first, own_cols, 0)
+    q_second = own_scale[:, None] * own_sums - jnp.dot(own_second, b_second.T, precision=HIGH)
+    v_output, a_third = orthonormal(q_second, all_sum(gram_of(q_second)))
     bidiagonal = jnp.stack([b_first, a_second, b_second, a_third])
     return (u_second, v_output, bidiagonal)
 
 
 def solution(mesh):
+    claim_n, feat_n = mesh.devices.shape
+    fine = Mesh(mesh.devices.reshape(2, claim_n // 16, 8, 2, feat_n // 2), FINE)
     placed = (
-        P("claim", "feat", None, None, None),
-        P("claim", "feat", None),
-        P("claim", "feat", None),
-        P("claim", "feat", None),
-        P("feat", None),
+        P(CLAIM, FEAT, None, None, None),
+        P(CLAIM, FEAT, None),
+        P(CLAIM, FEAT, None),
+        P(CLAIM, FEAT, None),
+        P(FEAT, None),
     )
     return jax.shard_map(
         per_device,
-        mesh=mesh,
+        mesh=fine,
         in_specs=placed,
-        out_specs=(P(("claim", "feat"), None), P(("feat", "claim"), None), P()),
+        out_specs=(P(CLAIM + FEAT, None), P(FEAT + CLAIM, None), P()),
         check_vma=False,
     )

time: 2200 us -> 890 us (0.40)
  waiting for transfers between devices: 1490 us -> 384 us
  blocking collectives: 540 us -> 336 us
    psum x2 -> x1, waiting for transfers between devices: 1390 us -> 91.8 us  [claim_sum(): part = lax.psum(part, ('yh', 'x'))]
    psum x6 -> x12, blocking collectives: 540 us -> 284 us  [the longest x3 123 us: all_sum(): return lax.psum(value, ('yh', 'x'))]
    reduce_scatter x2 -> x5, waiting for transfers between devices: 57.4 us -> 215 us  [the longest x1 79.6 us: claim_scatter(): return lax.psum_scatter(part, ('yh', 'x'), scatter_dimension=0, tiled=True)]
    all_gather x2 -> x3, waiting for transfers between devices: 41.5 us -> 76.8 us  [the longest x2 40 us: backward_partial(): gathered = lax.all_gather(operand, FEAT, axis=0, tiled=True)]
    unnamed x0 -> x1, blocking collectives: none -> 29.8 us
    all_gather x0 -> x1, blocking collectives: none -> 22 us  [claim_sum(): return lax.all_gather(part, 'z', axis=0, tiled=True)]
  transfers between devices with their start and end apart: 6 -> 9, of which waited for: 6 -> 9; matrix products, arithmetic and copies ran while one was open for 0% -> 0% of each run, Pallas kernels for 0% -> 0%
where the time goes in v1:
time: 890 us; the launch traced here: 883 us
  waiting for transfers between devices  384 us (43%)
  blocking collectives  336 us (38%)
  other arithmetic  64.9 us (7%)
  matrix products  55.8 us (6%)
  local copies, waits for them, and re-layouts  26.1 us (3%)
  between operations  15.8 us (2%)
    psum x3, blocking collectives, all_sum(): return lax.psum(value, ('yh', 'x'))  123 us
    psum x1, waiting for transfers between devices, claim_sum(): part = lax.psum(part, ('yh', 'x'))  91.8 us
    psum x3, blocking collectives, all_sum(): value = lax.psum(value, 'z')  83.8 us
    reduce_scatter x1, waiting for transfers between devices, claim_scatter(): return lax.psum_scatter(part, ('yh', 'x'), scatter_dimension=0, tiled=True)  79.6 us
    reduce_scatter x1, waiting for transfers between devices, claim_scatter(): part = lax.psum_scatter(blocks, 'z', scatter_dimension=0, tiled=True)  41.8 us
    all_gather x2, waiting for transfers between devices, backward_partial(): gathered = lax.all_gather(operand, FEAT, axis=0, tiled=True)  40 us
    reduce_scatter x1, waiting for transfers between devices, claim_sum(): part = lax.psum_scatter(value, 'z', scatter_dimension=0, tiled=True)  38.3 us
    all_gather x1, waiting for transfers between devices, claim_sum(): return lax.all_gather(part, 'z', axis=0, tiled=True)  36.8 us
  transfers between devices with their start and end apart: 9, of which 9 were waited for; matrix products, arithmetic and copies ran while one was open for 0% of the time, Pallas kernels for 0%

profile of v1, /device:TPU:64, one launch (start us, length us, event | category | flops | bytes accessed | tf_op | source)
XLA Modules:
  0.0 883.2 jit_solution(7263501189897861546)
XLA Ops:
  13.1 29.8 %all-reduce.1 = f32[4096]{0:T(1024)S(1)} all-reduce(f32[4096]{0:T(1024)S(1)} %convolution_bitcast_fusion.5), channel_id=3, replica_groups=mesh['yh'=2,'x'=4,'z'=8,'yl'=2,'c'=2] {'z'}, use_global_device_ids=true, to_apply=%region_3.0.clone | all-reduce | flops 4096 | bytes 32768
  44.1 24.3 %psum.91 = f32[512]{0:T(512)S(1)} all-reduce(f32[512]{0:T(512)S(1)} %dynamic-slice.3), channel_id=1, replica_groups=mesh['yh'=2,'x'=4,'z'=8,'yl'=2,'c'=2] {'yh','x'}, use_global_device_ids=true, to_apply=%region_4.0 | all-reduce | flops 512 | bytes 4096 | tf_op jit(solution)/shard_map/psum | solution.py:70
  68.5 22.0 %all-gather = f32[8,1,512]{2,1,0:T(1,128)S(1)} all-gather(f32[1,1,512]{2,1,0:T(1,128)S(1)} %bitcast.205), channel_id=1, replica_groups=mesh['yh'=2,'x'=4,'z'=8,'yl'=2,'c'=2] {'z'}, dimensions={0}, use_global_device_ids=true | all-gather | bytes 18432 | tf_op jit(solution)/shard_map/all_gather | solution.py:71
  90.8 11.3 %all-reduce.2 = (f32[64,64]{0,1:T(8,128)S(1)}, f32[8192]{0:T(1024)S(1)}) all-reduce(f32[64,64]{0,1:T(8,128)S(1)} %fusion.101, f32[8192]{0:T(1024)S(1)} %convolution_bitcast_fusion.4), channel_id=1, replica_groups=mesh['yh'=2,'x'=4,'z'=8,'yl'=2,'c'=2] {'yl','c'}, use_global_device_ids=true, to_apply=%region_5.0 | all-reduce | flops 12288 | bytes 98304 | tf_op jit(solution)/shard_map/psum | solution.py:103
  102.2 5.8 cholesky.89
  109.3 4.9 custom-call.14
  117.6 5.8 multiply_bitcast_fusion.3
  131.5 24.8 %reduce-scatter.6.cloned.1.call-done = f32[2048,64]{0,1:T(8,128)} async-done(((f32[8192,64]{0,1:T(8,128)}), f32[2048,64]{0,1:T(8,128)}) %reduce-scatter.6.cloned.1.call-update) | async-done | bytes 524304 | tf_op jit(solution)/shard_map/reduce_scatter | solution.py:107
  158.1 10.4 %psum.93 = f32[64,64]{0,1:T(8,128)S(1)} all-reduce(f32[64,64]{0,1:T(8,128)S(1)} %fusion.27), channel_id=1, replica_groups=mesh['yh'=2,'x'=4,'z'=8,'yl'=2,'c'=2] {'yl','c'}, use_global_device_ids=true, to_apply=%region_9.12 | all-reduce | flops 4096 | bytes 32768 | tf_op jit(solution)/shard_map/psum | solution.py:75
  168.5 27.9 %psum.94 = f32[64,64]{0,1:T(8,128)S(1)} all-reduce(f32[64,64]{0,1:T(8,128)S(1)} %psum.93), channel_id=1, replica_groups=mesh['yh'=2,'x'=4,'z'=8,'yl'=2,'c'=2] {'z'}, use_global_device_ids=true, to_apply=%region_10.13 | all-reduce | flops 4096 | bytes 32768 | tf_op jit(solution)/shard_map/psum | solution.py:76
  196.5 42.0 %psum.95 = f32[64,64]{0,1:T(8,128)S(1)} all-reduce(f32[64,64]{0,1:T(8,128)S(1)} %psum.94), channel_id=1, replica_groups=mesh['yh'=2,'x'=4,'z'=8,'yl'=2,'c'=2] {'yh','x'}, use_global_device_ids=true, to_apply=%region_11.14 | all-reduce | flops 4096 | bytes 32768 | tf_op jit(solution)/shard_map/psum | solution.py:77
  238.5 5.8 cholesky.100
  253.3 20.0 %all-gather.5.cloned.1.call-done = bf16[8192,64]{0,1:T(8,128)(2,1)} async-done(((bf16[2048,64]{0,1:T(8,128)(2,1)}), bf16[8192,64]{0,1:T(8,128)(2,1)}) %all-gather.5.cloned.1.call-update) | async-done | bytes 1048592 | tf_op jit(solution)/shard_map/all_gather | solution.py:115
  286.6 38.3 %reduce-scatter.8.cloned.1.call-done = f32[512,64]{0,1:T(8,128)} async-done(((f32[4096,64]{0,1:T(8,128)}), f32[512,64]{0,1:T(8,128)}) %reduce-scatter.8.cloned.1.call-update) | async-done | bytes 131088 | tf_op jit(solution)/shard_map/reduce_scatter | solution.py:69
  325.0 91.8 %all-reduce.5.cloned.1.call-done = f32[512,64]{0,1:T(8,128)} async-done(((f32[512,64]{0,1:T(8,128)}), f32[512,64]{0,1:T(8,128)}) %all-reduce.5.cloned.1.call-update) | async-done | bytes 131088 | tf_op jit(solution)/shard_map/psum | solution.py:70
  416.9 36.8 %all-gather.7.cloned.1.call-done = f32[4096,64]{0,1:T(8,128)} async-done(((f32[512,64]{0,1:T(8,128)}), f32[4096,64]{0,1:T(8,128)}) %all-gather.7.cloned.1.call-update) | async-done | bytes 1048592 | tf_op jit(solution)/shard_map/all_gather | solution.py:71
  457.6 10.7 %psum.97 = f32[64,64]{0,1:T(8,128)S(1)} all-reduce(f32[64,64]{0,1:T(8,128)S(1)} %fusion.102), channel_id=1, replica_groups=mesh['yh'=2,'x'=4,'z'=8,'yl'=2,'c'=2] {'yl','c'}, use_global_device_ids=true, to_apply=%region_14.18 | all-reduce | flops 4096 | bytes 32768 | tf_op jit(solution)/shard_map/psum | solution.py:121
  468.3 5.8 cholesky.111
  484.8 5.8 multiply_bitcast_fusion.1
  497.4 30.8 %reduce-scatter.10.cloned.1.call-done = f32[2048,64]{0,1:T(8,128)} async-done(((f32[8192,64]{0,1:T(8,128)}), f32[2048,64]{0,1:T(8,128)}) %reduce-scatter.10.cloned.1.call-update) | async-done | bytes 524304 | tf_op jit(solution)/shard_map/reduce_scatter | solution.py:124
  531.1 10.4 %psum.98 = f32[64,64]{0,1:T(8,128)S(1)} all-reduce(f32[64,64]{0,1:T(8,128)S(1)} %fusion.103), channel_id=1, replica_groups=mesh['yh'=2,'x'=4,'z'=8,'yl'=2,'c'=2] {'yl','c'}, use_global_device_ids=true, to_apply=%region_16.20 | all-reduce | flops 4096 | bytes 32768 | tf_op jit(solution)/shard_map/psum | solution.py:75
  541.5 27.9 %psum.99 = f32[64,64]{0,1:T(8,128)S(1)} all-reduce(f32[64,64]{0,1:T(8,128)S(1)} %psum.98), channel_id=1, replica_groups=mesh['yh'=2,'x'=4,'z'=8,'yl'=2,'c'=2] {'z'}, use_global_device_ids=true, to_apply=%region_17.21 | all-reduce | flops 4096 | bytes 32768 | tf_op jit(solution)/shard_map/psum | solution.py:76
  569.4 41.9 %psum.100 = f32[64,64]{0,1:T(8,128)S(1)} all-reduce(f32[64,64]{0,1:T(8,128)S(1)} %psum.99), channel_id=1, replica_groups=mesh['yh'=2,'x'=4,'z'=8,'yl'=2,'c'=2] {'yh','x'}, use_global_device_ids=true, to_apply=%region_18.22 | all-reduce | flops 4096 | bytes 32768 | tf_op jit(solution)/shard_map/psum | solution.py:77
  611.5 5.8 cholesky.122
  625.1 20.0 %all-gather.9.cloned.1.call-done = bf16[8192,64]{0,1:T(8,128)(2,1)} async-done(((bf16[2048,64]{0,1:T(8,128)(2,1)}), bf16[8192,64]{0,1:T(8,128)(2,1)}) %all-gather.9.cloned.1.call-update) | async-done | bytes 1048592 | tf_op jit(solution)/shard_map/all_gather | solution.py:115
  652.9 4.9 fusion.8
  661.8 41.8 %reduce-scatter.12.cloned.1.call-done = f32[512,64]{1,0:T(8,128)} async-done(((f32[4096,64]{1,0:T(8,128)}), f32[512,64]{1,0:T(8,128)}) %reduce-scatter.12.cloned.1.call-update) | async-done | bytes 131088 | tf_op jit(solution)/shard_map/reduce_scatter | solution.py:85
  703.7 79.6 %reduce-scatter.14.cloned.1.call-done = f32[64,64]{1,0:T(8,128)} async-done(((f32[512,64]{1,0:T(8,128)}), f32[64,64]{1,0:T(8,128)}) %reduce-scatter.14.cloned.1.call-update) | async-done | bytes 16400 | tf_op jit(solution)/shard_map/reduce_scatter | solution.py:86
  785.3 10.3 %psum.101 = f32[64,64]{0,1:T(8,128)S(1)} all-reduce(f32[64,64]{0,1:T(8,128)S(1)} %fusion.104), channel_id=1, replica_groups=mesh['yh'=2,'x'=4,'z'=8,'yl'=2,'c'=2] {'yl','c'}, use_global_device_ids=true, to_apply=%region_21.25 | all-reduce | flops 4096 | bytes 32768 | tf_op jit(solution)/shard_map/psum | solution.py:75
  795.6 28.0 %psum.102 = f32[64,64]{0,1:T(8,128)S(1)} all-reduce(f32[64,64]{0,1:T(8,128)S(1)} %psum.101), channel_id=1, replica_groups=mesh['yh'=2,'x'=4,'z'=8,'yl'=2,'c'=2] {'z'}, use_global_device_ids=true, to_apply=%region_22.26 | all-reduce | flops 4096 | bytes 32768 | tf_op jit(solution)/shard_map/psum | solution.py:76
  823.5 39.2 %psum.103 = f32[64,64]{0,1:T(8,128)S(1)} all-reduce(f32[64,64]{0,1:T(8,128)S(1)} %psum.102), channel_id=1, replica_groups=mesh['yh'=2,'x'=4,'z'=8,'yl'=2,'c'=2] {'yh','x'}, use_global_device_ids=true, to_apply=%region_23.27 | all-reduce | flops 4096 | bytes 32768 | tf_op jit(solution)/shard_map/psum | solution.py:77
  862.8 5.8 cholesky.133
  (109 shorter events, 96.7 us)
Async XLA Ops:
  7.2 1.3 copy-start
  7.2 35.6 %copy-start.7 = (u32[256]{0:T(256)S(1)}, u32[256]{0:T(256)}, u32[]{:S(2)}) copy-start(u32[256]{0:T(256)} %constant.80) | copy-start | bytes 3076
  7.2 5.7 copy-start.5
  7.2 5.7 copy-start.3
  7.2 83.3 %copy-start.4 = (s32[1,1,128]{2,1,0:T(1,128)S(1)}, s32[1,1,128]{2,1,0:T(1,128)}, u32[]{:S(2)}) copy-start(s32[1,1,128]{2,1,0:T(1,128)} %param.12) | copy-start | bytes 1540
  7.2 149.1 %reduce-scatter.6.cloned.1.call-start = ((), (), s32[]{:S(2)}) async-start(), calls=%async_computation.5 | async-start | bytes 2621440 | tf_op jit(solution)/shard_map/reduce_scatter | solution.py:107
  127.6 2.6 copy-start.6
  130.2 143.1 %all-gather.5.cloned.1.call-start = ((), (), s32[]{:S(2)}) async-start(), calls=%async_computation.6 | async-start | bytes 1310720 | tf_op jit(solution)/shard_map/all_gather | solution.py:115
  253.2 71.7 %reduce-scatter.8.cloned.1.call-start = ((), (), s32[]{:S(2)}) async-start(), calls=%async_computation.7 | async-start | bytes 1179648 | tf_op jit(solution)/shard_map/reduce_scatter | solution.py:69
  286.6 130.2 %all-reduce.5.cloned.1.call-start = ((), (), s32[]{:S(2)}) async-start(), calls=%async_computation.8 | async-start | bytes 262144 | tf_op jit(solution)/shard_map/psum | solution.py:70
  325.0 128.7 %all-gather.7.cloned.1.call-start = ((), (), s32[]{:S(2)}) async-start(), calls=%async_computation.9 | async-start | bytes 1179648 | tf_op jit(solution)/shard_map/all_gather | solution.py:71
  416.8 111.4 %reduce-scatter.10.cloned.1.call-start = ((), (), s32[]{:S(2)}) async-start(), calls=%async_computation.10 | async-start | bytes 2621440 | tf_op jit(solution)/shard_map/reduce_scatter | solution.py:124
  481.5 1.0 copy-start.1
  494.7 33.5 %copy-start.2 = (f32[2048,64]{0,1:T(8,128)S(1)}, f32[2048,64]{0,1:T(8,128)}, u32[]{:S(2)}) copy-start(f32[2048,64]{0,1:T(8,128)} %get-tuple-element.28) | copy-start | bytes 1572868
  497.3 147.9 %all-gather.9.cloned.1.call-start = ((), (), s32[]{:S(2)}) async-start(), calls=%async_computation.11 | async-start | bytes 1310720 | tf_op jit(solution)/shard_map/all_gather | solution.py:115
  625.1 78.5 %reduce-scatter.12.cloned.1.call-start = ((), (), s32[]{:S(2)}) async-start(), calls=%async_computation.12 | async-start | bytes 2359296 | tf_op jit(solution)/shard_map/reduce_scatter | solution.py:85
  661.7 121.6 %reduce-scatter.14.cloned.1.call-start = ((), (), s32[]{:S(2)}) async-start(), calls=%async_computation.13 | async-start | bytes 294912 | tf_op jit(solution)/shard_map/reduce_scatter | solution.py:86
Sparse Core Ops, SparseCore 0:
  130.3 25.9 reduce-scatter.5
  253.4 19.8 all-gather.4
  286.7 38.1 reduce-scatter.7
  327.6 89.1 all-reduce.4
  418.4 35.1 all-gather.6
  497.4 30.7 reduce-scatter.9
  625.2 19.9 all-gather.8
  661.8 41.6 reduce-scatter.11
  707.9 75.3 reduce-scatter.13

commit v2 on v1

--- a/solution.py
+++ b/solution.py
@@ -1,6 +1,10 @@
+import functools
+
 import jax
 import jax.numpy as jnp
 from jax import lax
+from jax.experimental import pallas as pl
+from jax.experimental.pallas import tpu as pltpu
 from jax.sharding import Mesh
 from jax.sharding import PartitionSpec as P
 
@@ -63,6 +67,57 @@
         factor, block, left_side=False, lower=True, transpose_a=True
     )
     return (basis, factor.T)
+
+
+def butterfly_kernel(stages, x_ref, o_ref, recv, send_sem, recv_sem):
+    coords = [lax.axis_index(name) for name in FINE]
+    partners = []
+    for axis, step in stages:
+        place = coords[axis]
+        flip = place + step * (1 - 2 * ((place // step) % 2))
+        partners.append(tuple(flip if i == axis else c for i, c in enumerate(coords)))
+    barrier = pltpu.get_barrier_semaphore()
+    for partner in partners:
+        pl.semaphore_signal(barrier, inc=1, device_id=partner, device_id_type=pl.DeviceIdType.MESH)
+    pl.semaphore_wait(barrier, len(partners))
+    o_ref[...] = x_ref[...]
+    for s, partner in enumerate(partners):
+        copy = pltpu.make_async_remote_copy(
+            src_ref=o_ref,
+            dst_ref=recv.at[s],
+            send_sem=send_sem.at[s],
+            recv_sem=recv_sem.at[s],
+            device_id=partner,
+            device_id_type=pl.DeviceIdType.MESH,
+        )
+        copy.start()
+        copy.wait()
+        o_ref[...] = o_ref[...] + recv[s]
+
+
+def butterfly_sum(value, names, cid):
+    stages = []
+    for name in names:
+        size = lax.axis_size(name)
+        step = 1
+        while step < size:
+            stages.append((FINE.index(name), step))
+            step *= 2
+    shape = value.shape
+    flat = value.reshape(-1, 128) if value.ndim == 1 else value
+    out = pl.pallas_call(
+        functools.partial(butterfly_kernel, tuple(stages)),
+        out_shape=jax.ShapeDtypeStruct(flat.shape, flat.dtype),
+        in_specs=[pl.BlockSpec(memory_space=pltpu.VMEM)],
+        out_specs=pl.BlockSpec(memory_space=pltpu.VMEM),
+        scratch_shapes=[
+            pltpu.VMEM((len(stages),) + flat.shape, flat.dtype),
+            pltpu.SemaphoreType.DMA((len(stages),)),
+            pltpu.SemaphoreType.DMA((len(stages),)),
+        ],
+        compiler_params=pltpu.CompilerParams(collective_id=cid, has_side_effects=True),
+    )(flat)
+    return out.reshape(shape)
 
 
 def claim_sum(value):
@@ -97,7 +152,7 @@
     own_cols = start_basis.shape[0] // claim_count
     own_first = lax.axis_index(CLAIM) * own_cols
     row_part, col_part = degree_local(tiles_here, scale_here, rows_here, cols_here, col_count)
-    col_total = claim_sum(col_part)
+    col_total = butterfly_sum(col_part, CLAIM, 0)
     col_scale = lax.rsqrt(col_total + 1.0)
     row_total = lax.psum_scatter(row_part, FEAT, scatter_dimension=0, tiled=True)
     start_total = lax.psum(gram_of(start_basis), FEAT)
@@ -107,15 +162,15 @@
     first_sums = lax.psum_scatter(first_partial, FEAT, scatter_dimension=0, tiled=True)
     row_scale = lax.rsqrt(row_total + 1.0)
 
-    def row_orthonormal(block):
-        return orthonormal(block, all_sum(gram_of(block)))
+    def row_orthonormal(block, cid):
+        return orthonormal(block, butterfly_sum(gram_of(block), FINE, cid))
 
     def backward_partial(basis):
         operand = (row_scale[:, None] * basis).astype(jnp.bfloat16)
         gathered = lax.all_gather(operand, FEAT, axis=0, tiled=True)
         return backward_local(tiles_here, scale_here, rows_here, cols_here, gathered, col_count)
 
-    u_first, b_first = row_orthonormal(row_scale[:, None] * first_sums)
+    u_first, b_first = row_orthonormal(row_scale[:, None] * first_sums, 1)
     summed = claim_sum(backward_partial(u_first))
     update = col_scale[:, None] * summed - jnp.dot(first_basis, b_first.T, precision=HIGH)
     v_second, a_second = orthonormal(update, lax.psum(gram_of(update), FEAT))
@@ -123,12 +178,12 @@
     second_partial = forward_local(tiles_here, scale_here, rows_here, cols_here, scaled)
     second_sums = lax.psum_scatter(second_partial, FEAT, scatter_dimension=0, tiled=True)
     p_second = row_scale[:, None] * second_sums - jnp.dot(u_first, a_second.T, precision=HIGH)
-    u_second, b_second = row_orthonormal(p_second)
+    u_second, b_second = row_orthonormal(p_second, 2)
     own_sums = claim_scatter(backward_partial(u_second))
     own_scale = lax.dynamic_slice_in_dim(col_scale, own_first, own_cols, 0)
     own_second = lax.dynamic_slice_in_dim(v_second, own_first, own_cols, 0)
     q_second = own_scale[:, None] * own_sums - jnp.dot(own_second, b_second.T, precision=HIGH)
-    v_output, a_third = orthonormal(q_second, all_sum(gram_of(q_second)))
+    v_output, a_third = orthonormal(q_second, butterfly_sum(gram_of(q_second), FINE, 3))
     bidiagonal = jnp.stack([b_first, a_second, b_second, a_third])
     return (u_second, v_output, bidiagonal)
 

time: 890 us -> 708 us (0.80)
  blocking collectives: 336 us -> 22.1 us
  Pallas kernels: 0 us -> 122 us
    psum x10 -> x0, blocking collectives: 262 us -> none  [the longest x3 123 us: all_sum(): return lax.psum(value, ('yh', 'x'))]
    pallas_call x0 -> x4, Pallas kernels: none -> 122 us  [butterfly_sum(): pl.pallas_call(functools.partial(butterfly_kernel, tuple(stages)), out_sh...]
    unnamed x1 -> x0, blocking collectives: 29.8 us -> none
    all_gather x1 -> x0, blocking collectives: 22 us -> none  [claim_sum(): return lax.all_gather(part, 'z', axis=0, tiled=True)]
where the time goes in v2:
time: 708 us; the launch traced here: 701 us
  waiting for transfers between devices  386 us (55%)
  Pallas kernels  122 us (17%)
  other arithmetic  67.9 us (10%)
  matrix products  58.2 us (8%)
  local copies, waits for them, and re-layouts  27.7 us (4%)
  blocking collectives  22.1 us (3%)
  between operations  15.4 us (2%)
    pallas_call x4, Pallas kernels, butterfly_sum(): pl.pallas_call(functools.partial(butterfly_kernel, tuple(stages)), out_sh...  122 us
    psum x1, waiting for transfers between devices, claim_sum(): part = lax.psum(part, ('yh', 'x'))  91.8 us
    reduce_scatter x1, waiting for transfers between devices, claim_scatter(): return lax.psum_scatter(part, ('yh', 'x'), scatter_dimension=0, tiled=True)  79.7 us
    reduce_scatter x1, waiting for transfers between devices, claim_scatter(): part = lax.psum_scatter(blocks, 'z', scatter_dimension=0, tiled=True)  41.5 us
    all_gather x2, waiting for transfers between devices, backward_partial(): gathered = lax.all_gather(operand, FEAT, axis=0, tiled=True)  41.3 us
    reduce_scatter x1, waiting for transfers between devices, claim_sum(): part = lax.psum_scatter(value, 'z', scatter_dimension=0, tiled=True)  38.3 us
    all_gather x1, waiting for transfers between devices, claim_sum(): return lax.all_gather(part, 'z', axis=0, tiled=True)  36.8 us
    another operation x15, other arithmetic, orthonormal(): factor = jnp.linalg.cholesky(gram_total)  32.6 us
  transfers between devices with their start and end apart: 9, of which 9 were waited for; matrix products, arithmetic and copies ran while one was open for 0% of the time, Pallas kernels for 0%

profile of v2, /device:TPU:64, one launch (start us, length us, event | category | flops | bytes accessed | tf_op | source)
XLA Modules:
  0.0 700.5 jit_solution(11168736802213740392)
XLA Ops:
  13.7 28.5 %shard_map.76 = f32[32,128]{1,0:T(8,128)} custom-call(f32[32,128]{1,0:T(8,128)} %fusion.31.x_ref), custom_call_target="tpu_custom_call" | custom-call | tf_op jit(solution)/shard_map/pallas_call | solution.py:108
  43.1 11.6 %all-reduce.1 = (f32[64,64]{0,1:T(8,128)S(1)}, f32[8192]{0:T(1024)S(1)}) all-reduce(f32[64,64]{0,1:T(8,128)S(1)} %fusion.102, f32[8192]{0:T(1024)S(1)} %convolution_bitcast_fusion.4), channel_id=1, replica_groups=mesh['yh'=2,'x'=4,'z'=8,'yl'=2,'c'=2] {'yl','c'}, use_global_device_ids=true, to_apply=%region_3.0 | all-reduce | flops 12288 | bytes 98304 | tf_op jit(solution)/shard_map/psum | solution.py:158
  54.9 5.8 cholesky.89
  62.1 4.9 custom-call.14
  70.3 5.8 multiply_bitcast_fusion.3
  76.1 4.2 fusion.14
  84.4 26.0 %reduce-scatter.6.cloned.1.call-done = f32[2048,64]{0,1:T(8,128)} async-done(((f32[8192,64]{0,1:T(8,128)}), f32[2048,64]{0,1:T(8,128)}) %reduce-scatter.6.cloned.1.call-update) | async-done | bytes 524304 | tf_op jit(solution)/shard_map/reduce_scatter | solution.py:162
  112.8 31.5 %shard_map.77 = f32[64,64]{1,0:T(8,128)} custom-call(f32[64,64]{1,0:T(8,128)} %fusion.27.x_ref), custom_call_target="tpu_custom_call" | custom-call | tf_op jit(solution)/shard_map/pallas_call | solution.py:108
  145.9 5.8 cholesky.100
  153.1 4.9 custom-call.15
  160.7 20.7 %all-gather.4.cloned.1.call-done = bf16[8192,64]{0,1:T(8,128)(2,1)} async-done(((bf16[2048,64]{0,1:T(8,128)(2,1)}), bf16[8192,64]{0,1:T(8,128)(2,1)}) %all-gather.4.cloned.1.call-update) | async-done | bytes 1048592 | tf_op jit(solution)/shard_map/all_gather | solution.py:170
  185.0 4.0 multiply_bitcast_fusion.2
  194.7 38.3 %reduce-scatter.8.cloned.1.call-done = f32[512,64]{0,1:T(8,128)} async-done(((f32[4096,64]{0,1:T(8,128)}), f32[512,64]{0,1:T(8,128)}) %reduce-scatter.8.cloned.1.call-update) | async-done | bytes 131088 | tf_op jit(solution)/shard_map/reduce_scatter | solution.py:124
  233.0 91.8 %all-reduce.4.cloned.1.call-done = f32[512,64]{0,1:T(8,128)} async-done(((f32[512,64]{0,1:T(8,128)}), f32[512,64]{0,1:T(8,128)}) %all-reduce.4.cloned.1.call-update) | async-done | bytes 131088 | tf_op jit(solution)/shard_map/psum | solution.py:125
  324.9 36.8 %all-gather.6.cloned.1.call-done = f32[4096,64]{0,1:T(8,128)} async-done(((f32[512,64]{0,1:T(8,128)}), f32[4096,64]{0,1:T(8,128)}) %all-gather.6.cloned.1.call-update) | async-done | bytes 1048592 | tf_op jit(solution)/shard_map/all_gather | solution.py:126
  365.6 10.5 %psum.23 = f32[64,64]{0,1:T(8,128)S(1)} all-reduce(f32[64,64]{0,1:T(8,128)S(1)} %fusion.103), channel_id=1, replica_groups=mesh['yh'=2,'x'=4,'z'=8,'yl'=2,'c'=2] {'yl','c'}, use_global_device_ids=true, to_apply=%region_9.13 | all-reduce | flops 4096 | bytes 32768 | tf_op jit(solution)/shard_map/psum | solution.py:176
  376.2 5.8 cholesky.111
  383.4 4.9 custom-call.16
  392.6 5.8 multiply_bitcast_fusion.1
  398.4 4.2 fusion.10
  405.5 30.6 %reduce-scatter.10.cloned.1.call-done = f32[2048,64]{0,1:T(8,128)} async-done(((f32[8192,64]{0,1:T(8,128)}), f32[2048,64]{0,1:T(8,128)}) %reduce-scatter.10.cloned.1.call-update) | async-done | bytes 524304 | tf_op jit(solution)/shard_map/reduce_scatter | solution.py:179
  439.5 31.5 %shard_map.78 = f32[64,64]{1,0:T(8,128)} custom-call(f32[64,64]{1,0:T(8,128)} %fusion.104.x_ref), custom_call_target="tpu_custom_call" | custom-call | tf_op jit(solution)/shard_map/pallas_call | solution.py:108
  472.6 5.8 cholesky.122
  479.8 4.9 custom-call.17
  486.3 20.7 %all-gather.8.cloned.1.call-done = bf16[8192,64]{0,1:T(8,128)(2,1)} async-done(((bf16[2048,64]{0,1:T(8,128)(2,1)}), bf16[8192,64]{0,1:T(8,128)(2,1)}) %all-gather.8.cloned.1.call-update) | async-done | bytes 1048592 | tf_op jit(solution)/shard_map/all_gather | solution.py:170
  510.7 4.0 multiply_bitcast_fusion
  514.7 4.9 fusion.8
  523.9 41.5 %reduce-scatter.12.cloned.1.call-done = f32[512,64]{1,0:T(8,128)} async-done(((f32[4096,64]{1,0:T(8,128)}), f32[512,64]{1,0:T(8,128)}) %reduce-scatter.12.cloned.1.call-update) | async-done | bytes 131088 | tf_op jit(solution)/shard_map/reduce_scatter | solution.py:140
  565.5 79.7 %reduce-scatter.14.cloned.1.call-done = f32[64,64]{1,0:T(8,128)} async-done(((f32[512,64]{1,0:T(8,128)}), f32[64,64]{1,0:T(8,128)}) %reduce-scatter.14.cloned.1.call-update) | async-done | bytes 16400 | tf_op jit(solution)/shard_map/reduce_scatter | solution.py:141
  647.7 30.5 %shard_map.79 = f32[64,64]{1,0:T(8,128)} custom-call(f32[64,64]{1,0:T(8,128)} %fusion.105.x_ref), custom_call_target="tpu_custom_call" | custom-call | tf_op jit(solution)/shard_map/pallas_call | solution.py:108
  679.8 5.8 cholesky.133
  687.8 4.9 custom-call.11
  (97 shorter events, 68.5 us)
Async XLA Ops:
  7.2 1.2 copy-start
  7.2 5.6 copy-start.5
  7.2 5.6 copy-start.3
  7.2 35.7 %copy-start.4 = (s32[1,1,128]{2,1,0:T(1,128)S(1)}, s32[1,1,128]{2,1,0:T(1,128)}, u32[]{:S(2)}) copy-start(s32[1,1,128]{2,1,0:T(1,128)} %param.12) | copy-start | bytes 1540
  7.2 103.2 %reduce-scatter.6.cloned.1.call-start = ((), (), s32[]{:S(2)}) async-start(), calls=%async_computation.5 | async-start | bytes 2621440 | tf_op jit(solution)/shard_map/reduce_scatter | solution.py:162
  80.3 2.8 copy-start.6
  82.9 98.4 %all-gather.4.cloned.1.call-start = ((), (), s32[]{:S(2)}) async-start(), calls=%async_computation.6 | async-start | bytes 1310720 | tf_op jit(solution)/shard_map/all_gather | solution.py:170
  160.6 72.4 %reduce-scatter.8.cloned.1.call-start = ((), (), s32[]{:S(2)}) async-start(), calls=%async_computation.7 | async-start | bytes 1179648 | tf_op jit(solution)/shard_map/reduce_scatter | solution.py:124
  194.6 130.2 %all-reduce.4.cloned.1.call-start = ((), (), s32[]{:S(2)}) async-start(), calls=%async_computation.8 | async-start | bytes 262144 | tf_op jit(solution)/shard_map/psum | solution.py:125
  233.0 128.7 %all-gather.6.cloned.1.call-start = ((), (), s32[]{:S(2)}) async-start(), calls=%async_computation.9 | async-start | bytes 1179648 | tf_op jit(solution)/shard_map/all_gather | solution.py:126
  324.9 111.2 %reduce-scatter.10.cloned.1.call-start = ((), (), s32[]{:S(2)}) async-start(), calls=%async_computation.10 | async-start | bytes 2621440 | tf_op jit(solution)/shard_map/reduce_scatter | solution.py:179
  389.3 1.0 copy-start.1
  402.6 33.5 %copy-start.2 = (f32[2048,64]{0,1:T(8,128)S(1)}, f32[2048,64]{0,1:T(8,128)}, u32[]{:S(2)}) copy-start(f32[2048,64]{0,1:T(8,128)} %get-tuple-element.28) | copy-start | bytes 1572868
  405.2 101.8 %all-gather.8.cloned.1.call-start = ((), (), s32[]{:S(2)}) async-start(), calls=%async_computation.11 | async-start | bytes 1310720 | tf_op jit(solution)/shard_map/all_gather | solution.py:170
  486.3 79.1 %reduce-scatter.12.cloned.1.call-start = ((), (), s32[]{:S(2)}) async-start(), calls=%async_computation.12 | async-start | bytes 2359296 | tf_op jit(solution)/shard_map/reduce_scatter | solution.py:140
  523.5 121.6 %reduce-scatter.14.cloned.1.call-start = ((), (), s32[]{:S(2)}) async-start(), calls=%async_computation.13 | async-start | bytes 294912 | tf_op jit(solution)/shard_map/reduce_scatter | solution.py:141
Sparse Core Ops, SparseCore 0:
  83.0 27.3 reduce-scatter.5
  160.7 20.5 all-gather.3
  194.7 38.1 reduce-scatter.7
  235.6 89.1 all-reduce.3
  326.5 35.1 all-gather.5
  405.3 30.7 reduce-scatter.9
  486.4 20.5 all-gather.7
  523.6 41.6 reduce-scatter.11
  569.7 75.4 reduce-scatter.13

commit v3 on v2

--- a/solution.py
+++ b/solution.py
@@ -120,6 +120,87 @@
     return out.reshape(shape)
 
 
+def halving_kernel(stages, gather, x_ref, o_ref, *scratch):
+    if gather:
+        work, recv, back, rs_send, rs_recv, ag_send, ag_recv = o_ref, *scratch
+    else:
+        work, recv, rs_send, rs_recv = scratch
+    coords = [lax.axis_index(name) for name in FINE]
+    partners, bits = [], []
+    for axis, step in stages:
+        place = coords[axis]
+        bit = (place // step) % 2
+        flip = place + step * (1 - 2 * bit)
+        partners.append(tuple(flip if i == axis else c for i, c in enumerate(coords)))
+        bits.append(bit)
+    barrier = pltpu.get_barrier_semaphore()
+    for partner in partners:
+        pl.semaphore_signal(barrier, inc=1, device_id=partner, device_id_type=pl.DeviceIdType.MESH)
+    pl.semaphore_wait(barrier, len(partners))
+    work[...] = x_ref[...]
+    total = work.shape[0]
+    base = 0
+    pieces = []
+    for s, partner in enumerate(partners):
+        size = total >> s
+        half = size // 2
+        keep = base + bits[s] * half
+        give = base + (1 - bits[s]) * half
+        slot = pl.ds(total - size, half)
+        copy = pltpu.make_async_remote_copy(
+            src_ref=work.at[pl.ds(give, half)],
+            dst_ref=recv.at[slot],
+            send_sem=rs_send.at[s],
+            recv_sem=rs_recv.at[s],
+            device_id=partner,
+            device_id_type=pl.DeviceIdType.MESH,
+        )
+        copy.start()
+        copy.wait()
+        work[pl.ds(keep, half), :] = work[pl.ds(keep, half), :] + recv[slot, :]
+        pieces.append((keep, give, slot))
+        base = keep
+    if gather:
+        for s in reversed(range(len(partners))):
+            keep, give, slot = pieces[s]
+            copy = pltpu.make_async_remote_copy(
+                src_ref=work.at[pl.ds(keep, slot.size)],
+                dst_ref=back.at[slot],
+                send_sem=ag_send.at[s],
+                recv_sem=ag_recv.at[s],
+                device_id=partners[s],
+                device_id_type=pl.DeviceIdType.MESH,
+            )
+            copy.start()
+            copy.wait()
+            work[pl.ds(give, slot.size), :] = back[slot, :]
+    else:
+        o_ref[...] = work[pl.ds(base, o_ref.shape[0]), :]
+
+
+CLAIM_STAGES = (("z", 1), ("x", 1), ("z", 2), ("x", 2), ("yh", 1), ("z", 4))
+
+
+def claim_halving(value, gather, cid):
+    stages = tuple((FINE.index(name), step) for name, step in CLAIM_STAGES)
+    count = len(stages)
+    flat = value.reshape(-1, 128)
+    rows = flat.shape[0]
+    out_rows = rows if gather else rows >> count
+    scratch = [] if gather else [pltpu.VMEM(flat.shape, flat.dtype)]
+    scratch += [pltpu.VMEM(flat.shape, flat.dtype)] * (2 if gather else 1)
+    scratch += [pltpu.SemaphoreType.DMA((count,))] * (4 if gather else 2)
+    out = pl.pallas_call(
+        functools.partial(halving_kernel, stages, gather),
+        out_shape=jax.ShapeDtypeStruct((out_rows, 128), flat.dtype),
+        in_specs=[pl.BlockSpec(memory_space=pltpu.VMEM)],
+        out_specs=pl.BlockSpec(memory_space=pltpu.VMEM),
+        scratch_shapes=scratch,
+        compiler_params=pltpu.CompilerParams(collective_id=cid, has_side_effects=True),
+    )(flat)
+    return out
+
+
 def claim_sum(value):
     part = lax.psum_scatter(value, "z", scatter_dimension=0, tiled=True)
     part = lax.psum(part, ("yh", "x"))
@@ -133,12 +214,11 @@
 
 
 def claim_scatter(value):
-    size_z = lax.axis_size("z")
-    size_o = lax.axis_size("yh") * lax.axis_size("x")
-    rows = value.shape[0] // (size_z * size_o)
-    blocks = value.reshape(size_o, size_z, rows, -1).transpose(1, 0, 2, 3).reshape(value.shape)
-    part = lax.psum_scatter(blocks, "z", scatter_dimension=0, tiled=True)
-    return lax.psum_scatter(part, ("yh", "x"), scatter_dimension=0, tiled=True)
+    width = value.shape[-1]
+    rows = value.shape[0] // lax.axis_size(CLAIM)
+    bits = value.reshape(2, 2, 2, 2, 2, 2, rows, width)
+    ordered = bits.transpose(5, 2, 4, 1, 0, 3, 6, 7).reshape(value.shape)
+    return claim_halving(ordered, False, 5).reshape(rows, width)
 
 
 def per_device(block_tiles, block_scale, row_index, col_index, start_basis):
@@ -171,7 +251,7 @@
         return backward_local(tiles_here, scale_here, rows_here, cols_here, gathered, col_count)
 
     u_first, b_first = row_orthonormal(row_scale[:, None] * first_sums, 1)
-    summed = claim_sum(backward_partial(u_first))
+    summed = claim_halving(backward_partial(u_first), True, 4).reshape(-1, u_first.shape[-1])
     update = col_scale[:, None] * summed - jnp.dot(first_basis, b_first.T, precision=HIGH)
     v_second, a_second = orthonormal(update, lax.psum(gram_of(update), FEAT))
     scaled = (col_scale[:, None] * v_second).astype(jnp.bfloat16)

time: 708 us -> 555 us (0.78)
  waiting for transfers between devices: 386 us -> 98.8 us
  Pallas kernels: 122 us -> 241 us
  local copies, waits for them, and re-layouts: 27.7 us -> 41.8 us
    reduce_scatter x3 -> x0, waiting for transfers between devices: 159 us -> none  [the longest x1 79.7 us: claim_scatter(): return lax.psum_scatter(part, ('yh', 'x'), scatter_dimension=0, tiled=True)]
    pallas_call x0 -> x2, Pallas kernels: none -> 121 us  [claim_halving(): pl.pallas_call(functools.partial(halving_kernel, stages, gather), out_sha...]
    psum x1 -> x0, waiting for transfers between devices: 91.8 us -> none  [claim_sum(): part = lax.psum(part, ('yh', 'x'))]
    all_gather x1 -> x0, waiting for transfers between devices: 36.8 us -> none  [claim_sum(): return lax.all_gather(part, 'z', axis=0, tiled=True)]
    another operation x1 -> x4, local copies, waits for them, and re-layouts: 1.58 us -> 10.8 us  [the longest x2 5.59 us: claim_scatter(): bits = value.reshape(2, 2, 2, 2, 2, 2, rows, width)]
  transfers between devices with their start and end apart: 9 -> 4, of which waited for: 9 -> 4; matrix products, arithmetic and copies ran while one was open for 0% -> 0% of each run, Pallas kernels for 0% -> 0%
where the time goes in v3:
time: 555 us; the launch traced here: 546 us
  Pallas kernels  241 us (43%)
  waiting for transfers between devices  98.8 us (18%)
  other arithmetic  67.9 us (12%)
  matrix products  58.2 us (10%)
  local copies, waits for them, and re-layouts  41.8 us (8%)
  blocking collectives  22.1 us (4%)
  between operations  15.1 us (3%)
    pallas_call x2, Pallas kernels, claim_halving(): pl.pallas_call(functools.partial(halving_kernel, stages, gather), out_sha...  121 us
    pallas_call x4, Pallas kernels, butterfly_sum(): pl.pallas_call(functools.partial(butterfly_kernel, tuple(stages)), out_sh...  120 us
    all_gather x2, waiting for transfers between devices, backward_partial(): gathered = lax.all_gather(operand, FEAT, axis=0, tiled=True)  41.5 us
    another operation x15, other arithmetic, orthonormal(): factor = jnp.linalg.cholesky(gram_total)  32.6 us
    reduce_scatter x1, waiting for transfers between devices, per_device(): lax.psum_scatter(second_partial, FEAT, scatter_dimension=0, tiled=True)  31.2 us
    reduce_scatter x1, waiting for transfers between devices, per_device(): lax.psum_scatter(first_partial, FEAT, scatter_dimension=0, tiled=True)  26 us
    another operation x6, other arithmetic, orthonormal(): lax.linalg.triangular_solve(factor, block, left_side=False, lower=True, t...  25.1 us
    dot_general x2, matrix products, forward_local(): jnp.einsum('bij,bjk->bik', block_tiles, picked, preferred_element_type=jn...  11.6 us
  transfers between devices with their start and end apart: 4, of which 4 were waited for; matrix products, arithmetic and copies ran while one was open for 0% of the time, Pallas kernels for 0%

profile of v3, /device:TPU:64, one launch (start us, length us, event | category | flops | bytes accessed | tf_op | source)
XLA Modules:
  0.0 545.6 jit_solution(18283591170079683402)
XLA Ops:
  9.4 3.4 convert_reduce_fusion.1
  13.7 28.5 %shard_map.76 = f32[32,128]{1,0:T(8,128)} custom-call(f32[32,128]{1,0:T(8,128)} %fusion.31.x_ref), custom_call_target="tpu_custom_call" | custom-call | tf_op jit(solution)/shard_map/pallas_call | solution.py:108
  43.1 11.3 %all-reduce.1 = (f32[64,64]{0,1:T(8,128)S(1)}, f32[8192]{0:T(1024)S(1)}) all-reduce(f32[64,64]{0,1:T(8,128)S(1)} %fusion.102, f32[8192]{0:T(1024)S(1)} %convolution_bitcast_fusion.4), channel_id=1, replica_groups=mesh['yh'=2,'x'=4,'z'=8,'yl'=2,'c'=2] {'yl','c'}, use_global_device_ids=true, to_apply=%region_3.0 | all-reduce | flops 12288 | bytes 98304 | tf_op jit(solution)/shard_map/psum | solution.py:238
  54.5 5.8 %cholesky.89 = f32[64,64]{1,0:T(8,128)S(1)} custom-call(f32[64,64]{1,0:T(8,128)S(1)} %fusion.45), custom_call_target="Cholesky" | custom-call | tf_op jit(solution)/shard_map/jit(cholesky)/cholesky | solution.py:65
  61.7 4.9 custom-call.14
  70.0 5.8 %multiply_bitcast_fusion.3 = f32[128,128,64]{1,2,0:T(8,128)S(1)} fusion(bf16[128,128,64]{1,2,0:T(8,128)(2,1)} %gather_fusion, bf16[1,1,128,128,128]{4,3,2,1,0:T(8,128)(2,1)} %param.10, f32[128]{0:T(128)S(1)} %bitcast.186), kind=kOutput, calls=%fused_computation.28 | convolution fusion | flops 269484032 | bytes 10486272 | tf_op jit(solution)/shard_map/bij,bjk->bik/dot_general | solution.py:24
  75.8 4.2 fusion.14
  84.1 26.0 %reduce-scatter.3.cloned.1.call-done = f32[2048,64]{0,1:T(8,128)} async-done(((f32[8192,64]{0,1:T(8,128)}), f32[2048,64]{0,1:T(8,128)}) %reduce-scatter.3.cloned.1.call-update) | async-done | bytes 524304 | tf_op jit(solution)/shard_map/reduce_scatter | solution.py:242
  112.4 31.5 %shard_map.77 = f32[64,64]{1,0:T(8,128)} custom-call(f32[64,64]{1,0:T(8,128)} %fusion.27.x_ref), custom_call_target="tpu_custom_call" | custom-call | tf_op jit(solution)/shard_map/pallas_call | solution.py:108
  145.5 5.8 %cholesky.100 = f32[64,64]{1,0:T(8,128)S(1)} custom-call(f32[64,64]{1,0:T(8,128)S(1)} %fusion.43), custom_call_target="Cholesky" | custom-call | tf_op jit(solution)/shard_map/jit(cholesky)/cholesky | solution.py:65
  152.7 4.9 custom-call.15
  160.3 20.7 %all-gather.3.cloned.1.call-done = bf16[8192,64]{0,1:T(8,128)(2,1)} async-done(((bf16[2048,64]{0,1:T(8,128)(2,1)}), bf16[8192,64]{0,1:T(8,128)(2,1)}) %all-gather.3.cloned.1.call-update) | async-done | bytes 1048592 | tf_op jit(solution)/shard_map/all_gather | solution.py:250
  184.6 4.0 multiply_bitcast_fusion.2
  188.7 3.9 fusion.12
  197.2 75.6 %shard_map.78 = f32[2048,128]{1,0:T(8,128)} custom-call(f32[2048,128]{1,0:T(8,128)} %reshape_reshape.9.x_ref), custom_call_target="tpu_custom_call" | custom-call | tf_op jit(solution)/shard_map/pallas_call | solution.py:193
  275.6 3.2 copy.42
  282.7 10.8 %psum.15 = f32[64,64]{0,1:T(8,128)S(1)} all-reduce(f32[64,64]{0,1:T(8,128)S(1)} %fusion.103), channel_id=1, replica_groups=mesh['yh'=2,'x'=4,'z'=8,'yl'=2,'c'=2] {'yl','c'}, use_global_device_ids=true, to_apply=%region_7.11 | all-reduce | flops 4096 | bytes 32768 | tf_op jit(solution)/shard_map/psum | solution.py:256
  293.6 5.8 %cholesky.111 = f32[64,64]{1,0:T(8,128)S(1)} custom-call(f32[64,64]{1,0:T(8,128)S(1)} %fusion.41), custom_call_target="Cholesky" | custom-call | tf_op jit(solution)/shard_map/jit(cholesky)/cholesky | solution.py:65
  300.8 4.9 custom-call.16
  310.1 5.8 %multiply_bitcast_fusion.1 = f32[128,128,64]{1,2,0:T(8,128)S(1)} fusion(bf16[128,128,64]{1,2,0:T(8,128)(2,1)} %gather_fusion.2, bf16[1,1,128,128,128]{4,3,2,1,0:T(8,128)(2,1)} %param.10, f32[128]{0:T(128)S(1)} %bitcast.188), kind=kOutput, calls=%fused_computation.26 | convolution fusion | flops 269484032 | bytes 10486272 | tf_op jit(solution)/shard_map/bij,bjk->bik/dot_general | solution.py:24
  315.9 4.2 fusion.10
  322.8 31.2 %reduce-scatter.5.cloned.1.call-done = f32[2048,64]{0,1:T(8,128)} async-done(((f32[8192,64]{0,1:T(8,128)}), f32[2048,64]{0,1:T(8,128)}) %reduce-scatter.5.cloned.1.call-update) | async-done | bytes 524304 | tf_op jit(solution)/shard_map/reduce_scatter | solution.py:259
  357.6 31.5 %shard_map.79 = f32[64,64]{1,0:T(8,128)} custom-call(f32[64,64]{1,0:T(8,128)} %fusion.104.x_ref), custom_call_target="tpu_custom_call" | custom-call | tf_op jit(solution)/shard_map/pallas_call | solution.py:108
  390.7 5.8 %cholesky.122 = f32[64,64]{1,0:T(8,128)S(1)} custom-call(f32[64,64]{1,0:T(8,128)S(1)} %fusion.39), custom_call_target="Cholesky" | custom-call | tf_op jit(solution)/shard_map/jit(cholesky)/cholesky | solution.py:65
  397.8 4.9 custom-call.17
  404.4 20.9 %all-gather.5.cloned.1.call-done = bf16[8192,64]{0,1:T(8,128)(2,1)} async-done(((bf16[2048,64]{0,1:T(8,128)(2,1)}), bf16[8192,64]{0,1:T(8,128)(2,1)}) %all-gather.5.cloned.1.call-update) | async-done | bytes 1048592 | tf_op jit(solution)/shard_map/all_gather | solution.py:250
  428.9 4.0 multiply_bitcast_fusion
  433.0 4.9 fusion.8
  446.1 45.3 %shard_map.80 = f32[32,128]{1,0:T(8,128)} custom-call(f32[2048,128]{1,0:T(8,128)} %reshape_reshape.11.x_ref), custom_call_target="tpu_custom_call" | custom-call | tf_op jit(solution)/shard_map/pallas_call | solution.py:193
  494.7 28.9 %shard_map.81 = f32[64,64]{1,0:T(8,128)} custom-call(f32[64,64]{1,0:T(8,128)} %fusion.105.x_ref), custom_call_target="tpu_custom_call" | custom-call | tf_op jit(solution)/shard_map/pallas_call | solution.py:108
  525.2 5.8 %cholesky.133 = f32[64,64]{1,0:T(8,128)S(1)} custom-call(f32[64,64]{1,0:T(8,128)S(1)} %fusion.37), custom_call_target="Cholesky" | custom-call | tf_op jit(solution)/shard_map/jit(cholesky)/cholesky | solution.py:65
  533.2 4.9 custom-call.11
  (89 shorter events, 71.4 us)
Async XLA Ops:
  7.2 1.2 copy-start
  7.2 5.6 %copy-start.5 = (s32[1,1,128]{2,1,0:T(1,128)S(1)}, s32[1,1,128]{2,1,0:T(1,128)}, u32[]{:S(2)}) copy-start(s32[1,1,128]{2,1,0:T(1,128)} %param.13) | copy-start | bytes 1540
  7.2 5.6 %copy-start.3 = (f32[1,1,128]{2,1,0:T(1,128)S(1)}, f32[1,1,128]{2,1,0:T(1,128)}, u32[]{:S(2)}) copy-start(f32[1,1,128]{2,1,0:T(1,128)} %param.11) | copy-start | bytes 1540
  7.2 35.7 %copy-start.4 = (s32[1,1,128]{2,1,0:T(1,128)S(1)}, s32[1,1,128]{2,1,0:T(1,128)}, u32[]{:S(2)}) copy-start(s32[1,1,128]{2,1,0:T(1,128)} %param.12) | copy-start | bytes 1540
  7.2 102.8 %reduce-scatter.3.cloned.1.call-start = ((), (), s32[]{:S(2)}) async-start(), calls=%async_computation.2 | async-start | bytes 2621440 | tf_op jit(solution)/shard_map/reduce_scatter | solution.py:242
  79.9 2.9 copy-start.6
  82.5 98.4 %all-gather.3.cloned.1.call-start = ((), (), s32[]{:S(2)}) async-start(), calls=%async_computation.3 | async-start | bytes 1310720 | tf_op jit(solution)/shard_map/all_gather | solution.py:250
  160.2 193.8 %reduce-scatter.5.cloned.1.call-start = ((), (), s32[]{:S(2)}) async-start(), calls=%async_computation.4 | async-start | bytes 2621440 | tf_op jit(solution)/shard_map/reduce_scatter | solution.py:259
  306.8 1.0 copy-start.1
  320.0 34.0 %copy-start.2 = (f32[2048,64]{0,1:T(8,128)S(1)}, f32[2048,64]{0,1:T(8,128)}, u32[]{:S(2)}) copy-start(f32[2048,64]{0,1:T(8,128)} %get-tuple-element.28) | copy-start | bytes 1572868
  322.6 102.6 %all-gather.5.cloned.1.call-start = ((), (), s32[]{:S(2)}) async-start(), calls=%async_computation.5 | async-start | bytes 1310720 | tf_op jit(solution)/shard_map/all_gather | solution.py:250
Sparse Core Ops, SparseCore 0:
  82.6 27.3 reduce-scatter.2
  160.4 20.5 all-gather.2
  322.7 31.2 reduce-scatter.4
  404.4 20.7 all-gather.4

commit v4 on v3

--- a/solution.py
+++ b/solution.py
@@ -69,55 +69,94 @@
     return (basis, factor.T)
 
 
-def butterfly_kernel(stages, x_ref, o_ref, recv, send_sem, recv_sem):
+def group_kernel(groups, x_ref, o_ref, slots, send_sem, recv_sem):
     coords = [lax.axis_index(name) for name in FINE]
-    partners = []
-    for axis, step in stages:
-        place = coords[axis]
-        flip = place + step * (1 - 2 * ((place // step) % 2))
-        partners.append(tuple(flip if i == axis else c for i, c in enumerate(coords)))
+    plans = []
+    for axes, sizes in groups:
+        count = 1
+        for size in sizes:
+            count *= size
+        me = 0
+        for axis, size in zip(axes, sizes):
+            me = me * size + coords[axis]
+        targets = []
+        for k in range(1, count):
+            member = (me + k) % count
+            place = list(coords)
+            rest = member
+            for axis, size in reversed(list(zip(axes, sizes))):
+                place[axis] = rest % size
+                rest = rest // size
+            targets.append((tuple(place), (me + count - k) % count))
+        plans.append((count, me, targets))
     barrier = pltpu.get_barrier_semaphore()
-    for partner in partners:
-        pl.semaphore_signal(barrier, inc=1, device_id=partner, device_id_type=pl.DeviceIdType.MESH)
-    pl.semaphore_wait(barrier, len(partners))
+    total = 0
+    for count, me, targets in plans:
+        for place, _ in targets:
+            pl.semaphore_signal(barrier, inc=1, device_id=place, device_id_type=pl.DeviceIdType.MESH)
+        total += len(targets)
+    pl.semaphore_wait(barrier, total)
     o_ref[...] = x_ref[...]
-    for s, partner in enumerate(partners):
-        copy = pltpu.make_async_remote_copy(
-            src_ref=o_ref,
-            dst_ref=recv.at[s],
-            send_sem=send_sem.at[s],
-            recv_sem=recv_sem.at[s],
-            device_id=partner,
-            device_id_type=pl.DeviceIdType.MESH,
-        )
-        copy.start()
-        copy.wait()
-        o_ref[...] = o_ref[...] + recv[s]
-
-
-def butterfly_sum(value, names, cid):
-    stages = []
-    for name in names:
-        size = lax.axis_size(name)
-        step = 1
-        while step < size:
-            stages.append((FINE.index(name), step))
-            step *= 2
+    for g, (count, me, targets) in enumerate(plans):
+        slots[g, me] = o_ref[...]
+        copies = []
+        for k, (place, _) in enumerate(targets):
+            copy = pltpu.make_async_remote_copy(
+                src_ref=o_ref,
+                dst_ref=slots.at[g, me],
+                send_sem=send_sem.at[g, k],
+                recv_sem=recv_sem.at[g, me],
+                device_id=place,
+                device_id_type=pl.DeviceIdType.MESH,
+            )
+            copy.start()
+            copies.append(copy)
+        for copy in copies:
+            copy.wait_send()
+        for place, sender in targets:
+            pltpu.make_async_remote_copy(
+                src_ref=o_ref,
+                dst_ref=slots.at[g, sender],
+                send_sem=send_sem.at[g, 0],
+                recv_sem=recv_sem.at[g, sender],
+                device_id=place,
+                device_id_type=pl.DeviceIdType.MESH,
+            ).wait_recv()
+        acc = slots[g, 0]
+        for j in range(1, count):
+            acc = acc + slots[g, j]
+        o_ref[...] = acc
+
+
+def group_sum(value, groups, cid):
+    spec = []
+    widest = 1
+    for names in groups:
+        sizes = tuple(lax.axis_size(name) for name in names)
+        count = 1
+        for size in sizes:
+            count *= size
+        widest = max(widest, count)
+        spec.append((tuple(FINE.index(name) for name in names), sizes))
     shape = value.shape
     flat = value.reshape(-1, 128) if value.ndim == 1 else value
     out = pl.pallas_call(
-        functools.partial(butterfly_kernel, tuple(stages)),
+        functools.partial(group_kernel, tuple(spec)),
         out_shape=jax.ShapeDtypeStruct(flat.shape, flat.dtype),
         in_specs=[pl.BlockSpec(memory_space=pltpu.VMEM)],
         out_specs=pl.BlockSpec(memory_space=pltpu.VMEM),
         scratch_shapes=[
-            pltpu.VMEM((len(stages),) + flat.shape, flat.dtype),
-            pltpu.SemaphoreType.DMA((len(stages),)),
-            pltpu.SemaphoreType.DMA((len(stages),)),
+            pltpu.VMEM((len(spec), widest) + flat.shape, flat.dtype),
+            pltpu.SemaphoreType.DMA((len(spec), widest)),
+            pltpu.SemaphoreType.DMA((len(spec), widest)),
         ],
         compiler_params=pltpu.CompilerParams(collective_id=cid, has_side_effects=True),
     )(flat)
     return out.reshape(shape)
+
+
+ALL_GROUPS = (FEAT, ("z",), ("yh", "x"))
+CLAIM_GROUPS = (("z",), ("yh", "x"))
 
 
 def halving_kernel(stages, gather, x_ref, o_ref, *scratch):
@@ -232,7 +271,7 @@
     own_cols = start_basis.shape[0] // claim_count
     own_first = lax.axis_index(CLAIM) * own_cols
     row_part, col_part = degree_local(tiles_here, scale_here, rows_here, cols_here, col_count)
-    col_total = butterfly_sum(col_part, CLAIM, 0)
+    col_total = group_sum(col_part, CLAIM_GROUPS, 0)
     col_scale = lax.rsqrt(col_total + 1.0)
     row_total = lax.psum_scatter(row_part, FEAT, scatter_dimension=0, tiled=True)
     start_total = lax.psum(gram_of(start_basis), FEAT)
@@ -243,7 +282,7 @@
     row_scale = lax.rsqrt(row_total + 1.0)
 
     def row_orthonormal(block, cid):
-        return orthonormal(block, butterfly_sum(gram_of(block), FINE, cid))
+        return orthonormal(block, group_sum(gram_of(block), ALL_GROUPS, cid))
 
     def backward_partial(basis):
         operand = (row_scale[:, None] * basis).astype(jnp.bfloat16)
@@ -263,7 +302,7 @@
     own_scale = lax.dynamic_slice_in_dim(col_scale, own_first, own_cols, 0)
     own_second = lax.dynamic_slice_in_dim(v_second, own_first, own_cols, 0)
     q_second = own_scale[:, None] * own_sums - jnp.dot(own_second, b_second.T, precision=HIGH)
-    v_output, a_third = orthonormal(q_second, butterfly_sum(gram_of(q_second), FINE, 3))
+    v_output, a_third = orthonormal(q_second, group_sum(gram_of(q_second), ALL_GROUPS, 3))
     bidiagonal = jnp.stack([b_first, a_second, b_second, a_third])
     return (u_second, v_output, bidiagonal)
 

time: 555 us -> 524 us (0.944)
  Pallas kernels: 241 us -> 214 us
    pallas_call x4, Pallas kernels: 120 us -> 93 us  [group_sum(): pl.pallas_call(functools.partial(group_kernel, tuple(spec)), out_shape=ja...]
where the time goes in v4:
time: 524 us; the launch traced here: 520 us
  Pallas kernels  214 us (41%)
  waiting for transfers between devices  101 us (19%)
  other arithmetic  67.9 us (13%)
  matrix products  58.2 us (11%)
  local copies, waits for them, and re-layouts  41.8 us (8%)
  blocking collectives  21.8 us (4%)
  between operations  15.1 us (3%)
    pallas_call x2, Pallas kernels, claim_halving(): pl.pallas_call(functools.partial(halving_kernel, stages, gather), out_sha...  121 us
    pallas_call x4, Pallas kernels, group_sum(): pl.pallas_call(functools.partial(group_kernel, tuple(spec)), out_shape=ja...  93 us
    all_gather x2, waiting for transfers between devices, backward_partial(): gathered = lax.all_gather(operand, FEAT, axis=0, tiled=True)  42.6 us
    another operation x15, other arithmetic, orthonormal(): factor = jnp.linalg.cholesky(gram_total)  32.6 us
    reduce_scatter x1, waiting for transfers between devices, per_device(): lax.psum_scatter(second_partial, FEAT, scatter_dimension=0, tiled=True)  31.1 us
    reduce_scatter x1, waiting for transfers between devices, per_device(): lax.psum_scatter(first_partial, FEAT, scatter_dimension=0, tiled=True)  27.1 us
    another operation x6, other arithmetic, orthonormal(): lax.linalg.triangular_solve(factor, block, left_side=False, lower=True, t...  25.1 us
    dot_general x2, matrix products, forward_local(): jnp.einsum('bij,bjk->bik', block_tiles, picked, preferred_element_type=jn...  11.6 us
  transfers between devices with their start and end apart: 4, of which 4 were waited for; matrix products, arithmetic and copies ran while one was open for 0% of the time, Pallas kernels for 0%

profile of v4, /device:TPU:64, one launch (start us, length us, event | category | flops | bytes accessed | tf_op | source)
XLA Modules:
  0.0 520.0 jit_solution(1726207437306960669)
XLA Ops:
  9.4 3.4 convert_reduce_fusion.1
  13.7 19.1 %shard_map.76 = f32[32,128]{1,0:T(8,128)} custom-call(f32[32,128]{1,0:T(8,128)} %fusion.31.x_ref), custom_call_target="tpu_custom_call" | custom-call | tf_op jit(solution)/shard_map/pallas_call | solution.py:143
  33.7 10.9 %all-reduce.1 = (f32[64,64]{0,1:T(8,128)S(1)}, f32[8192]{0:T(1024)S(1)}) all-reduce(f32[64,64]{0,1:T(8,128)S(1)} %fusion.102, f32[8192]{0:T(1024)S(1)} %convolution_bitcast_fusion.4), channel_id=1, replica_groups=mesh['yh'=2,'x'=4,'z'=8,'yl'=2,'c'=2] {'yl','c'}, use_global_device_ids=true, to_apply=%region_3.0 | all-reduce | flops 12288 | bytes 98304 | tf_op jit(solution)/shard_map/psum | solution.py:277
  44.7 5.8 %cholesky.89 = f32[64,64]{1,0:T(8,128)S(1)} custom-call(f32[64,64]{1,0:T(8,128)S(1)} %fusion.45), custom_call_target="Cholesky" | custom-call | tf_op jit(solution)/shard_map/jit(cholesky)/cholesky | solution.py:65
  51.9 4.9 custom-call.14
  60.1 5.8 %multiply_bitcast_fusion.3 = f32[128,128,64]{1,2,0:T(8,128)S(1)} fusion(bf16[128,128,64]{1,2,0:T(8,128)(2,1)} %gather_fusion, bf16[1,1,128,128,128]{4,3,2,1,0:T(8,128)(2,1)} %param.10, f32[128]{0:T(128)S(1)} %bitcast.186), kind=kOutput, calls=%fused_computation.28 | convolution fusion | flops 269484032 | bytes 10486272 | tf_op jit(solution)/shard_map/bij,bjk->bik/dot_general | solution.py:24
  65.9 4.2 fusion.14
  74.2 27.1 %reduce-scatter.3.cloned.1.call-done = f32[2048,64]{0,1:T(8,128)} async-done(((f32[8192,64]{0,1:T(8,128)}), f32[2048,64]{0,1:T(8,128)}) %reduce-scatter.3.cloned.1.call-update) | async-done | bytes 524304 | tf_op jit(solution)/shard_map/reduce_scatter | solution.py:281
  103.7 24.7 %shard_map.77 = f32[64,64]{1,0:T(8,128)} custom-call(f32[64,64]{1,0:T(8,128)} %fusion.27.x_ref), custom_call_target="tpu_custom_call" | custom-call | tf_op jit(solution)/shard_map/pallas_call | solution.py:143
  130.0 5.8 %cholesky.100 = f32[64,64]{1,0:T(8,128)S(1)} custom-call(f32[64,64]{1,0:T(8,128)S(1)} %fusion.43), custom_call_target="Cholesky" | custom-call | tf_op jit(solution)/shard_map/jit(cholesky)/cholesky | solution.py:65
  137.1 4.9 custom-call.15
  144.7 21.3 %all-gather.3.cloned.1.call-done = bf16[8192,64]{0,1:T(8,128)(2,1)} async-done(((bf16[2048,64]{0,1:T(8,128)(2,1)}), bf16[8192,64]{0,1:T(8,128)(2,1)}) %all-gather.3.cloned.1.call-update) | async-done | bytes 1048592 | tf_op jit(solution)/shard_map/all_gather | solution.py:289
  169.7 4.0 multiply_bitcast_fusion.2
  173.7 3.9 fusion.12
  182.3 75.6 %shard_map.78 = f32[2048,128]{1,0:T(8,128)} custom-call(f32[2048,128]{1,0:T(8,128)} %reshape_reshape.9.x_ref), custom_call_target="tpu_custom_call" | custom-call | tf_op jit(solution)/shard_map/pallas_call | solution.py:232
  260.7 3.2 copy.42
  267.7 10.9 %psum.15 = f32[64,64]{0,1:T(8,128)S(1)} all-reduce(f32[64,64]{0,1:T(8,128)S(1)} %fusion.103), channel_id=1, replica_groups=mesh['yh'=2,'x'=4,'z'=8,'yl'=2,'c'=2] {'yl','c'}, use_global_device_ids=true, to_apply=%region_7.11 | all-reduce | flops 4096 | bytes 32768 | tf_op jit(solution)/shard_map/psum | solution.py:295
  278.8 5.8 %cholesky.111 = f32[64,64]{1,0:T(8,128)S(1)} custom-call(f32[64,64]{1,0:T(8,128)S(1)} %fusion.41), custom_call_target="Cholesky" | custom-call | tf_op jit(solution)/shard_map/jit(cholesky)/cholesky | solution.py:65
  286.0 4.9 custom-call.16
  295.2 5.8 %multiply_bitcast_fusion.1 = f32[128,128,64]{1,2,0:T(8,128)S(1)} fusion(bf16[128,128,64]{1,2,0:T(8,128)(2,1)} %gather_fusion.2, bf16[1,1,128,128,128]{4,3,2,1,0:T(8,128)(2,1)} %param.10, f32[128]{0:T(128)S(1)} %bitcast.188), kind=kOutput, calls=%fused_computation.26 | convolution fusion | flops 269484032 | bytes 10486272 | tf_op jit(solution)/shard_map/bij,bjk->bik/dot_general | solution.py:24
  301.0 4.2 fusion.10
  308.0 31.1 %reduce-scatter.5.cloned.1.call-done = f32[2048,64]{0,1:T(8,128)} async-done(((f32[8192,64]{0,1:T(8,128)}), f32[2048,64]{0,1:T(8,128)}) %reduce-scatter.5.cloned.1.call-update) | async-done | bytes 524304 | tf_op jit(solution)/shard_map/reduce_scatter | solution.py:298
  342.6 24.7 %shard_map.79 = f32[64,64]{1,0:T(8,128)} custom-call(f32[64,64]{1,0:T(8,128)} %fusion.104.x_ref), custom_call_target="tpu_custom_call" | custom-call | tf_op jit(solution)/shard_map/pallas_call | solution.py:143
  368.9 5.8 %cholesky.122 = f32[64,64]{1,0:T(8,128)S(1)} custom-call(f32[64,64]{1,0:T(8,128)S(1)} %fusion.39), custom_call_target="Cholesky" | custom-call | tf_op jit(solution)/shard_map/jit(cholesky)/cholesky | solution.py:65
  376.1 4.9 custom-call.17
  382.6 21.3 %all-gather.5.cloned.1.call-done = bf16[8192,64]{0,1:T(8,128)(2,1)} async-done(((bf16[2048,64]{0,1:T(8,128)(2,1)}), bf16[8192,64]{0,1:T(8,128)(2,1)}) %all-gather.5.cloned.1.call-update) | async-done | bytes 1048592 | tf_op jit(solution)/shard_map/all_gather | solution.py:289
  407.6 4.0 multiply_bitcast_fusion
  411.6 4.9 fusion.8
  424.7 45.3 %shard_map.80 = f32[32,128]{1,0:T(8,128)} custom-call(f32[2048,128]{1,0:T(8,128)} %reshape_reshape.11.x_ref), custom_call_target="tpu_custom_call" | custom-call | tf_op jit(solution)/shard_map/pallas_call | solution.py:232
  473.4 24.6 %shard_map.81 = f32[64,64]{1,0:T(8,128)} custom-call(f32[64,64]{1,0:T(8,128)} %fusion.105.x_ref), custom_call_target="tpu_custom_call" | custom-call | tf_op jit(solution)/shard_map/pallas_call | solution.py:143
  499.6 5.8 %cholesky.133 = f32[64,64]{1,0:T(8,128)S(1)} custom-call(f32[64,64]{1,0:T(8,128)S(1)} %fusion.37), custom_call_target="Cholesky" | custom-call | tf_op jit(solution)/shard_map/jit(cholesky)/cholesky | solution.py:65
  507.6 4.9 custom-call.11
  (89 shorter events, 71.4 us)
Async XLA Ops:
  7.2 1.2 copy-start
  7.2 5.6 %copy-start.5 = (s32[1,1,128]{2,1,0:T(1,128)S(1)}, s32[1,1,128]{2,1,0:T(1,128)}, u32[]{:S(2)}) copy-start(s32[1,1,128]{2,1,0:T(1,128)} %param.13) | copy-start | bytes 1540
  7.2 5.6 %copy-start.3 = (f32[1,1,128]{2,1,0:T(1,128)S(1)}, f32[1,1,128]{2,1,0:T(1,128)}, u32[]{:S(2)}) copy-start(f32[1,1,128]{2,1,0:T(1,128)} %param.11) | copy-start | bytes 1540
  7.2 26.3 %copy-start.4 = (s32[1,1,128]{2,1,0:T(1,128)S(1)}, s32[1,1,128]{2,1,0:T(1,128)}, u32[]{:S(2)}) copy-start(s32[1,1,128]{2,1,0:T(1,128)} %param.12) | copy-start | bytes 1540
  7.2 94.1 %reduce-scatter.3.cloned.1.call-start = ((), (), s32[]{:S(2)}) async-start(), calls=%async_computation.2 | async-start | bytes 2621440 | tf_op jit(solution)/shard_map/reduce_scatter | solution.py:281
  70.1 2.9 copy-start.6
  72.7 93.3 %all-gather.3.cloned.1.call-start = ((), (), s32[]{:S(2)}) async-start(), calls=%async_computation.3 | async-start | bytes 1310720 | tf_op jit(solution)/shard_map/all_gather | solution.py:289
  144.6 194.5 %reduce-scatter.5.cloned.1.call-start = ((), (), s32[]{:S(2)}) async-start(), calls=%async_computation.4 | async-start | bytes 2621440 | tf_op jit(solution)/shard_map/reduce_scatter | solution.py:298
  291.9 1.0 copy-start.1
  305.2 33.9 %copy-start.2 = (f32[2048,64]{0,1:T(8,128)S(1)}, f32[2048,64]{0,1:T(8,128)}, u32[]{:S(2)}) copy-start(f32[2048,64]{0,1:T(8,128)} %get-tuple-element.28) | copy-start | bytes 1572868
  307.8 96.2 %all-gather.5.cloned.1.call-start = ((), (), s32[]{:S(2)}) async-start(), calls=%async_computation.5 | async-start | bytes 1310720 | tf_op jit(solution)/shard_map/all_gather | solution.py:289
Sparse Core Ops, SparseCore 0:
  72.8 28.4 reduce-scatter.2
  144.8 21.2 all-gather.2
  307.9 31.1 reduce-scatter.4
  382.7 21.2 all-gather.4

commit v5 on v4

--- a/solution.py
+++ b/solution.py
@@ -17,30 +17,80 @@
 FEAT = ("yl", "c")
 
 
+TILES_PER_STEP = 16
+
+
+def forward_kernel(rows_ref, cols_ref, scale_ref, tiles_ref, operand_ref, out_ref):
+    step = pl.program_id(0)
+    edge = tiles_ref.shape[-1]
+
+    @pl.when(step == 0)
+    def _():
+        out_ref[...] = jnp.zeros_like(out_ref)
+
+    for t in range(tiles_ref.shape[0]):
+        b = step * tiles_ref.shape[0] + t
+        picked = operand_ref[pl.ds(pl.multiple_of(cols_ref[b] * edge, edge), edge), :]
+        product = jnp.dot(tiles_ref[t], picked, preferred_element_type=jnp.float32) * scale_ref[b]
+        target = pl.ds(pl.multiple_of(rows_ref[b] * edge, edge), edge)
+        out_ref[target, :] = out_ref[target, :] + product
+
+
+def backward_kernel(rows_ref, cols_ref, scale_ref, tiles_ref, operand_ref, out_ref):
+    step = pl.program_id(0)
+    edge = tiles_ref.shape[-1]
+
+    @pl.when(step == 0)
+    def _():
+        out_ref[...] = jnp.zeros_like(out_ref)
+
+    for t in range(tiles_ref.shape[0]):
+        b = step * tiles_ref.shape[0] + t
+        picked = operand_ref[:, pl.ds(pl.multiple_of(rows_ref[b] * edge, edge), edge)]
+        product = jnp.dot(picked, tiles_ref[t], preferred_element_type=jnp.float32) * scale_ref[b]
+        target = pl.ds(pl.multiple_of(cols_ref[b] * edge, edge), edge)
+        out_ref[:, target] = out_ref[:, target] + product
+
+
+def block_product(kernel, block_tiles, block_scale, row_index, col_index, operand, out_shape):
+    count, edge, _ = block_tiles.shape
+    per = TILES_PER_STEP
+    grid_spec = pltpu.PrefetchScalarGridSpec(
+        num_scalar_prefetch=2,
+        grid=(count // per,),
+        in_specs=[
+            pl.BlockSpec(memory_space=pltpu.SMEM),
+            pl.BlockSpec((per, edge, edge), lambda i, rows, cols: (i, 0, 0)),
+            pl.BlockSpec(operand.shape, lambda i, rows, cols: (0, 0)),
+        ],
+        out_specs=pl.BlockSpec(out_shape, lambda i, rows, cols: (0, 0)),
+    )
+    width = min(operand.shape)
+    return pl.pallas_call(
+        kernel,
+        grid_spec=grid_spec,
+        out_shape=jax.ShapeDtypeStruct(out_shape, jnp.float32),
+        cost_estimate=pl.CostEstimate(
+            flops=2 * count * edge * edge * width,
+            bytes_accessed=block_tiles.size * 2 + operand.size * 2 + out_shape[0] * out_shape[1] * 4,
+            transcendentals=0,
+        ),
+    )(row_index, col_index, block_scale, block_tiles, operand)
+
+
 def forward_local(block_tiles, block_scale, row_index, col_index, operand):
     edge = block_tiles.shape[-1]
-    width = operand.shape[-1]
-    picked = operand.reshape(-1, edge, width)[col_index]
-    products = jnp.einsum("bij,bjk->bik", block_tiles, picked, preferred_element_type=jnp.float32)
-    products = products * block_scale[:, None, None]
-    selector = (row_index[None, :] == jnp.arange(BLK_ROWS, dtype=jnp.int32)[:, None]).astype(
-        jnp.float32
-    )
-    summed = jnp.einsum("rb,bik->rik", selector, products, precision=HIGH)
-    return summed.reshape(BLK_ROWS * edge, width)
+    out_shape = (BLK_ROWS * edge, operand.shape[-1])
+    return block_product(forward_kernel, block_tiles, block_scale, row_index, col_index, operand, out_shape)
 
 
 def backward_local(block_tiles, block_scale, row_index, col_index, operand, col_count):
     edge = block_tiles.shape[-1]
-    width = operand.shape[-1]
-    picked = operand.reshape(-1, edge, width)[row_index]
-    products = jnp.einsum("bij,bik->bjk", block_tiles, picked, preferred_element_type=jnp.float32)
-    products = products * block_scale[:, None, None]
-    selector = (col_index[None, :] == jnp.arange(col_count, dtype=jnp.int32)[:, None]).astype(
-        jnp.float32
-    )
-    summed = jnp.einsum("cb,bjk->cjk", selector, products, precision=HIGH)
-    return summed.reshape(col_count * edge, width)
+    out_shape = (operand.shape[-1], col_count * edge)
+    flipped = block_product(
+        backward_kernel, block_tiles, block_scale, row_index, col_index, operand.T, out_shape
+    )
+    return flipped.T
 
 
 def degree_local(block_tiles, block_scale, row_index, col_index, col_count):

time: 524 us -> 523 us (level); the launches traced: 520 us -> 513 us
  Pallas kernels: 214 us -> 248 us
  matrix products: 58.2 us -> 32.5 us
  local copies, waits for them, and re-layouts: 41.8 us -> 28.2 us
    dot_general x8 -> x0, matrix products: 36.8 us -> none  [the longest x2 11.6 us: forward_local(): jnp.einsum('bij,bjk->bik', block_tiles, picked, preferred_element_type=jn...]
    pallas_call x0 -> x4, Pallas kernels: none -> 34.3 us  [block_product(): pl.pallas_call(kernel, grid_spec=grid_spec, out_shape=jax.ShapeDtypeStruc...]
    gather x4 -> x0, local copies, waits for them, and re-layouts: 8.67 us -> none  [the longest x2 4.34 us: forward_local(): picked = operand.reshape(-1, edge, width)[col_index]]
    pallas_call x0 -> x2, local copies, waits for them, and re-layouts: none -> 7.61 us  [block_product(): pl.pallas_call(kernel, grid_spec=grid_spec, out_shape=jax.ShapeDtypeStruc...]
    another operation x5, matrix products: 7.01 us -> 13.9 us  [orthonormal(): lax.linalg.triangular_solve(factor, block, left_side=False, lower=True, t...]
    another operation x2 -> x0, local copies, waits for them, and re-layouts: 5.59 us -> none  [claim_scatter(): bits = value.reshape(2, 2, 2, 2, 2, 2, rows, width)]
where the time goes in v5:
time: 523 us; the launch traced here: 513 us
  Pallas kernels  248 us (47%)
  waiting for transfers between devices  101 us (19%)
  other arithmetic  66.9 us (13%)
  matrix products  32.5 us (6%)
  local copies, waits for them, and re-layouts  28.2 us (5%)
  blocking collectives  21.3 us (4%)
  between operations  15.1 us (3%)
    pallas_call x2, Pallas kernels, claim_halving(): pl.pallas_call(functools.partial(halving_kernel, stages, gather), out_sha...  121 us
    pallas_call x4, Pallas kernels, group_sum(): pl.pallas_call(functools.partial(group_kernel, tuple(spec)), out_shape=ja...  92.9 us
    all_gather x2, waiting for transfers between devices, backward_partial(): gathered = lax.all_gather(operand, FEAT, axis=0, tiled=True)  42.6 us
    pallas_call x4, Pallas kernels, block_product(): pl.pallas_call(kernel, grid_spec=grid_spec, out_shape=jax.ShapeDtypeStruc...  34.3 us
    another operation x15, other arithmetic, orthonormal(): factor = jnp.linalg.cholesky(gram_total)  32.6 us
    reduce_scatter x1, waiting for transfers between devices, per_device(): lax.psum_scatter(second_partial, FEAT, scatter_dimension=0, tiled=True)  31.6 us
    reduce_scatter x1, waiting for transfers between devices, per_device(): lax.psum_scatter(first_partial, FEAT, scatter_dimension=0, tiled=True)  26.7 us
    another operation x6, other arithmetic, orthonormal(): lax.linalg.triangular_solve(factor, block, left_side=False, lower=True, t...  25.1 us
  transfers between devices with their start and end apart: 4, of which 4 were waited for; matrix products, arithmetic and copies ran while one was open for 0% of the time, Pallas kernels for 0%

profile of v5, /device:TPU:64, one launch (start us, length us, event | category | flops | bytes accessed | tf_op | source)
XLA Modules:
  0.0 513.4 jit_solution(8345582437937890425)
XLA Ops:
  13.7 19.1 %shard_map.76 = f32[32,128]{1,0:T(8,128)} custom-call(f32[32,128]{1,0:T(8,128)} %fusion.5.x_ref), custom_call_target="tpu_custom_call" | custom-call | tf_op jit(solution)/shard_map/pallas_call | solution.py:193
  33.7 10.7 %all-reduce.1 = (f32[64,64]{0,1:T(8,128)S(1)}, f32[8192]{0:T(1024)S(1)}) all-reduce(f32[64,64]{0,1:T(8,128)S(1)} %fusion.64, f32[8192]{0:T(1024)S(1)} %convolution_bitcast_fusion.4), channel_id=1, replica_groups=mesh['yh'=2,'x'=4,'z'=8,'yl'=2,'c'=2] {'yl','c'}, use_global_device_ids=true, to_apply=%region_3.0 | all-reduce | flops 12288 | bytes 98304 | tf_op jit(solution)/shard_map/psum | solution.py:327
  44.5 5.8 %cholesky.89 = f32[64,64]{1,0:T(8,128)S(1)} custom-call(f32[64,64]{1,0:T(8,128)S(1)} %fusion.19), custom_call_target="Cholesky" | custom-call | tf_op jit(solution)/shard_map/jit(cholesky)/cholesky | solution.py:115
  51.7 4.9 custom-call.14
  56.6 5.5 %multiply_convert_fusion.1 = (bf16[4096,64]{1,0:T(8,128)(2,1)}, f32[4096,64]{1,0:T(8,128)}) fusion(f32[4096]{0:T(1024)S(1)} %rsqrt_bitcast_fusion, f32[4096,64]{0,1:T(8,128)S(1)} %copy-done, f32[1,64,64]{1,2,0:T(8,128)S(1)} %custom-call.14), kind=kOutput, calls=%fused_computation.9 | convolution fusion | flops 201850880 | bytes 2654208 | tf_op jit(solution)/shard_map/triangular_solve/dot.9 | solution.py:116
  62.1 9.2 %shard_map.77 = f32[8192,64]{1,0:T(8,128)} custom-call(s32[128]{0:T(128)} %bitcast.126, s32[128]{0:T(128)} %bitcast.131, f32[128]{0:T(128)} %bitcast.120, bf16[128,128,128]{2,1,0:T(8,128)(2,1)} %bitcast.111, bf16[4096,64]{1,0:T(8,128)(2,1)} %get-tuple-element.27.operand_ref), custom_call_target="tpu_custom_call" | custom-call | flops 268435456 | bytes 6815744 | tf_op jit(solution)/shard_map/pallas_call | solution.py:69
  71.3 3.8 copy.41
  77.0 26.7 %reduce-scatter.3.cloned.1.call-done = f32[2048,64]{0,1:T(8,128)} async-done(((f32[8192,64]{0,1:T(8,128)}), f32[2048,64]{0,1:T(8,128)}) %reduce-scatter.3.cloned.1.call-update) | async-done | bytes 524304 | tf_op jit(solution)/shard_map/reduce_scatter | solution.py:331
  106.2 24.7 %shard_map.78 = f32[64,64]{1,0:T(8,128)} custom-call(f32[64,64]{1,0:T(8,128)} %fusion.1.x_ref), custom_call_target="tpu_custom_call" | custom-call | tf_op jit(solution)/shard_map/pallas_call | solution.py:193
  132.4 5.8 %cholesky.100 = f32[64,64]{1,0:T(8,128)S(1)} custom-call(f32[64,64]{1,0:T(8,128)S(1)} %fusion.17), custom_call_target="Cholesky" | custom-call | tf_op jit(solution)/shard_map/jit(cholesky)/cholesky | solution.py:115
  139.6 4.9 custom-call.15
  147.2 21.3 %all-gather.3.cloned.1.call-done = bf16[8192,64]{0,1:T(8,128)(2,1)} async-done(((bf16[2048,64]{0,1:T(8,128)(2,1)}), bf16[8192,64]{0,1:T(8,128)(2,1)}) %all-gather.3.cloned.1.call-update) | async-done | bytes 1048592 | tf_op jit(solution)/shard_map/all_gather | solution.py:339
  168.5 8.0 %shard_map.79 = f32[64,4096]{1,0:T(8,128)} custom-call(s32[128]{0:T(128)} %bitcast.127, s32[128]{0:T(128)} %bitcast.132, f32[128]{0:T(128)} %bitcast.121, bf16[128,128,128]{2,1,0:T(8,128)(2,1)} %bitcast.112, bf16[64,8192]{1,0:T(8,128)(2,1)} %bitcast.119), custom_call_target="tpu_custom_call" | custom-call | flops 268435456 | bytes 6291456 | tf_op jit(solution)/shard_map/pallas_call | solution.py:69
  179.6 75.6 %shard_map.80 = f32[2048,128]{1,0:T(8,128)} custom-call(f32[2048,128]{1,0:T(8,128)} %reshape.67.x_ref), custom_call_target="tpu_custom_call" | custom-call | tf_op jit(solution)/shard_map/pallas_call | solution.py:282
  258.0 4.6 convolution_subtract_fusion
  262.6 3.6 fusion.65
  266.2 10.6 %psum.15 = f32[64,64]{0,1:T(8,128)S(1)} all-reduce(f32[64,64]{0,1:T(8,128)S(1)} %fusion.65), channel_id=1, replica_groups=mesh['yh'=2,'x'=4,'z'=8,'yl'=2,'c'=2] {'yl','c'}, use_global_device_ids=true, to_apply=%region_7.11 | all-reduce | flops 4096 | bytes 32768 | tf_op jit(solution)/shard_map/psum | solution.py:345
  276.9 5.8 %cholesky.111 = f32[64,64]{1,0:T(8,128)S(1)} custom-call(f32[64,64]{1,0:T(8,128)S(1)} %fusion.15), custom_call_target="Cholesky" | custom-call | tf_op jit(solution)/shard_map/jit(cholesky)/cholesky | solution.py:115
  284.1 4.9 custom-call.16
  289.0 3.5 multiply_convert_fusion
  292.5 9.2 %shard_map.81 = f32[8192,64]{1,0:T(8,128)} custom-call(s32[128]{0:T(128)} %bitcast.128, s32[128]{0:T(128)} %bitcast.133, f32[128]{0:T(128)} %bitcast.122, bf16[128,128,128]{2,1,0:T(8,128)(2,1)} %bitcast.113, bf16[4096,64]{1,0:T(8,128)(2,1)} %get-tuple-element.31.operand_ref), custom_call_target="tpu_custom_call" | custom-call | flops 268435456 | bytes 6815744 | tf_op jit(solution)/shard_map/pallas_call | solution.py:69
  301.7 3.8 copy.48
  305.6 31.6 %reduce-scatter.5.cloned.1.call-done = f32[2048,64]{0,1:T(8,128)} async-done(((f32[8192,64]{0,1:T(8,128)}), f32[2048,64]{0,1:T(8,128)}) %reduce-scatter.5.cloned.1.call-update) | async-done | bytes 524304 | tf_op jit(solution)/shard_map/reduce_scatter | solution.py:348
  340.7 24.7 %shard_map.82 = f32[64,64]{1,0:T(8,128)} custom-call(f32[64,64]{1,0:T(8,128)} %fusion.66.x_ref), custom_call_target="tpu_custom_call" | custom-call | tf_op jit(solution)/shard_map/pallas_call | solution.py:193
  366.9 5.8 %cholesky.122 = f32[64,64]{1,0:T(8,128)S(1)} custom-call(f32[64,64]{1,0:T(8,128)S(1)} %fusion.13), custom_call_target="Cholesky" | custom-call | tf_op jit(solution)/shard_map/jit(cholesky)/cholesky | solution.py:115
  374.1 4.9 custom-call.17
  380.7 21.3 %all-gather.5.cloned.1.call-done = bf16[8192,64]{0,1:T(8,128)(2,1)} async-done(((bf16[2048,64]{0,1:T(8,128)(2,1)}), bf16[8192,64]{0,1:T(8,128)(2,1)}) %all-gather.5.cloned.1.call-update) | async-done | bytes 1048592 | tf_op jit(solution)/shard_map/all_gather | solution.py:339
  401.9 8.0 %shard_map.83 = f32[64,4096]{1,0:T(8,128)} custom-call(s32[128]{0:T(128)} %bitcast.129, s32[128]{0:T(128)} %bitcast.134, f32[128]{0:T(128)} %bitcast.123, bf16[128,128,128]{2,1,0:T(8,128)(2,1)} %bitcast.114, bf16[64,8192]{1,0:T(8,128)(2,1)} %bitcast.118), custom_call_target="tpu_custom_call" | custom-call | flops 268435456 | bytes 6291456 | tf_op jit(solution)/shard_map/pallas_call | solution.py:69
  418.2 45.3 %shard_map.84 = f32[32,128]{1,0:T(8,128)} custom-call(f32[2048,128]{1,0:T(8,128)} %reshape_reshape.3.x_ref), custom_call_target="tpu_custom_call" | custom-call | tf_op jit(solution)/shard_map/pallas_call | solution.py:282
  466.7 24.6 %shard_map.85 = f32[64,64]{1,0:T(8,128)} custom-call(f32[64,64]{1,0:T(8,128)} %fusion.67.x_ref), custom_call_target="tpu_custom_call" | custom-call | tf_op jit(solution)/shard_map/pallas_call | solution.py:193
  492.9 5.8 %cholesky.133 = f32[64,64]{1,0:T(8,128)S(1)} custom-call(f32[64,64]{1,0:T(8,128)S(1)} %fusion.11), custom_call_target="Cholesky" | custom-call | tf_op jit(solution)/shard_map/jit(cholesky)/cholesky | solution.py:115
  500.8 4.9 custom-call.11
  (70 shorter events, 49.4 us)
Async XLA Ops:
  7.2 1.2 copy-start
  7.2 96.6 %reduce-scatter.3.cloned.1.call-start = ((), (), s32[]{:S(2)}) async-start(), calls=%async_computation.2 | async-start | bytes 2621440 | tf_op jit(solution)/shard_map/reduce_scatter | solution.py:331
  9.4 3.5 copy-start.2
  9.4 3.5 copy-start.4
  9.4 24.1 %copy-start.3 = (s32[1,1,128]{2,1,0:T(1,128)S(1)}, s32[1,1,128]{2,1,0:T(1,128)}, u32[]{:S(2)}) copy-start(s32[1,1,128]{2,1,0:T(1,128)} %param.12) | copy-start | bytes 1540
  75.1 0.7 copy-start.5
  75.1 93.4 %all-gather.3.cloned.1.call-start = ((), (), s32[]{:S(2)}) async-start(), calls=%async_computation.3 | async-start | bytes 1310720 | tf_op jit(solution)/shard_map/all_gather | solution.py:339
  147.1 190.1 %reduce-scatter.5.cloned.1.call-start = ((), (), s32[]{:S(2)}) async-start(), calls=%async_computation.4 | async-start | bytes 2621440 | tf_op jit(solution)/shard_map/reduce_scatter | solution.py:348
  305.5 31.7 %copy-start.1 = (f32[2048,64]{0,1:T(8,128)S(1)}, f32[2048,64]{0,1:T(8,128)}, u32[]{:S(2)}) copy-start(f32[2048,64]{0,1:T(8,128)} %get-tuple-element.30) | copy-start | bytes 1572868
  305.5 96.4 %all-gather.5.cloned.1.call-start = ((), (), s32[]{:S(2)}) async-start(), calls=%async_computation.5 | async-start | bytes 1310720 | tf_op jit(solution)/shard_map/all_gather | solution.py:339
Sparse Core Ops, SparseCore 0:
  75.2 28.4 reduce-scatter.2
  147.2 21.1 all-gather.2
  305.7 31.4 reduce-scatter.4
  380.7 21.1 all-gather.4

commit v6 on v5

--- a/solution.py
+++ b/solution.py
@@ -111,12 +111,33 @@
     return jnp.dot(block.T, block, precision=HIGH)
 
 
+def factor_kernel(g_ref, o_ref):
+    n = g_ref.shape[0]
+    o_ref[:, :n] = g_ref[...]
+    rows = lax.broadcasted_iota(jnp.int32, (n, 2 * n), 0)
+    cols = lax.broadcasted_iota(jnp.int32, (n, 2 * n), 1)
+    o_ref[:, n:] = jnp.where(rows[:, n:] == cols[:, n:] - n, 1.0, 0.0).astype(o_ref.dtype)
+    m = o_ref[...]
+    below = lax.broadcasted_iota(jnp.int32, (n, 1), 0)
+    for j in range(n):
+        factor = jnp.where(below > j, m[:, j : j + 1] / m[j : j + 1, j : j + 1], 0.0)
+        m = m - factor * m[j : j + 1, :]
+    diagonal = jnp.sum(jnp.where(rows == cols, m, 0.0), axis=1, keepdims=True)
+    m = m * lax.rsqrt(diagonal)
+    o_ref[...] = jnp.where((cols < n) & (cols < rows), 0.0, m)
+
+
 def orthonormal(block, gram_total):
-    factor = jnp.linalg.cholesky(gram_total)
-    basis = lax.linalg.triangular_solve(
-        factor, block, left_side=False, lower=True, transpose_a=True
-    )
-    return (basis, factor.T)
+    n = gram_total.shape[0]
+    both = pl.pallas_call(
+        factor_kernel,
+        out_shape=jax.ShapeDtypeStruct((n, 2 * n), jnp.float32),
+        in_specs=[pl.BlockSpec(memory_space=pltpu.VMEM)],
+        out_specs=pl.BlockSpec(memory_space=pltpu.VMEM),
+    )(gram_total)
+    upper, inverse = both[:, :n], both[:, n:]
+    basis = jnp.dot(block, inverse.T, precision=HIGH)
+    return (basis, upper)
 
 
 def group_kernel(groups, x_ref, o_ref, slots, send_sem, recv_sem):

time: 523 us -> 492 us (0.941); the launches traced: 513 us -> 490 us
  other arithmetic: 66.9 us -> 9.04 us
  Pallas kernels: 248 us -> 281 us
    another operation x21 -> x0, other arithmetic: 57.7 us -> none  [the longest x15 32.6 us: orthonormal(): factor = jnp.linalg.cholesky(gram_total)]
    pallas_call x0 -> x5, Pallas kernels: none -> 33.3 us  [orthonormal(): pl.pallas_call(factor_kernel, out_shape=jax.ShapeDtypeStruct((n, 2 * n),...]
    another operation x5 -> x0, matrix products: 13.9 us -> none  [orthonormal(): lax.linalg.triangular_solve(factor, block, left_side=False, lower=True, t...]
    dot_general x0 -> x5, matrix products: none -> 12.5 us  [orthonormal(): basis = jnp.dot(block, inverse.T, precision=HIGH)]
where the time goes in v6:
time: 492 us; the launch traced here: 490 us
  Pallas kernels  281 us (57%)
  waiting for transfers between devices  99.3 us (20%)
  matrix products  31 us (6%)
  local copies, waits for them, and re-layouts  30.3 us (6%)
  blocking collectives  23.6 us (5%)
  between operations  14.6 us (3%)
  other arithmetic  9.04 us (2%)
    pallas_call x2, Pallas kernels, claim_halving(): pl.pallas_call(functools.partial(halving_kernel, stages, gather), out_sha...  121 us
    pallas_call x4, Pallas kernels, group_sum(): pl.pallas_call(functools.partial(group_kernel, tuple(spec)), out_shape=ja...  92.7 us
    all_gather x2, waiting for transfers between devices, backward_partial(): gathered = lax.all_gather(operand, FEAT, axis=0, tiled=True)  41.7 us
    pallas_call x4, Pallas kernels, block_product(): pl.pallas_call(kernel, grid_spec=grid_spec, out_shape=jax.ShapeDtypeStruc...  34.3 us
    pallas_call x5, Pallas kernels, orthonormal(): pl.pallas_call(factor_kernel, out_shape=jax.ShapeDtypeStruct((n, 2 * n),...  33.3 us
    reduce_scatter x1, waiting for transfers between devices, per_device(): lax.psum_scatter(second_partial, FEAT, scatter_dimension=0, tiled=True)  31.2 us
    reduce_scatter x1, waiting for transfers between devices, per_device(): lax.psum_scatter(first_partial, FEAT, scatter_dimension=0, tiled=True)  26.4 us
    psum x1, blocking collectives, per_device(): start_total = lax.psum(gram_of(start_basis), FEAT)  12.6 us
  transfers between devices with their start and end apart: 4, of which 4 were waited for; matrix products, arithmetic and copies ran while one was open for 0% of the time, Pallas kernels for 0%

profile of v6, /device:TPU:64, one launch (start us, length us, event | category | flops | bytes accessed | tf_op | source)
XLA Modules:
  0.0 489.7 jit_solution(13851613746320080039)
XLA Ops:
  9.4 3.4 convert_reduce_fusion.1
  13.1 12.6 %all-reduce.1 = (f32[64,64]{1,0:T(8,128)}, f32[8192]{0:T(1024)S(1)}) all-reduce(f32[64,64]{1,0:T(8,128)S(1)} %fusion.29, f32[8192]{0:T(1024)S(1)} %convolution_bitcast_fusion), channel_id=1, replica_groups=mesh['yh'=2,'x'=4,'z'=8,'yl'=2,'c'=2] {'yl','c'}, use_global_device_ids=true, to_apply=%region_3.0 | all-reduce | flops 12288 | bytes 98304 | tf_op jit(solution)/shard_map/psum | solution.py:348
  25.7 6.7 %shard_map.77 = f32[64,128]{1,0:T(8,128)} custom-call(f32[64,64]{1,0:T(8,128)} %get-tuple-element.5.g_ref), custom_call_target="tpu_custom_call" | custom-call | tf_op jit(solution)/shard_map/pallas_call | solution.py:132
  37.0 18.8 %shard_map.76 = f32[32,128]{1,0:T(8,128)} custom-call(f32[32,128]{1,0:T(8,128)} %fusion.7.x_ref), custom_call_target="tpu_custom_call" | custom-call | tf_op jit(solution)/shard_map/pallas_call | solution.py:214
  56.5 2.7 fusion.operand_ref
  59.2 9.2 %shard_map.78 = f32[8192,64]{1,0:T(8,128)} custom-call(s32[128]{0:T(128)} %bitcast.59, s32[128]{0:T(128)} %bitcast.64, f32[128]{0:T(128)} %bitcast.53, bf16[128,128,128]{2,1,0:T(8,128)(2,1)} %bitcast.44, bf16[4096,64]{1,0:T(8,128)(2,1)} %fusion.operand_ref), custom_call_target="tpu_custom_call" | custom-call | flops 268435456 | bytes 6815744 | tf_op jit(solution)/shard_map/pallas_call | solution.py:69
  68.4 3.8 copy.31
  74.1 26.4 %reduce-scatter.3.cloned.1.call-done = f32[2048,64]{0,1:T(8,128)} async-done(((f32[8192,64]{0,1:T(8,128)}), f32[2048,64]{0,1:T(8,128)}) %reduce-scatter.3.cloned.1.call-update) | async-done | bytes 524304 | tf_op jit(solution)/shard_map/reduce_scatter | solution.py:352
  103.0 24.7 %shard_map.79.g_ref = f32[64,64]{1,0:T(8,128)} custom-call(f32[64,64]{1,0:T(8,128)} %fusion.3.x_ref), custom_call_target="tpu_custom_call" | custom-call | tf_op jit(solution)/shard_map/pallas_call | solution.py:214
  127.6 6.7 %shard_map.80 = f32[64,128]{1,0:T(8,128)} custom-call(f32[64,64]{1,0:T(8,128)} %shard_map.79.g_ref), custom_call_target="tpu_custom_call" | custom-call | tf_op jit(solution)/shard_map/pallas_call | solution.py:132
  137.1 21.1 %all-gather.3.cloned.1.call-done = bf16[8192,64]{0,1:T(8,128)(2,1)} async-done(((bf16[2048,64]{0,1:T(8,128)(2,1)}), bf16[8192,64]{0,1:T(8,128)(2,1)}) %all-gather.3.cloned.1.call-update) | async-done | bytes 1048592 | tf_op jit(solution)/shard_map/all_gather | solution.py:360
  158.2 8.0 %shard_map.81 = f32[64,4096]{1,0:T(8,128)} custom-call(s32[128]{0:T(128)} %bitcast.60, s32[128]{0:T(128)} %bitcast.65, f32[128]{0:T(128)} %bitcast.54, bf16[128,128,128]{2,1,0:T(8,128)(2,1)} %bitcast.45, bf16[64,8192]{1,0:T(8,128)(2,1)} %bitcast.52), custom_call_target="tpu_custom_call" | custom-call | flops 268435456 | bytes 6291456 | tf_op jit(solution)/shard_map/pallas_call | solution.py:69
  169.3 75.6 %shard_map.82 = f32[2048,128]{1,0:T(8,128)} custom-call(f32[2048,128]{1,0:T(8,128)} %reshape.47.x_ref), custom_call_target="tpu_custom_call" | custom-call | tf_op jit(solution)/shard_map/pallas_call | solution.py:303
  245.0 2.7 reshape.48
  247.7 5.8 %convolution_subtract_fusion = f32[4096,64]{1,0:T(8,128)S(1)} fusion(f32[64,4096]{1,0:T(8,128)} %copy-done.1, f32[4096,64]{1,0:T(8,128)} %reshape.48, f32[4096]{0:T(1024)S(1)} %rsqrt_bitcast_fusion, f32[64,128]{1,0:T(8,128)S(1)} %copy-done.4), kind=kOutput, calls=%fused_computation.2 | convolution fusion | flops 201850880 | bytes 3194880 | tf_op jit(solution)/shard_map/dot_general | solution.py:365
  253.5 3.6 fusion.30
  257.1 11.0 %psum.15.g_ref = f32[64,64]{1,0:T(8,128)} all-reduce(f32[64,64]{1,0:T(8,128)S(1)} %fusion.30), channel_id=1, replica_groups=mesh['yh'=2,'x'=4,'z'=8,'yl'=2,'c'=2] {'yl','c'}, use_global_device_ids=true, to_apply=%region_5.0 | all-reduce | flops 4096 | bytes 32768 | tf_op jit(solution)/shard_map/psum | solution.py:366
  268.0 6.7 %shard_map.83 = f32[64,128]{1,0:T(8,128)} custom-call(f32[64,64]{1,0:T(8,128)} %psum.15.g_ref), custom_call_target="tpu_custom_call" | custom-call | tf_op jit(solution)/shard_map/pallas_call | solution.py:132
  274.7 4.2 fusion.14
  282.3 9.2 %shard_map.84 = f32[8192,64]{1,0:T(8,128)} custom-call(s32[128]{0:T(128)} %bitcast.61, s32[128]{0:T(128)} %bitcast.66, f32[128]{0:T(128)} %bitcast.55, bf16[128,128,128]{2,1,0:T(8,128)(2,1)} %bitcast.46, bf16[4096,64]{1,0:T(8,128)(2,1)} %multiply_convert_fusion.operand_ref), custom_call_target="tpu_custom_call" | custom-call | flops 268435456 | bytes 6815744 | tf_op jit(solution)/shard_map/pallas_call | solution.py:69
  291.5 3.8 copy.35
  295.5 31.2 %reduce-scatter.5.cloned.1.call-done = f32[2048,64]{0,1:T(8,128)} async-done(((f32[8192,64]{0,1:T(8,128)}), f32[2048,64]{0,1:T(8,128)}) %reduce-scatter.5.cloned.1.call-update) | async-done | bytes 524304 | tf_op jit(solution)/shard_map/reduce_scatter | solution.py:369
  329.6 24.6 %shard_map.85.g_ref = f32[64,64]{1,0:T(8,128)} custom-call(f32[64,64]{1,0:T(8,128)} %fusion.31.x_ref), custom_call_target="tpu_custom_call" | custom-call | tf_op jit(solution)/shard_map/pallas_call | solution.py:214
  354.2 6.7 %shard_map.86 = f32[64,128]{1,0:T(8,128)} custom-call(f32[64,64]{1,0:T(8,128)} %shard_map.85.g_ref), custom_call_target="tpu_custom_call" | custom-call | tf_op jit(solution)/shard_map/pallas_call | solution.py:132
  364.0 20.6 %all-gather.5.cloned.1.call-done = bf16[8192,64]{0,1:T(8,128)(2,1)} async-done(((bf16[2048,64]{0,1:T(8,128)(2,1)}), bf16[8192,64]{0,1:T(8,128)(2,1)}) %all-gather.5.cloned.1.call-update) | async-done | bytes 1048592 | tf_op jit(solution)/shard_map/all_gather | solution.py:360
  384.6 8.0 %shard_map.87 = f32[64,4096]{1,0:T(8,128)} custom-call(s32[128]{0:T(128)} %bitcast.62, s32[128]{0:T(128)} %bitcast.67, f32[128]{0:T(128)} %bitcast.56, bf16[128,128,128]{2,1,0:T(8,128)(2,1)} %bitcast.47, bf16[64,8192]{1,0:T(8,128)(2,1)} %bitcast.51), custom_call_target="tpu_custom_call" | custom-call | flops 268435456 | bytes 6291456 | tf_op jit(solution)/shard_map/pallas_call | solution.py:69
  392.5 2.8 reshape.49
  395.3 2.9 copy.36
  398.2 2.6 reshape_reshape.3.x_ref
  400.8 45.3 %shard_map.88 = f32[32,128]{1,0:T(8,128)} custom-call(f32[2048,128]{1,0:T(8,128)} %reshape_reshape.3.x_ref), custom_call_target="tpu_custom_call" | custom-call | tf_op jit(solution)/shard_map/pallas_call | solution.py:303
  448.8 24.6 %shard_map.89.g_ref = f32[64,64]{1,0:T(8,128)} custom-call(f32[64,64]{1,0:T(8,128)} %fusion.32.x_ref), custom_call_target="tpu_custom_call" | custom-call | tf_op jit(solution)/shard_map/pallas_call | solution.py:214
  473.5 6.7 %shard_map.90 = f32[64,128]{1,0:T(8,128)} custom-call(f32[64,64]{1,0:T(8,128)} %shard_map.89.g_ref), custom_call_target="tpu_custom_call" | custom-call | tf_op jit(solution)/shard_map/pallas_call | solution.py:132
  (55 shorter events, 32.7 us)
Async XLA Ops:
  7.2 1.2 copy-start
  7.2 93.3 %reduce-scatter.3.cloned.1.call-start = ((), (), s32[]{:S(2)}) async-start(), calls=%async_computation.2 | async-start | bytes 2621440 | tf_op jit(solution)/shard_map/reduce_scatter | solution.py:352
  9.4 3.5 copy-start.6
  9.4 3.5 copy-start.7
  34.2 25.0 %copy-start.1 = (f32[64,4096]{1,0:T(8,128)}, f32[64,4096]{1,0:T(8,128)S(1)}, u32[]{:S(2)}) copy-start(f32[64,4096]{1,0:T(8,128)S(1)} %fusion.17) | copy-start | bytes 3145732
  34.2 2.0 copy-start.8
  72.2 0.7 copy-start.9
  72.2 86.0 %all-gather.3.cloned.1.call-start = ((), (), s32[]{:S(2)}) async-start(), calls=%async_computation.3 | async-start | bytes 1310720 | tf_op jit(solution)/shard_map/all_gather | solution.py:360
  136.9 189.8 %reduce-scatter.5.cloned.1.call-start = ((), (), s32[]{:S(2)}) async-start(), calls=%async_computation.4 | async-start | bytes 2621440 | tf_op jit(solution)/shard_map/reduce_scatter | solution.py:369
  245.0 2.7 copy-start.4
  295.2 31.5 %copy-start.2 = (f32[2048,64]{0,1:T(8,128)S(1)}, f32[2048,64]{0,1:T(8,128)}, u32[]{:S(2)}) copy-start(f32[2048,64]{0,1:T(8,128)} %get-tuple-element.8) | copy-start | bytes 1572868
  295.2 31.5 %copy-start.3 = (f32[64,128]{1,0:T(8,128)S(1)}, f32[64,128]{1,0:T(8,128)}, u32[]{:S(2)}) copy-start(f32[64,128]{1,0:T(8,128)} %shard_map.83) | copy-start | bytes 98308
  295.3 89.3 %all-gather.5.cloned.1.call-start = ((), (), s32[]{:S(2)}) async-start(), calls=%async_computation.5 | async-start | bytes 1310720 | tf_op jit(solution)/shard_map/all_gather | solution.py:360
  398.2 48.7 %copy-start.5 = (f32[64,128]{1,0:T(8,128)S(1)}, f32[64,128]{1,0:T(8,128)}, u32[]{:S(2)}) copy-start(f32[64,128]{1,0:T(8,128)} %shard_map.86) | copy-start | bytes 98308
Sparse Core Ops, SparseCore 0:
  72.3 28.1 reduce-scatter.2
  137.0 21.2 all-gather.2
  295.4 31.2 reduce-scatter.4
  363.3 21.2 all-gather.4

commit v7 on v6

--- a/solution.py
+++ b/solution.py
@@ -120,7 +120,7 @@
     m = o_ref[...]
     below = lax.broadcasted_iota(jnp.int32, (n, 1), 0)
     for j in range(n):
-        factor = jnp.where(below > j, m[:, j : j + 1] / m[j : j + 1, j : j + 1], 0.0)
+        factor = jnp.where(below > j, m[:, j : j + 1], 0.0) * (1.0 / m[j : j + 1, j : j + 1])
         m = m - factor * m[j : j + 1, :]
     diagonal = jnp.sum(jnp.where(rows == cols, m, 0.0), axis=1, keepdims=True)
     m = m * lax.rsqrt(diagonal)

time: 492 us -> 492 us (level)
  no operation moved by 1% of the time
where the time goes in v7:
time: 492 us; the launch traced here: 490 us
  Pallas kernels  282 us (57%)
  waiting for transfers between devices  98.9 us (20%)
  matrix products  31.1 us (6%)
  local copies, waits for them, and re-layouts  30.3 us (6%)
  blocking collectives  23.9 us (5%)
  between operations  14.6 us (3%)
  other arithmetic  9.04 us (2%)
    pallas_call x2, Pallas kernels, claim_halving(): pl.pallas_call(functools.partial(halving_kernel, stages, gather), out_sha...  121 us
    pallas_call x4, Pallas kernels, group_sum(): pl.pallas_call(functools.partial(group_kernel, tuple(spec)), out_shape=ja...  92.9 us
    all_gather x2, waiting for transfers between devices, backward_partial(): gathered = lax.all_gather(operand, FEAT, axis=0, tiled=True)  41.7 us
    pallas_call x4, Pallas kernels, block_product(): pl.pallas_call(kernel, grid_spec=grid_spec, out_shape=jax.ShapeDtypeStruc...  34.3 us
    pallas_call x5, Pallas kernels, orthonormal(): pl.pallas_call(factor_kernel, out_shape=jax.ShapeDtypeStruct((n, 2 * n),...  33.4 us
    reduce_scatter x1, waiting for transfers between devices, per_device(): lax.psum_scatter(second_partial, FEAT, scatter_dimension=0, tiled=True)  30.9 us
    reduce_scatter x1, waiting for transfers between devices, per_device(): lax.psum_scatter(first_partial, FEAT, scatter_dimension=0, tiled=True)  26.2 us
    psum x1, blocking collectives, per_device(): start_total = lax.psum(gram_of(start_basis), FEAT)  12.6 us
  transfers between devices with their start and end apart: 4, of which 4 were waited for; matrix products, arithmetic and copies ran while one was open for 0% of the time, Pallas kernels for 0%

profile of v7, /device:TPU:64, one launch (start us, length us, event | category | flops | bytes accessed | tf_op | source)
XLA Modules:
  0.0 489.8 jit_solution(4801384166053460610)
XLA Ops:
  9.4 3.4 convert_reduce_fusion.1
  13.1 12.6 %all-reduce.1 = (f32[64,64]{1,0:T(8,128)}, f32[8192]{0:T(1024)S(1)}) all-reduce(f32[64,64]{1,0:T(8,128)S(1)} %fusion.29, f32[8192]{0:T(1024)S(1)} %convolution_bitcast_fusion), channel_id=1, replica_groups=mesh['yh'=2,'x'=4,'z'=8,'yl'=2,'c'=2] {'yl','c'}, use_global_device_ids=true, to_apply=%region_3.0 | all-reduce | flops 12288 | bytes 98304 | tf_op jit(solution)/shard_map/psum | solution.py:348
  25.7 6.7 %shard_map.77 = f32[64,128]{1,0:T(8,128)} custom-call(f32[64,64]{1,0:T(8,128)} %get-tuple-element.5.g_ref), custom_call_target="tpu_custom_call" | custom-call | tf_op jit(solution)/shard_map/pallas_call | solution.py:132
  37.0 18.9 %shard_map.76 = f32[32,128]{1,0:T(8,128)} custom-call(f32[32,128]{1,0:T(8,128)} %fusion.7.x_ref), custom_call_target="tpu_custom_call" | custom-call | tf_op jit(solution)/shard_map/pallas_call | solution.py:214
  56.7 2.7 fusion.operand_ref
  59.4 9.2 %shard_map.78 = f32[8192,64]{1,0:T(8,128)} custom-call(s32[128]{0:T(128)} %bitcast.59, s32[128]{0:T(128)} %bitcast.64, f32[128]{0:T(128)} %bitcast.53, bf16[128,128,128]{2,1,0:T(8,128)(2,1)} %bitcast.44, bf16[4096,64]{1,0:T(8,128)(2,1)} %fusion.operand_ref), custom_call_target="tpu_custom_call" | custom-call | flops 268435456 | bytes 6815744 | tf_op jit(solution)/shard_map/pallas_call | solution.py:69
  68.6 3.8 copy.31
  74.3 26.2 %reduce-scatter.3.cloned.1.call-done = f32[2048,64]{0,1:T(8,128)} async-done(((f32[8192,64]{0,1:T(8,128)}), f32[2048,64]{0,1:T(8,128)}) %reduce-scatter.3.cloned.1.call-update) | async-done | bytes 524304 | tf_op jit(solution)/shard_map/reduce_scatter | solution.py:352
  103.0 24.6 %shard_map.79.g_ref = f32[64,64]{1,0:T(8,128)} custom-call(f32[64,64]{1,0:T(8,128)} %fusion.3.x_ref), custom_call_target="tpu_custom_call" | custom-call | tf_op jit(solution)/shard_map/pallas_call | solution.py:214
  127.6 6.7 %shard_map.80 = f32[64,128]{1,0:T(8,128)} custom-call(f32[64,64]{1,0:T(8,128)} %shard_map.79.g_ref), custom_call_target="tpu_custom_call" | custom-call | tf_op jit(solution)/shard_map/pallas_call | solution.py:132
  137.1 21.2 %all-gather.3.cloned.1.call-done = bf16[8192,64]{0,1:T(8,128)(2,1)} async-done(((bf16[2048,64]{0,1:T(8,128)(2,1)}), bf16[8192,64]{0,1:T(8,128)(2,1)}) %all-gather.3.cloned.1.call-update) | async-done | bytes 1048592 | tf_op jit(solution)/shard_map/all_gather | solution.py:360
  158.3 8.0 %shard_map.81 = f32[64,4096]{1,0:T(8,128)} custom-call(s32[128]{0:T(128)} %bitcast.60, s32[128]{0:T(128)} %bitcast.65, f32[128]{0:T(128)} %bitcast.54, bf16[128,128,128]{2,1,0:T(8,128)(2,1)} %bitcast.45, bf16[64,8192]{1,0:T(8,128)(2,1)} %bitcast.52), custom_call_target="tpu_custom_call" | custom-call | flops 268435456 | bytes 6291456 | tf_op jit(solution)/shard_map/pallas_call | solution.py:69
  169.4 75.6 %shard_map.82 = f32[2048,128]{1,0:T(8,128)} custom-call(f32[2048,128]{1,0:T(8,128)} %reshape.47.x_ref), custom_call_target="tpu_custom_call" | custom-call | tf_op jit(solution)/shard_map/pallas_call | solution.py:303
  245.0 2.7 reshape.48
  247.7 5.8 %convolution_subtract_fusion = f32[4096,64]{1,0:T(8,128)S(1)} fusion(f32[64,4096]{1,0:T(8,128)} %copy-done.1, f32[4096,64]{1,0:T(8,128)} %reshape.48, f32[4096]{0:T(1024)S(1)} %rsqrt_bitcast_fusion, f32[64,128]{1,0:T(8,128)S(1)} %copy-done.4), kind=kOutput, calls=%fused_computation.2 | convolution fusion | flops 201850880 | bytes 3194880 | tf_op jit(solution)/shard_map/dot_general | solution.py:365
  253.5 3.6 fusion.30
  257.1 11.2 %psum.15.g_ref = f32[64,64]{1,0:T(8,128)} all-reduce(f32[64,64]{1,0:T(8,128)S(1)} %fusion.30), channel_id=1, replica_groups=mesh['yh'=2,'x'=4,'z'=8,'yl'=2,'c'=2] {'yl','c'}, use_global_device_ids=true, to_apply=%region_5.0 | all-reduce | flops 4096 | bytes 32768 | tf_op jit(solution)/shard_map/psum | solution.py:366
  268.3 6.7 %shard_map.83 = f32[64,128]{1,0:T(8,128)} custom-call(f32[64,64]{1,0:T(8,128)} %psum.15.g_ref), custom_call_target="tpu_custom_call" | custom-call | tf_op jit(solution)/shard_map/pallas_call | solution.py:132
  275.0 4.3 fusion.14
  282.6 9.2 %shard_map.84 = f32[8192,64]{1,0:T(8,128)} custom-call(s32[128]{0:T(128)} %bitcast.61, s32[128]{0:T(128)} %bitcast.66, f32[128]{0:T(128)} %bitcast.55, bf16[128,128,128]{2,1,0:T(8,128)(2,1)} %bitcast.46, bf16[4096,64]{1,0:T(8,128)(2,1)} %multiply_convert_fusion.operand_ref), custom_call_target="tpu_custom_call" | custom-call | flops 268435456 | bytes 6815744 | tf_op jit(solution)/shard_map/pallas_call | solution.py:69
  291.8 3.8 copy.35
  295.9 30.9 %reduce-scatter.5.cloned.1.call-done = f32[2048,64]{0,1:T(8,128)} async-done(((f32[8192,64]{0,1:T(8,128)}), f32[2048,64]{0,1:T(8,128)}) %reduce-scatter.5.cloned.1.call-update) | async-done | bytes 524304 | tf_op jit(solution)/shard_map/reduce_scatter | solution.py:369
  329.6 24.7 %shard_map.85.g_ref = f32[64,64]{1,0:T(8,128)} custom-call(f32[64,64]{1,0:T(8,128)} %fusion.31.x_ref), custom_call_target="tpu_custom_call" | custom-call | tf_op jit(solution)/shard_map/pallas_call | solution.py:214
  354.3 6.7 %shard_map.86 = f32[64,128]{1,0:T(8,128)} custom-call(f32[64,64]{1,0:T(8,128)} %shard_map.85.g_ref), custom_call_target="tpu_custom_call" | custom-call | tf_op jit(solution)/shard_map/pallas_call | solution.py:132
  364.2 20.5 %all-gather.5.cloned.1.call-done = bf16[8192,64]{0,1:T(8,128)(2,1)} async-done(((bf16[2048,64]{0,1:T(8,128)(2,1)}), bf16[8192,64]{0,1:T(8,128)(2,1)}) %all-gather.5.cloned.1.call-update) | async-done | bytes 1048592 | tf_op jit(solution)/shard_map/all_gather | solution.py:360
  384.7 8.0 %shard_map.87 = f32[64,4096]{1,0:T(8,128)} custom-call(s32[128]{0:T(128)} %bitcast.62, s32[128]{0:T(128)} %bitcast.67, f32[128]{0:T(128)} %bitcast.56, bf16[128,128,128]{2,1,0:T(8,128)(2,1)} %bitcast.47, bf16[64,8192]{1,0:T(8,128)(2,1)} %bitcast.51), custom_call_target="tpu_custom_call" | custom-call | flops 268435456 | bytes 6291456 | tf_op jit(solution)/shard_map/pallas_call | solution.py:69
  392.6 2.8 reshape.49
  395.4 2.9 copy.36
  398.3 2.6 reshape_reshape.3.x_ref
  400.9 45.3 %shard_map.88 = f32[32,128]{1,0:T(8,128)} custom-call(f32[2048,128]{1,0:T(8,128)} %reshape_reshape.3.x_ref), custom_call_target="tpu_custom_call" | custom-call | tf_op jit(solution)/shard_map/pallas_call | solution.py:303
  448.9 24.6 %shard_map.89.g_ref = f32[64,64]{1,0:T(8,128)} custom-call(f32[64,64]{1,0:T(8,128)} %fusion.32.x_ref), custom_call_target="tpu_custom_call" | custom-call | tf_op jit(solution)/shard_map/pallas_call | solution.py:214
  473.5 6.7 %shard_map.90 = f32[64,128]{1,0:T(8,128)} custom-call(f32[64,64]{1,0:T(8,128)} %shard_map.89.g_ref), custom_call_target="tpu_custom_call" | custom-call | tf_op jit(solution)/shard_map/pallas_call | solution.py:132
  (55 shorter events, 32.7 us)
Async XLA Ops:
  7.2 1.2 copy-start
  7.2 93.4 %reduce-scatter.3.cloned.1.call-start = ((), (), s32[]{:S(2)}) async-start(), calls=%async_computation.2 | async-start | bytes 2621440 | tf_op jit(solution)/shard_map/reduce_scatter | solution.py:352
  9.4 3.5 copy-start.6
  9.4 3.5 copy-start.7
  34.2 25.2 %copy-start.1 = (f32[64,4096]{1,0:T(8,128)}, f32[64,4096]{1,0:T(8,128)S(1)}, u32[]{:S(2)}) copy-start(f32[64,4096]{1,0:T(8,128)S(1)} %fusion.17) | copy-start | bytes 3145732
  34.2 2.0 copy-start.8
  72.4 0.7 copy-start.9
  72.4 85.9 %all-gather.3.cloned.1.call-start = ((), (), s32[]{:S(2)}) async-start(), calls=%async_computation.3 | async-start | bytes 1310720 | tf_op jit(solution)/shard_map/all_gather | solution.py:360
  136.9 189.9 %reduce-scatter.5.cloned.1.call-start = ((), (), s32[]{:S(2)}) async-start(), calls=%async_computation.4 | async-start | bytes 2621440 | tf_op jit(solution)/shard_map/reduce_scatter | solution.py:369
  245.0 2.7 copy-start.4
  295.6 31.2 %copy-start.2 = (f32[2048,64]{0,1:T(8,128)S(1)}, f32[2048,64]{0,1:T(8,128)}, u32[]{:S(2)}) copy-start(f32[2048,64]{0,1:T(8,128)} %get-tuple-element.8) | copy-start | bytes 1572868
  295.6 31.2 %copy-start.3 = (f32[64,128]{1,0:T(8,128)S(1)}, f32[64,128]{1,0:T(8,128)}, u32[]{:S(2)}) copy-start(f32[64,128]{1,0:T(8,128)} %shard_map.83) | copy-start | bytes 98308
  295.6 89.0 %all-gather.5.cloned.1.call-start = ((), (), s32[]{:S(2)}) async-start(), calls=%async_computation.5 | async-start | bytes 1310720 | tf_op jit(solution)/shard_map/all_gather | solution.py:360
  398.3 48.7 %copy-start.5 = (f32[64,128]{1,0:T(8,128)S(1)}, f32[64,128]{1,0:T(8,128)}, u32[]{:S(2)}) copy-start(f32[64,128]{1,0:T(8,128)} %shard_map.86) | copy-start | bytes 98308
Sparse Core Ops, SparseCore 0:
  72.5 27.9 reduce-scatter.2
  137.0 21.2 all-gather.2
  295.7 31.0 reduce-scatter.4
  363.4 21.1 all-gather.4

commit v8 on v7

--- a/solution.py
+++ b/solution.py
@@ -30,10 +30,12 @@
 
     for t in range(tiles_ref.shape[0]):
         b = step * tiles_ref.shape[0] + t
-        picked = operand_ref[pl.ds(pl.multiple_of(cols_ref[b] * edge, edge), edge), :]
-        product = jnp.dot(tiles_ref[t], picked, preferred_element_type=jnp.float32) * scale_ref[b]
+        picked = operand_ref[:, pl.ds(pl.multiple_of(cols_ref[b] * edge, edge), edge)]
+        product = lax.dot_general(
+            picked, tiles_ref[t], (((1,), (1,)), ((), ())), preferred_element_type=jnp.float32
+        )
         target = pl.ds(pl.multiple_of(rows_ref[b] * edge, edge), edge)
-        out_ref[target, :] = out_ref[target, :] + product
+        out_ref[:, target] = out_ref[:, target] + product * scale_ref[b]
 
 
 def backward_kernel(rows_ref, cols_ref, scale_ref, tiles_ref, operand_ref, out_ref):
@@ -80,8 +82,10 @@
 
 def forward_local(block_tiles, block_scale, row_index, col_index, operand):
     edge = block_tiles.shape[-1]
-    out_shape = (BLK_ROWS * edge, operand.shape[-1])
-    return block_product(forward_kernel, block_tiles, block_scale, row_index, col_index, operand, out_shape)
+    out_shape = (operand.shape[-1], BLK_ROWS * edge)
+    return block_product(
+        forward_kernel, block_tiles, block_scale, row_index, col_index, operand.T, out_shape
+    )
 
 
 def backward_local(block_tiles, block_scale, row_index, col_index, operand, col_count):
@@ -349,7 +353,7 @@
     first_basis, _ = orthonormal(start_basis, start_total)
     first_operand = (col_scale[:, None] * first_basis).astype(jnp.bfloat16)
     first_partial = forward_local(tiles_here, scale_here, rows_here, cols_here, first_operand)
-    first_sums = lax.psum_scatter(first_partial, FEAT, scatter_dimension=0, tiled=True)
+    first_sums = lax.psum_scatter(first_partial, FEAT, scatter_dimension=1, tiled=True).T
     row_scale = lax.rsqrt(row_total + 1.0)
 
     def row_orthonormal(block, cid):
@@ -366,7 +370,7 @@
     v_second, a_second = orthonormal(update, lax.psum(gram_of(update), FEAT))
     scaled = (col_scale[:, None] * v_second).astype(jnp.bfloat16)
     second_partial = forward_local(tiles_here, scale_here, rows_here, cols_here, scaled)
-    second_sums = lax.psum_scatter(second_partial, FEAT, scatter_dimension=0, tiled=True)
+    second_sums = lax.psum_scatter(second_partial, FEAT, scatter_dimension=1, tiled=True).T
     p_second = row_scale[:, None] * second_sums - jnp.dot(u_first, a_second.T, precision=HIGH)
     u_second, b_second = row_orthonormal(p_second, 2)
     own_sums = claim_scatter(backward_partial(u_second))

time: 492 us -> 470 us (0.955)
  local copies, waits for them, and re-layouts: 30.3 us -> 19.1 us
  matrix products: 31.1 us -> 24 us
    pallas_call x2 -> x0, local copies, waits for them, and re-layouts: 7.57 us -> none  [block_product(): pl.pallas_call(kernel, grid_spec=grid_spec, out_shape=jax.ShapeDtypeStruc...]
where the time goes in v8:
time: 470 us; the launch traced here: 468 us
  Pallas kernels  282 us (60%)
  waiting for transfers between devices  99.7 us (21%)
  matrix products  24 us (5%)
  blocking collectives  22.4 us (5%)
  local copies, waits for them, and re-layouts  19.1 us (4%)
  between operations  14.7 us (3%)
  other arithmetic  5.76 us (1%)
    pallas_call x2, Pallas kernels, claim_halving(): pl.pallas_call(functools.partial(halving_kernel, stages, gather), out_sha...  121 us
    pallas_call x4, Pallas kernels, group_sum(): pl.pallas_call(functools.partial(group_kernel, tuple(spec)), out_shape=ja...  93.1 us
    all_gather x2, waiting for transfers between devices, backward_partial(): gathered = lax.all_gather(operand, FEAT, axis=0, tiled=True)  41.6 us
    pallas_call x4, Pallas kernels, block_product(): pl.pallas_call(kernel, grid_spec=grid_spec, out_shape=jax.ShapeDtypeStruc...  34 us
    pallas_call x5, Pallas kernels, orthonormal(): pl.pallas_call(factor_kernel, out_shape=jax.ShapeDtypeStruct((n, 2 * n),...  33.4 us
    reduce_scatter x1, waiting for transfers between devices, per_device(): lax.psum_scatter(second_partial, FEAT, scatter_dimension=1, tiled=True)  31.3 us
    reduce_scatter x1, waiting for transfers between devices, per_device(): lax.psum_scatter(first_partial, FEAT, scatter_dimension=1, tiled=True)  26.7 us
    psum x1, blocking collectives, per_device(): start_total = lax.psum(gram_of(start_basis), FEAT)  11.3 us
  transfers between devices with their start and end apart: 4, of which 4 were waited for; matrix products, arithmetic and copies ran while one was open for 0% of the time, Pallas kernels for 0%

profile of v8, /device:TPU:64, one launch (start us, length us, event | category | flops | bytes accessed | tf_op | source)
XLA Modules:
  0.0 467.7 jit_solution(2878400066235314399)
XLA Ops:
  7.2 3.5 convert_reduce_fusion.1
  11.6 19.1 %shard_map.76 = f32[32,128]{1,0:T(8,128)} custom-call(f32[32,128]{1,0:T(8,128)} %fusion.7.x_ref), custom_call_target="tpu_custom_call" | custom-call | tf_op jit(solution)/shard_map/pallas_call | solution.py:218
  32.6 11.3 %all-reduce.1 = (f32[64,64]{1,0:T(8,128)}, f32[8192]{0:T(1024)S(1)}) all-reduce(f32[64,64]{1,0:T(8,128)S(1)} %fusion.29, f32[8192]{0:T(1024)S(1)} %convolution_bitcast_fusion), channel_id=1, replica_groups=mesh['yh'=2,'x'=4,'z'=8,'yl'=2,'c'=2] {'yl','c'}, use_global_device_ids=true, to_apply=%region_3.0 | all-reduce | flops 12288 | bytes 98304 | tf_op jit(solution)/shard_map/psum | solution.py:352
  43.9 6.7 %shard_map.77 = f32[64,128]{1,0:T(8,128)} custom-call(f32[64,64]{1,0:T(8,128)} %get-tuple-element.5.g_ref), custom_call_target="tpu_custom_call" | custom-call | tf_op jit(solution)/shard_map/pallas_call | solution.py:136
  50.6 2.9 multiply_convert_fusion.1
  53.5 9.1 %shard_map.78 = f32[64,8192]{1,0:T(8,128)} custom-call(s32[128]{0:T(128)} %bitcast.61, s32[128]{0:T(128)} %bitcast.66, f32[128]{0:T(128)} %bitcast.55, bf16[128,128,128]{2,1,0:T(8,128)(2,1)} %bitcast.46, bf16[64,4096]{1,0:T(8,128)(2,1)} %get-tuple-element.7.operand_ref), custom_call_target="tpu_custom_call" | custom-call | flops 268435456 | bytes 6815744 | tf_op jit(solution)/shard_map/pallas_call | solution.py:71
  64.5 26.7 %reduce-scatter.3.cloned.1.call-done = f32[64,2048]{1,0:T(8,128)} async-done(((f32[64,8192]{1,0:T(8,128)}), f32[64,2048]{1,0:T(8,128)}) %reduce-scatter.3.cloned.1.call-update) | async-done | bytes 524304 | tf_op jit(solution)/shard_map/reduce_scatter | solution.py:356
  91.2 2.4 fusion.3.x_ref
  93.6 24.7 %shard_map.79.g_ref = f32[64,64]{1,0:T(8,128)} custom-call(f32[64,64]{1,0:T(8,128)} %fusion.3.x_ref), custom_call_target="tpu_custom_call" | custom-call | tf_op jit(solution)/shard_map/pallas_call | solution.py:218
  118.3 6.7 %shard_map.80 = f32[64,128]{1,0:T(8,128)} custom-call(f32[64,64]{1,0:T(8,128)} %shard_map.79.g_ref), custom_call_target="tpu_custom_call" | custom-call | tf_op jit(solution)/shard_map/pallas_call | solution.py:136
  125.0 2.5 multiply_convert_fusion.3
  127.8 21.1 %all-gather.3.cloned.1.call-done = bf16[8192,64]{0,1:T(8,128)(2,1)} async-done(((bf16[2048,64]{0,1:T(8,128)(2,1)}), bf16[8192,64]{0,1:T(8,128)(2,1)}) %all-gather.3.cloned.1.call-update) | async-done | bytes 1048592 | tf_op jit(solution)/shard_map/all_gather | solution.py:364
  149.0 7.9 %shard_map.81 = f32[64,4096]{1,0:T(8,128)} custom-call(s32[128]{0:T(128)} %bitcast.62, s32[128]{0:T(128)} %bitcast.67, f32[128]{0:T(128)} %bitcast.56, bf16[128,128,128]{2,1,0:T(8,128)(2,1)} %bitcast.47, bf16[64,8192]{1,0:T(8,128)(2,1)} %bitcast.54), custom_call_target="tpu_custom_call" | custom-call | flops 268435456 | bytes 6291456 | tf_op jit(solution)/shard_map/pallas_call | solution.py:71
  156.9 1.8 copy.13
  160.1 75.7 %shard_map.82 = f32[2048,128]{1,0:T(8,128)} custom-call(f32[2048,128]{1,0:T(8,128)} %reshape.47.x_ref), custom_call_target="tpu_custom_call" | custom-call | tf_op jit(solution)/shard_map/pallas_call | solution.py:307
  238.9 2.6 convolution_subtract_fusion
  242.5 11.1 %psum.15.g_ref = f32[64,64]{1,0:T(8,128)} all-reduce(f32[64,64]{1,0:T(8,128)S(1)} %fusion.30), channel_id=1, replica_groups=mesh['yh'=2,'x'=4,'z'=8,'yl'=2,'c'=2] {'yl','c'}, use_global_device_ids=true, to_apply=%region_5.0 | all-reduce | flops 4096 | bytes 32768 | tf_op jit(solution)/shard_map/psum | solution.py:370
  253.6 6.7 %shard_map.83 = f32[64,128]{1,0:T(8,128)} custom-call(f32[64,64]{1,0:T(8,128)} %psum.15.g_ref), custom_call_target="tpu_custom_call" | custom-call | tf_op jit(solution)/shard_map/pallas_call | solution.py:136
  260.3 1.8 fusion.14
  264.0 9.1 %shard_map.84 = f32[64,8192]{1,0:T(8,128)} custom-call(s32[128]{0:T(128)} %bitcast.63, s32[128]{0:T(128)} %bitcast.68, f32[128]{0:T(128)} %bitcast.57, bf16[128,128,128]{2,1,0:T(8,128)(2,1)} %bitcast.48, bf16[64,4096]{1,0:T(8,128)(2,1)} %fusion.operand_ref), custom_call_target="tpu_custom_call" | custom-call | flops 268435456 | bytes 6815744 | tf_op jit(solution)/shard_map/pallas_call | solution.py:71
  273.3 31.3 %reduce-scatter.5.cloned.1.call-done = f32[64,2048]{1,0:T(8,128)} async-done(((f32[64,8192]{1,0:T(8,128)}), f32[64,2048]{1,0:T(8,128)}) %reduce-scatter.5.cloned.1.call-update) | async-done | bytes 524304 | tf_op jit(solution)/shard_map/reduce_scatter | solution.py:373
  307.5 24.7 %shard_map.85.g_ref = f32[64,64]{1,0:T(8,128)} custom-call(f32[64,64]{1,0:T(8,128)} %fusion.31.x_ref), custom_call_target="tpu_custom_call" | custom-call | tf_op jit(solution)/shard_map/pallas_call | solution.py:218
  332.2 6.7 %shard_map.86 = f32[64,128]{1,0:T(8,128)} custom-call(f32[64,64]{1,0:T(8,128)} %shard_map.85.g_ref), custom_call_target="tpu_custom_call" | custom-call | tf_op jit(solution)/shard_map/pallas_call | solution.py:136
  338.9 2.3 multiply_convert_fusion.2
  342.0 20.5 %all-gather.5.cloned.1.call-done = bf16[8192,64]{0,1:T(8,128)(2,1)} async-done(((bf16[2048,64]{0,1:T(8,128)(2,1)}), bf16[8192,64]{0,1:T(8,128)(2,1)}) %all-gather.5.cloned.1.call-update) | async-done | bytes 1048592 | tf_op jit(solution)/shard_map/all_gather | solution.py:364
  362.5 8.0 %shard_map.87 = f32[64,4096]{1,0:T(8,128)} custom-call(s32[128]{0:T(128)} %bitcast.64, s32[128]{0:T(128)} %bitcast.69, f32[128]{0:T(128)} %bitcast.58, bf16[128,128,128]{2,1,0:T(8,128)(2,1)} %bitcast.49, bf16[64,8192]{1,0:T(8,128)(2,1)} %bitcast.53), custom_call_target="tpu_custom_call" | custom-call | flops 268435456 | bytes 6291456 | tf_op jit(solution)/shard_map/pallas_call | solution.py:71
  370.4 2.8 reshape.49
  373.2 2.9 copy.15
  376.1 2.6 reshape_reshape.3.x_ref
  378.7 45.3 %shard_map.88 = f32[32,128]{1,0:T(8,128)} custom-call(f32[2048,128]{1,0:T(8,128)} %reshape_reshape.3.x_ref), custom_call_target="tpu_custom_call" | custom-call | tf_op jit(solution)/shard_map/pallas_call | solution.py:307
  426.8 24.6 %shard_map.89.g_ref = f32[64,64]{1,0:T(8,128)} custom-call(f32[64,64]{1,0:T(8,128)} %fusion.32.x_ref), custom_call_target="tpu_custom_call" | custom-call | tf_op jit(solution)/shard_map/pallas_call | solution.py:218
  451.4 6.7 %shard_map.90 = f32[64,128]{1,0:T(8,128)} custom-call(f32[64,64]{1,0:T(8,128)} %shard_map.89.g_ref), custom_call_target="tpu_custom_call" | custom-call | tf_op jit(solution)/shard_map/pallas_call | solution.py:136
  (51 shorter events, 21.3 us)
Async XLA Ops:
  7.2 24.2 %copy-start = (f32[4096,64]{0,1:T(8,128)S(1)}, f32[4096,64]{0,1:T(8,128)}, u32[]{:S(2)}) copy-start(f32[4096,64]{0,1:T(8,128)} %param.9) | copy-start | bytes 3145732
  7.2 3.6 copy-start.6
  7.2 3.6 copy-start.8
  7.2 84.0 %reduce-scatter.3.cloned.1.call-start = ((), (), s32[]{:S(2)}) async-start(), calls=%async_computation.2 | async-start | bytes 2621440 | tf_op jit(solution)/shard_map/reduce_scatter | solution.py:356
  10.8 21.6 %copy-start.7 = (s32[1,1,128]{2,1,0:T(1,128)S(1)}, s32[1,1,128]{2,1,0:T(1,128)}, u32[]{:S(2)}) copy-start(s32[1,1,128]{2,1,0:T(1,128)} %param.7) | copy-start | bytes 1540
  62.6 0.7 copy-start.9
  62.6 86.3 %all-gather.3.cloned.1.call-start = ((), (), s32[]{:S(2)}) async-start(), calls=%async_computation.3 | async-start | bytes 1310720 | tf_op jit(solution)/shard_map/all_gather | solution.py:364
  127.6 177.1 %reduce-scatter.5.cloned.1.call-start = ((), (), s32[]{:S(2)}) async-start(), calls=%async_computation.4 | async-start | bytes 2621440 | tf_op jit(solution)/shard_map/reduce_scatter | solution.py:373
  237.3 1.6 copy-start.4
  262.1 1.0 copy-start.1
  273.0 31.6 %copy-start.2 = (f32[2048,64]{0,1:T(8,128)S(1)}, f32[2048,64]{0,1:T(8,128)}, u32[]{:S(2)}) copy-start(f32[2048,64]{0,1:T(8,128)} %get-tuple-element.10) | copy-start | bytes 1572868
  273.0 31.6 %copy-start.3 = (f32[64,128]{1,0:T(8,128)S(1)}, f32[64,128]{1,0:T(8,128)}, u32[]{:S(2)}) copy-start(f32[64,128]{1,0:T(8,128)} %shard_map.83) | copy-start | bytes 98308
  273.1 89.4 %all-gather.5.cloned.1.call-start = ((), (), s32[]{:S(2)}) async-start(), calls=%async_computation.5 | async-start | bytes 1310720 | tf_op jit(solution)/shard_map/all_gather | solution.py:364
  376.1 48.7 %copy-start.5 = (f32[64,128]{1,0:T(8,128)S(1)}, f32[64,128]{1,0:T(8,128)}, u32[]{:S(2)}) copy-start(f32[64,128]{1,0:T(8,128)} %shard_map.86) | copy-start | bytes 98308
Sparse Core Ops, SparseCore 0:
  62.7 28.4 reduce-scatter.2
  127.7 21.2 all-gather.2
  273.2 31.4 reduce-scatter.4
  341.3 21.1 all-gather.4

commit v9 on v8

--- a/solution.py
+++ b/solution.py
@@ -88,11 +88,11 @@
     )
 
 
-def backward_local(block_tiles, block_scale, row_index, col_index, operand, col_count):
+def backward_local(block_tiles, block_scale, row_index, col_index, operand_t, col_count):
     edge = block_tiles.shape[-1]
-    out_shape = (operand.shape[-1], col_count * edge)
+    out_shape = (operand_t.shape[0], col_count * edge)
     flipped = block_product(
-        backward_kernel, block_tiles, block_scale, row_index, col_index, operand.T, out_shape
+        backward_kernel, block_tiles, block_scale, row_index, col_index, operand_t, out_shape
     )
     return flipped.T
 
@@ -131,7 +131,7 @@
     o_ref[...] = jnp.where((cols < n) & (cols < rows), 0.0, m)
 
 
-def orthonormal(block, gram_total):
+def factor_of(gram_total):
     n = gram_total.shape[0]
     both = pl.pallas_call(
         factor_kernel,
@@ -139,7 +139,11 @@
         in_specs=[pl.BlockSpec(memory_space=pltpu.VMEM)],
         out_specs=pl.BlockSpec(memory_space=pltpu.VMEM),
     )(gram_total)
-    upper, inverse = both[:, :n], both[:, n:]
+    return both[:, :n], both[:, n:]
+
+
+def orthonormal(block, gram_total):
+    upper, inverse = factor_of(gram_total)
     basis = jnp.dot(block, inverse.T, precision=HIGH)
     return (basis, upper)
 
@@ -348,38 +352,48 @@
     row_part, col_part = degree_local(tiles_here, scale_here, rows_here, cols_here, col_count)
     col_total = group_sum(col_part, CLAIM_GROUPS, 0)
     col_scale = lax.rsqrt(col_total + 1.0)
-    row_total = lax.psum_scatter(row_part, FEAT, scatter_dimension=0, tiled=True)
+    row_total = lax.psum(row_part, FEAT)
+    row_scale_all = lax.rsqrt(row_total + 1.0)
+    own_rows = row_part.shape[0] // lax.axis_size(FEAT)
+    own_start = lax.axis_index(FEAT) * own_rows
+    row_scale = lax.dynamic_slice_in_dim(row_scale_all, own_start, own_rows, 0)
     start_total = lax.psum(gram_of(start_basis), FEAT)
     first_basis, _ = orthonormal(start_basis, start_total)
     first_operand = (col_scale[:, None] * first_basis).astype(jnp.bfloat16)
     first_partial = forward_local(tiles_here, scale_here, rows_here, cols_here, first_operand)
-    first_sums = lax.psum_scatter(first_partial, FEAT, scatter_dimension=1, tiled=True).T
-    row_scale = lax.rsqrt(row_total + 1.0)
-
-    def row_orthonormal(block, cid):
-        return orthonormal(block, group_sum(gram_of(block), ALL_GROUPS, cid))
-
-    def backward_partial(basis):
-        operand = (row_scale[:, None] * basis).astype(jnp.bfloat16)
-        gathered = lax.all_gather(operand, FEAT, axis=0, tiled=True)
-        return backward_local(tiles_here, scale_here, rows_here, cols_here, gathered, col_count)
-
-    u_first, b_first = row_orthonormal(row_scale[:, None] * first_sums, 1)
-    summed = claim_halving(backward_partial(u_first), True, 4).reshape(-1, u_first.shape[-1])
+
+    def row_step(partial_t, previous_t, coupling, cid):
+        sums_t = lax.psum_scatter(partial_t, FEAT, scatter_dimension=1, tiled=True)
+        all_t = lax.all_gather(sums_t, FEAT, axis=1, tiled=True)
+        block_t = row_scale[None, :] * sums_t
+        wide_t = row_scale_all[None, :] * all_t
+        if previous_t is not None:
+            own_previous = lax.dynamic_slice_in_dim(previous_t, own_start, own_rows, 1)
+            block_t = block_t - jnp.dot(coupling, own_previous, precision=HIGH)
+            wide_t = wide_t - jnp.dot(coupling, previous_t, precision=HIGH)
+        gram = jnp.dot(block_t, block_t.T, precision=HIGH)
+        upper, inverse = factor_of(group_sum(gram, ALL_GROUPS, cid))
+        return jnp.dot(inverse, wide_t, precision=HIGH), upper
+
+    def backward_partial(basis_t):
+        operand_t = (row_scale_all[None, :] * basis_t).astype(jnp.bfloat16)
+        return backward_local(tiles_here, scale_here, rows_here, cols_here, operand_t, col_count)
+
+    u_first, b_first = row_step(first_partial, None, None, 1)
+    summed = claim_halving(backward_partial(u_first), True, 4).reshape(-1, first_basis.shape[-1])
     update = col_scale[:, None] * summed - jnp.dot(first_basis, b_first.T, precision=HIGH)
     v_second, a_second = orthonormal(update, lax.psum(gram_of(update), FEAT))
     scaled = (col_scale[:, None] * v_second).astype(jnp.bfloat16)
     second_partial = forward_local(tiles_here, scale_here, rows_here, cols_here, scaled)
-    second_sums = lax.psum_scatter(second_partial, FEAT, scatter_dimension=1, tiled=True).T
-    p_second = row_scale[:, None] * second_sums - jnp.dot(u_first, a_second.T, precision=HIGH)
-    u_second, b_second = row_orthonormal(p_second, 2)
+    u_second, b_second = row_step(second_partial, u_first, a_second, 2)
     own_sums = claim_scatter(backward_partial(u_second))
     own_scale = lax.dynamic_slice_in_dim(col_scale, own_first, own_cols, 0)
     own_second = lax.dynamic_slice_in_dim(v_second, own_first, own_cols, 0)
     q_second = own_scale[:, None] * own_sums - jnp.dot(own_second, b_second.T, precision=HIGH)
     v_output, a_third = orthonormal(q_second, group_sum(gram_of(q_second), ALL_GROUPS, 3))
     bidiagonal = jnp.stack([b_first, a_second, b_second, a_third])
-    return (u_second, v_output, bidiagonal)
+    u_output = lax.dynamic_slice_in_dim(u_second, own_start, own_rows, 1).T
+    return (u_output, v_output, bidiagonal)
 
 
 def solution(mesh):

time: 470 us -> 444 us (0.945)
  waiting for transfers between devices: 99.7 us -> 65.6 us
  matrix products: 24 us -> 31.6 us
    all_gather x2, waiting for transfers between devices: 41.6 us -> 5.39 us  [row_step(): all_t = lax.all_gather(sums_t, FEAT, axis=1, tiled=True)]
    dot_general x1 -> x6, matrix products: 1.65 us -> 17.6 us  [the longest x2 8.78 us: row_step(): return (jnp.dot(inverse, wide_t, precision=HIGH), upper)]
    dot_general x5 -> x3, matrix products: 11.2 us -> 6.39 us  [orthonormal(): basis = jnp.dot(block, inverse.T, precision=HIGH)]
  transfers between devices with their start and end apart: 4 -> 4, of which waited for: 4 -> 4; matrix products, arithmetic and copies ran while one was open for 0% -> 1% of each run, Pallas kernels for 0% -> 14%
where the time goes in v9:
time: 444 us; the launch traced here: 441 us
  Pallas kernels  283 us (64%)
  waiting for transfers between devices  65.6 us (15%)
  matrix products  31.6 us (7%)
  blocking collectives  22.3 us (5%)
  local copies, waits for them, and re-layouts  19.1 us (4%)
  between operations  14 us (3%)
  other arithmetic  5.77 us (1%)
    pallas_call x2, Pallas kernels, claim_halving(): pl.pallas_call(functools.partial(halving_kernel, stages, gather), out_sha...  122 us
    pallas_call x4, Pallas kernels, group_sum(): pl.pallas_call(functools.partial(group_kernel, tuple(spec)), out_shape=ja...  93.1 us
    reduce_scatter x2, waiting for transfers between devices, row_step(): sums_t = lax.psum_scatter(partial_t, FEAT, scatter_dimension=1, tiled=True)  60.1 us
    pallas_call x4, Pallas kernels, block_product(): pl.pallas_call(kernel, grid_spec=grid_spec, out_shape=jax.ShapeDtypeStruc...  34.2 us
    pallas_call x5, Pallas kernels, factor_of(): pl.pallas_call(factor_kernel, out_shape=jax.ShapeDtypeStruct((n, 2 * n),...  33.4 us
    psum x1, blocking collectives, per_device(): start_total = lax.psum(gram_of(start_basis), FEAT)  11.3 us
    psum x1, blocking collectives, per_device(): v_second, a_second = orthonormal(update, lax.psum(gram_of(update), FEAT))  11.1 us
  transfers between devices with their start and end apart: 4, of which 4 were waited for; matrix products, arithmetic and copies ran while one was open for 1% of the time, Pallas kernels for 14%

profile of v9, /device:TPU:64, one launch (start us, length us, event | category | flops | bytes accessed | tf_op | source)
XLA Modules:
  0.0 441.4 jit_solution(4587907277447172208)
XLA Ops:
  7.2 3.5 convert_reduce_fusion.1
  12.6 19.1 %shard_map.76 = f32[32,128]{1,0:T(8,128)} custom-call(f32[32,128]{1,0:T(8,128)} %fusion.8.x_ref), custom_call_target="tpu_custom_call" | custom-call | tf_op jit(solution)/shard_map/pallas_call | solution.py:222
  32.6 11.3 %all-reduce = (f32[64,64]{1,0:T(8,128)}, f32[8192]{0:T(1024)S(1)}) all-reduce(f32[64,64]{1,0:T(8,128)S(1)} %fusion.31, f32[8192]{0:T(1024)S(1)} %convolution_bitcast_fusion), channel_id=1, replica_groups=mesh['yh'=2,'x'=4,'z'=8,'yl'=2,'c'=2] {'yl','c'}, use_global_device_ids=true, to_apply=%region_3.0 | all-reduce | flops 12288 | bytes 98304 | tf_op jit(solution)/shard_map/psum | solution.py:360
  43.9 6.7 %shard_map.77 = f32[64,128]{1,0:T(8,128)} custom-call(f32[64,64]{1,0:T(8,128)} %get-tuple-element.5.g_ref), custom_call_target="tpu_custom_call" | custom-call | tf_op jit(solution)/shard_map/pallas_call | solution.py:136
  50.6 2.9 multiply_convert_fusion.3
  53.5 9.1 %shard_map.78 = f32[64,8192]{1,0:T(8,128)} custom-call(s32[128]{0:T(128)} %bitcast.56, s32[128]{0:T(128)} %bitcast.61, f32[128]{0:T(128)} %bitcast.50, bf16[128,128,128]{2,1,0:T(8,128)(2,1)} %bitcast.43, bf16[64,4096]{1,0:T(8,128)(2,1)} %get-tuple-element.7.operand_ref), custom_call_target="tpu_custom_call" | custom-call | flops 268435456 | bytes 6815744 | tf_op jit(solution)/shard_map/pallas_call | solution.py:71
  62.7 28.6 %reduce-scatter.3.cloned.1.call-done = f32[64,2048]{1,0:T(8,128)} async-done(((f32[64,8192]{1,0:T(8,128)}), f32[64,2048]{1,0:T(8,128)}) %reduce-scatter.3.cloned.1.call-update) | async-done | bytes 524304 | tf_op jit(solution)/shard_map/reduce_scatter | solution.py:366
  91.5 2.4 fusion.5.x_ref
  94.0 24.9 %shard_map.79.g_ref = f32[64,64]{1,0:T(8,128)} custom-call(f32[64,64]{1,0:T(8,128)} %fusion.5.x_ref), custom_call_target="tpu_custom_call" | custom-call | tf_op jit(solution)/shard_map/pallas_call | solution.py:222
  118.9 6.7 %shard_map.80 = f32[64,128]{1,0:T(8,128)} custom-call(f32[64,64]{1,0:T(8,128)} %shard_map.79.g_ref), custom_call_target="tpu_custom_call" | custom-call | tf_op jit(solution)/shard_map/pallas_call | solution.py:136
  125.6 3.0 all-gather.3.cloned.1.call-done
  128.5 5.2 %multiply_convert_fusion.1 = (bf16[64,8192]{1,0:T(8,128)(2,1)}, f32[64,8192]{1,0:T(8,128)}) fusion(f32[8192]{0:T(1024)S(1)} %add_rsqrt_fusion, f32[64,8192]{1,0:T(8,128)} %all-gather.3.cloned.1.call-done, f32[64,128]{1,0:T(8,128)} %shard_map.80), kind=kOutput, calls=%fused_computation.6 | convolution fusion | flops 404226048 | bytes 5341184 | tf_op jit(solution)/shard_map/dot_general | solution.py:376
  133.7 7.9 %shard_map.81 = f32[64,4096]{1,0:T(8,128)} custom-call(s32[128]{0:T(128)} %bitcast.57, s32[128]{0:T(128)} %bitcast.62, f32[128]{0:T(128)} %bitcast.51, bf16[128,128,128]{2,1,0:T(8,128)(2,1)} %bitcast.44, bf16[64,8192]{1,0:T(8,128)(2,1)} %get-tuple-element.9.operand_ref), custom_call_target="tpu_custom_call" | custom-call | flops 268435456 | bytes 6291456 | tf_op jit(solution)/shard_map/pallas_call | solution.py:71
  144.8 76.2 %shard_map.82 = f32[2048,128]{1,0:T(8,128)} custom-call(f32[2048,128]{1,0:T(8,128)} %reshape.48.x_ref), custom_call_target="tpu_custom_call" | custom-call | tf_op jit(solution)/shard_map/pallas_call | solution.py:311
  224.1 2.6 convolution_subtract_fusion.1
  227.7 11.1 %psum.23.g_ref = f32[64,64]{1,0:T(8,128)} all-reduce(f32[64,64]{1,0:T(8,128)S(1)} %fusion.32), channel_id=1, replica_groups=mesh['yh'=2,'x'=4,'z'=8,'yl'=2,'c'=2] {'yl','c'}, use_global_device_ids=true, to_apply=%region_5.0 | all-reduce | flops 4096 | bytes 32768 | tf_op jit(solution)/shard_map/psum | solution.py:385
  238.8 6.7 %shard_map.83 = f32[64,128]{1,0:T(8,128)} custom-call(f32[64,64]{1,0:T(8,128)} %psum.23.g_ref), custom_call_target="tpu_custom_call" | custom-call | tf_op jit(solution)/shard_map/pallas_call | solution.py:136
  249.2 9.0 %shard_map.84 = f32[64,8192]{1,0:T(8,128)} custom-call(s32[128]{0:T(128)} %bitcast.58, s32[128]{0:T(128)} %bitcast.63, f32[128]{0:T(128)} %bitcast.52, bf16[128,128,128]{2,1,0:T(8,128)(2,1)} %bitcast.45, bf16[64,4096]{1,0:T(8,128)(2,1)} %fusion.3.operand_ref), custom_call_target="tpu_custom_call" | custom-call | flops 268435456 | bytes 6815744 | tf_op jit(solution)/shard_map/pallas_call | solution.py:71
  258.3 31.5 %reduce-scatter.5.cloned.1.call-done = f32[64,2048]{1,0:T(8,128)} async-done(((f32[64,8192]{1,0:T(8,128)}), f32[64,2048]{1,0:T(8,128)}) %reduce-scatter.5.cloned.1.call-update) | async-done | bytes 524304 | tf_op jit(solution)/shard_map/reduce_scatter | solution.py:366
  292.8 24.9 %shard_map.85.g_ref = f32[64,64]{1,0:T(8,128)} custom-call(f32[64,64]{1,0:T(8,128)} %fusion.33.x_ref), custom_call_target="tpu_custom_call" | custom-call | tf_op jit(solution)/shard_map/pallas_call | solution.py:222
  317.7 6.7 %shard_map.86 = f32[64,128]{1,0:T(8,128)} custom-call(f32[64,64]{1,0:T(8,128)} %shard_map.85.g_ref), custom_call_target="tpu_custom_call" | custom-call | tf_op jit(solution)/shard_map/pallas_call | solution.py:136
  324.4 2.4 all-gather.5.cloned.1.call-done
  326.8 3.6 convolution_subtract_fusion
  330.5 3.6 multiply_convert_fusion
  334.1 8.2 %shard_map.87 = f32[64,4096]{1,0:T(8,128)} custom-call(s32[128]{0:T(128)} %bitcast.59, s32[128]{0:T(128)} %bitcast.64, f32[128]{0:T(128)} %bitcast.53, bf16[128,128,128]{2,1,0:T(8,128)(2,1)} %bitcast.46, bf16[64,8192]{1,0:T(8,128)(2,1)} %get-tuple-element.11.operand_ref), custom_call_target="tpu_custom_call" | custom-call | flops 268435456 | bytes 6291456 | tf_op jit(solution)/shard_map/pallas_call | solution.py:71
  342.3 2.8 reshape.50
  345.1 2.9 copy.12
  347.9 2.6 reshape_reshape.3.x_ref
  350.6 45.8 %shard_map.88 = f32[32,128]{1,0:T(8,128)} custom-call(f32[2048,128]{1,0:T(8,128)} %reshape_reshape.3.x_ref), custom_call_target="tpu_custom_call" | custom-call | tf_op jit(solution)/shard_map/pallas_call | solution.py:311
  399.0 24.2 %shard_map.89.g_ref = f32[64,64]{1,0:T(8,128)} custom-call(f32[64,64]{1,0:T(8,128)} %fusion.34.x_ref), custom_call_target="tpu_custom_call" | custom-call | tf_op jit(solution)/shard_map/pallas_call | solution.py:222
  423.3 6.7 %shard_map.90 = f32[64,128]{1,0:T(8,128)} custom-call(f32[64,64]{1,0:T(8,128)} %shard_map.89.g_ref), custom_call_target="tpu_custom_call" | custom-call | tf_op jit(solution)/shard_map/pallas_call | solution.py:136
  432.4 1.9 dynamic-slice_bitcast_fusion
  (50 shorter events, 22.8 us)
Async XLA Ops:
  7.2 3.6 copy-start
  7.2 84.1 %reduce-scatter.3.cloned.1.call-start = ((), (), s32[]{:S(2)}) async-start(), calls=%async_computation.2 | async-start | bytes 2621440 | tf_op jit(solution)/shard_map/reduce_scatter | solution.py:366
  10.7 1.0 copy-start.6
  10.8 1.0 copy-start.8
  10.8 21.6 %copy-start.7 = (s32[1,1,128]{2,1,0:T(1,128)S(1)}, s32[1,1,128]{2,1,0:T(1,128)}, u32[]{:S(2)}) copy-start(s32[1,1,128]{2,1,0:T(1,128)} %param.7) | copy-start | bytes 1540
  62.6 65.9 %all-gather.3.cloned.1.call-start = ((), (), s32[]{:S(2)}) async-start(), calls=%async_computation.3 | async-start | bytes 2621440 | tf_op jit(solution)/shard_map/all_gather | solution.py:367
  91.3 198.6 %reduce-scatter.5.cloned.1.call-start = ((), (), s32[]{:S(2)}) async-start(), calls=%async_computation.4 | async-start | bytes 2621440 | tf_op jit(solution)/shard_map/reduce_scatter | solution.py:366
  222.6 1.6 copy-start.4
  247.3 1.0 copy-start.2
  258.2 31.7 %copy-start.3 = (f32[64,128]{1,0:T(8,128)S(1)}, f32[64,128]{1,0:T(8,128)}, u32[]{:S(2)}) copy-start(f32[64,128]{1,0:T(8,128)} %shard_map.83) | copy-start | bytes 98308
  258.2 31.8 %copy-start.1 = (f32[64,8192]{1,0:T(8,128)S(1)}, f32[64,8192]{1,0:T(8,128)}, u32[]{:S(2)}) copy-start(f32[64,8192]{1,0:T(8,128)} %get-tuple-element.10) | copy-start | bytes 6291460
  258.2 68.6 %all-gather.5.cloned.1.call-start = ((), (), s32[]{:S(2)}) async-start(), calls=%async_computation.5 | async-start | bytes 2621440 | tf_op jit(solution)/shard_map/all_gather | solution.py:367
  324.4 6.1 %copy-start.5 = (f32[64,128]{1,0:T(8,128)S(1)}, f32[64,128]{1,0:T(8,128)}, u32[]{:S(2)}) copy-start(f32[64,128]{1,0:T(8,128)} %shard_map.86) | copy-start | bytes 98308
Sparse Core Ops, SparseCore 0:
  62.7 28.4 reduce-scatter.2
  93.2 35.2 all-gather.2
  258.4 31.4 reduce-scatter.4
  291.5 35.2 all-gather.4

commit v10 on v9

--- a/solution.py
+++ b/solution.py
@@ -148,8 +148,7 @@
     return (basis, upper)
 
 
-def group_kernel(groups, x_ref, o_ref, slots, send_sem, recv_sem):
-    coords = [lax.axis_index(name) for name in FINE]
+def group_plan(groups, coords):
     plans = []
     for axes, sizes in groups:
         count = 1
@@ -168,70 +167,100 @@
                 rest = rest // size
             targets.append((tuple(place), (me + count - k) % count))
         plans.append((count, me, targets))
+    return plans
+
+
+def group_kernel(all_groups, *refs):
+    n = len(all_groups)
+    x_refs, o_refs, scratch = refs[:n], refs[n : 2 * n], refs[2 * n :]
+    coords = [lax.axis_index(name) for name in FINE]
+    plans = [group_plan(groups, coords) for groups in all_groups]
     barrier = pltpu.get_barrier_semaphore()
     total = 0
-    for count, me, targets in plans:
-        for place, _ in targets:
-            pl.semaphore_signal(barrier, inc=1, device_id=place, device_id_type=pl.DeviceIdType.MESH)
-        total += len(targets)
+    for plan in plans:
+        for count, me, targets in plan:
+            for place, _ in targets:
+                pl.semaphore_signal(barrier, inc=1, device_id=place, device_id_type=pl.DeviceIdType.MESH)
+            total += len(targets)
     pl.semaphore_wait(barrier, total)
-    o_ref[...] = x_ref[...]
-    for g, (count, me, targets) in enumerate(plans):
-        slots[g, me] = o_ref[...]
-        copies = []
-        for k, (place, _) in enumerate(targets):
-            copy = pltpu.make_async_remote_copy(
-                src_ref=o_ref,
-                dst_ref=slots.at[g, me],
-                send_sem=send_sem.at[g, k],
-                recv_sem=recv_sem.at[g, me],
-                device_id=place,
-                device_id_type=pl.DeviceIdType.MESH,
-            )
-            copy.start()
-            copies.append(copy)
-        for copy in copies:
-            copy.wait_send()
-        for place, sender in targets:
-            pltpu.make_async_remote_copy(
-                src_ref=o_ref,
-                dst_ref=slots.at[g, sender],
-                send_sem=send_sem.at[g, 0],
-                recv_sem=recv_sem.at[g, sender],
-                device_id=place,
-                device_id_type=pl.DeviceIdType.MESH,
-            ).wait_recv()
-        acc = slots[g, 0]
-        for j in range(1, count):
-            acc = acc + slots[g, j]
-        o_ref[...] = acc
-
-
-def group_sum(value, groups, cid):
-    spec = []
-    widest = 1
-    for names in groups:
-        sizes = tuple(lax.axis_size(name) for name in names)
-        count = 1
-        for size in sizes:
-            count *= size
-        widest = max(widest, count)
-        spec.append((tuple(FINE.index(name) for name in names), sizes))
-    shape = value.shape
-    flat = value.reshape(-1, 128) if value.ndim == 1 else value
-    out = pl.pallas_call(
-        functools.partial(group_kernel, tuple(spec)),
-        out_shape=jax.ShapeDtypeStruct(flat.shape, flat.dtype),
-        in_specs=[pl.BlockSpec(memory_space=pltpu.VMEM)],
-        out_specs=pl.BlockSpec(memory_space=pltpu.VMEM),
-        scratch_shapes=[
+    for a in range(n):
+        o_refs[a][...] = x_refs[a][...]
+    for g in range(max(len(plan) for plan in plans)):
+        started = []
+        for a in range(n):
+            if g >= len(plans[a]):
+                continue
+            o_ref = o_refs[a]
+            slots, send_sem, recv_sem = scratch[3 * a : 3 * a + 3]
+            count, me, targets = plans[a][g]
+            slots[g, me] = o_ref[...]
+            copies = []
+            for k, (place, _) in enumerate(targets):
+                copy = pltpu.make_async_remote_copy(
+                    src_ref=o_ref,
+                    dst_ref=slots.at[g, me],
+                    send_sem=send_sem.at[g, k],
+                    recv_sem=recv_sem.at[g, me],
+                    device_id=place,
+                    device_id_type=pl.DeviceIdType.MESH,
+                )
+                copy.start()
+                copies.append(copy)
+            started.append((a, copies))
+        for a, copies in started:
+            o_ref = o_refs[a]
+            slots, send_sem, recv_sem = scratch[3 * a : 3 * a + 3]
+            count, me, targets = plans[a][g]
+            for copy in copies:
+                copy.wait_send()
+            for place, sender in targets:
+                pltpu.make_async_remote_copy(
+                    src_ref=o_ref,
+                    dst_ref=slots.at[g, sender],
+                    send_sem=send_sem.at[g, 0],
+                    recv_sem=recv_sem.at[g, sender],
+                    device_id=place,
+                    device_id_type=pl.DeviceIdType.MESH,
+                ).wait_recv()
+            acc = slots[g, 0]
+            for j in range(1, count):
+                acc = acc + slots[g, j]
+            o_ref[...] = acc
+
+
+def group_sums(values, all_groups, cid):
+    specs, flats, scratch = [], [], []
+    for value, groups in zip(values, all_groups):
+        spec = []
+        widest = 1
+        for names in groups:
+            sizes = tuple(lax.axis_size(name) for name in names)
+            count = 1
+            for size in sizes:
+                count *= size
+            widest = max(widest, count)
+            spec.append((tuple(FINE.index(name) for name in names), sizes))
+        flat = value.reshape(-1, 128) if value.ndim == 1 else value
+        specs.append(tuple(spec))
+        flats.append(flat)
+        scratch += [
             pltpu.VMEM((len(spec), widest) + flat.shape, flat.dtype),
             pltpu.SemaphoreType.DMA((len(spec), widest)),
             pltpu.SemaphoreType.DMA((len(spec), widest)),
-        ],
+        ]
+    outs = pl.pallas_call(
+        functools.partial(group_kernel, tuple(specs)),
+        out_shape=[jax.ShapeDtypeStruct(flat.shape, flat.dtype) for flat in flats],
+        in_specs=[pl.BlockSpec(memory_space=pltpu.VMEM)] * len(flats),
+        out_specs=[pl.BlockSpec(memory_space=pltpu.VMEM)] * len(flats),
+        scratch_shapes=scratch,
         compiler_params=pltpu.CompilerParams(collective_id=cid, has_side_effects=True),
-    )(flat)
-    return out.reshape(shape)
+    )(*flats)
+    return [out.reshape(value.shape) for out, value in zip(outs, values)]
+
+
+def group_sum(value, groups, cid):
+    return group_sums([value], [groups], cid)[0]
 
 
 ALL_GROUPS = (FEAT, ("z",), ("yh", "x"))
@@ -350,14 +379,14 @@
     own_cols = start_basis.shape[0] // claim_count
     own_first = lax.axis_index(CLAIM) * own_cols
     row_part, col_part = degree_local(tiles_here, scale_here, rows_here, cols_here, col_count)
-    col_total = group_sum(col_part, CLAIM_GROUPS, 0)
+    col_total, row_total, start_total = group_sums(
+        [col_part, row_part, gram_of(start_basis)], [CLAIM_GROUPS, (FEAT,), (FEAT,)], 0
+    )
     col_scale = lax.rsqrt(col_total + 1.0)
-    row_total = lax.psum(row_part, FEAT)
     row_scale_all = lax.rsqrt(row_total + 1.0)
     own_rows = row_part.shape[0] // lax.axis_size(FEAT)
     own_start = lax.axis_index(FEAT) * own_rows
     row_scale = lax.dynamic_slice_in_dim(row_scale_all, own_start, own_rows, 0)
-    start_total = lax.psum(gram_of(start_basis), FEAT)
     first_basis, _ = orthonormal(start_basis, start_total)
     first_operand = (col_scale[:, None] * first_basis).astype(jnp.bfloat16)
     first_partial = forward_local(tiles_here, scale_here, rows_here, cols_here, first_operand)

time: 444 us -> 434 us (0.977)
  blocking collectives: 22.3 us -> 11.1 us
    psum x1 -> x0, blocking collectives: 11.3 us -> none  [per_device(): start_total = lax.psum(gram_of(start_basis), FEAT)]
  transfers between devices with their start and end apart: 4 -> 4, of which waited for: 4 -> 4; matrix products, arithmetic and copies ran while one was open for 1% -> 1% of each run, Pallas kernels for 14% -> 15%
where the time goes in v10:
time: 434 us; the launch traced here: 431 us
  Pallas kernels  284 us (65%)
  waiting for transfers between devices  64.6 us (15%)
  matrix products  32.8 us (8%)
  local copies, waits for them, and re-layouts  19.1 us (4%)
  between operations  14 us (3%)
  blocking collectives  11.1 us (3%)
  other arithmetic  5.77 us (1%)
    pallas_call x2, Pallas kernels, claim_halving(): pl.pallas_call(functools.partial(halving_kernel, stages, gather), out_sha...  122 us
    pallas_call x4, Pallas kernels, group_sums(): pl.pallas_call(functools.partial(group_kernel, tuple(specs)), out_shape=[...  94.1 us
    reduce_scatter x2, waiting for transfers between devices, row_step(): sums_t = lax.psum_scatter(partial_t, FEAT, scatter_dimension=1, tiled=True)  59.3 us
    pallas_call x4, Pallas kernels, block_product(): pl.pallas_call(kernel, grid_spec=grid_spec, out_shape=jax.ShapeDtypeStruc...  34.1 us
    pallas_call x5, Pallas kernels, factor_of(): pl.pallas_call(factor_kernel, out_shape=jax.ShapeDtypeStruct((n, 2 * n),...  33.4 us
    psum x1, blocking collectives, per_device(): v_second, a_second = orthonormal(update, lax.psum(gram_of(update), FEAT))  11.1 us
    dot_general x2, matrix products, row_step(): return (jnp.dot(inverse, wide_t, precision=HIGH), upper)  8.79 us
  transfers between devices with their start and end apart: 4, of which 4 were waited for; matrix products, arithmetic and copies ran while one was open for 1% of the time, Pallas kernels for 15%

profile of v10, /device:TPU:64, one launch (start us, length us, event | category | flops | bytes accessed | tf_op | source)
XLA Modules:
  0.0 431.3 jit_solution(4407673593647278857)
XLA Ops:
  7.2 3.5 convert_reduce_fusion
  14.1 20.0 %shard_map.76 = (f32[32,128]{1,0:T(8,128)}, f32[64,128]{1,0:T(8,128)}, f32[64,64]{1,0:T(8,128)}) custom-call(f32[32,128]{1,0:T(8,128)} %fusion.10.refs_0_, f32[64,128]{1,0:T(8,128)} %fusion.8.refs_1_, f32[64,64]{1,0:T(8,128)} %fusion.32.refs_2_), custom_call_target="tpu_custom_call" | custom-call | tf_op jit(solution)/shard_map/pallas_call | solution.py:251
  34.8 6.7 %shard_map.77 = f32[64,128]{1,0:T(8,128)} custom-call(f32[64,64]{1,0:T(8,128)} %get-tuple-element.8.g_ref), custom_call_target="tpu_custom_call" | custom-call | tf_op jit(solution)/shard_map/pallas_call | solution.py:136
  41.5 2.9 multiply_convert_fusion.3
  44.4 9.0 %shard_map.78 = f32[64,8192]{1,0:T(8,128)} custom-call(s32[128]{0:T(128)} %bitcast.56, s32[128]{0:T(128)} %bitcast.61, f32[128]{0:T(128)} %bitcast.50, bf16[128,128,128]{2,1,0:T(8,128)(2,1)} %bitcast.43, bf16[64,4096]{1,0:T(8,128)(2,1)} %get-tuple-element.11.operand_ref), custom_call_target="tpu_custom_call" | custom-call | flops 268435456 | bytes 6815744 | tf_op jit(solution)/shard_map/pallas_call | solution.py:71
  53.5 27.6 %reduce-scatter.3.cloned.1.call-done = f32[64,2048]{1,0:T(8,128)} async-done(((f32[64,8192]{1,0:T(8,128)}), f32[64,2048]{1,0:T(8,128)}) %reduce-scatter.3.cloned.1.call-update) | async-done | bytes 524304 | tf_op jit(solution)/shard_map/reduce_scatter | solution.py:395
  81.4 2.4 fusion.5.refs_0_
  83.9 25.0 %shard_map.79.g_ref = f32[64,64]{1,0:T(8,128)} custom-call(f32[64,64]{1,0:T(8,128)} %fusion.5.refs_0_), custom_call_target="tpu_custom_call" | custom-call | tf_op jit(solution)/shard_map/pallas_call | solution.py:251
  108.8 6.7 %shard_map.80 = f32[64,128]{1,0:T(8,128)} custom-call(f32[64,64]{1,0:T(8,128)} %shard_map.79.g_ref), custom_call_target="tpu_custom_call" | custom-call | tf_op jit(solution)/shard_map/pallas_call | solution.py:136
  115.5 2.9 all-gather.3.cloned.1.call-done
  118.4 5.2 %multiply_convert_fusion.1 = (bf16[64,8192]{1,0:T(8,128)(2,1)}, f32[64,8192]{1,0:T(8,128)}) fusion(f32[8192]{0:T(1024)S(1)} %rsqrt_bitcast_fusion, f32[64,8192]{1,0:T(8,128)} %all-gather.3.cloned.1.call-done, f32[64,128]{1,0:T(8,128)} %shard_map.80), kind=kOutput, calls=%fused_computation.6 | convolution fusion | flops 404226048 | bytes 5341184 | tf_op jit(solution)/shard_map/dot_general | solution.py:405
  123.6 7.9 %shard_map.81 = f32[64,4096]{1,0:T(8,128)} custom-call(s32[128]{0:T(128)} %bitcast.57, s32[128]{0:T(128)} %bitcast.62, f32[128]{0:T(128)} %bitcast.51, bf16[128,128,128]{2,1,0:T(8,128)(2,1)} %bitcast.44, bf16[64,8192]{1,0:T(8,128)(2,1)} %get-tuple-element.13.operand_ref), custom_call_target="tpu_custom_call" | custom-call | flops 268435456 | bytes 6291456 | tf_op jit(solution)/shard_map/pallas_call | solution.py:71
  131.5 1.8 copy.10
  134.7 76.1 %shard_map.82 = f32[2048,128]{1,0:T(8,128)} custom-call(f32[2048,128]{1,0:T(8,128)} %reshape.50.x_ref), custom_call_target="tpu_custom_call" | custom-call | tf_op jit(solution)/shard_map/pallas_call | solution.py:340
  213.9 2.6 convolution_subtract_fusion.1
  217.5 11.1 %psum.7.g_ref = f32[64,64]{1,0:T(8,128)} all-reduce(f32[64,64]{1,0:T(8,128)S(1)} %fusion.33), channel_id=1, replica_groups=mesh['yh'=2,'x'=4,'z'=8,'yl'=2,'c'=2] {'yl','c'}, use_global_device_ids=true, to_apply=%region_3.0 | all-reduce | flops 4096 | bytes 32768 | tf_op jit(solution)/shard_map/psum | solution.py:414
  228.6 6.7 %shard_map.83 = f32[64,128]{1,0:T(8,128)} custom-call(f32[64,64]{1,0:T(8,128)} %psum.7.g_ref), custom_call_target="tpu_custom_call" | custom-call | tf_op jit(solution)/shard_map/pallas_call | solution.py:136
  238.9 9.0 %shard_map.84 = f32[64,8192]{1,0:T(8,128)} custom-call(s32[128]{0:T(128)} %bitcast.58, s32[128]{0:T(128)} %bitcast.63, f32[128]{0:T(128)} %bitcast.52, bf16[128,128,128]{2,1,0:T(8,128)(2,1)} %bitcast.45, bf16[64,4096]{1,0:T(8,128)(2,1)} %fusion.3.operand_ref), custom_call_target="tpu_custom_call" | custom-call | flops 268435456 | bytes 6815744 | tf_op jit(solution)/shard_map/pallas_call | solution.py:71
  248.0 31.7 %reduce-scatter.5.cloned.1.call-done = f32[64,2048]{1,0:T(8,128)} async-done(((f32[64,8192]{1,0:T(8,128)}), f32[64,2048]{1,0:T(8,128)}) %reduce-scatter.5.cloned.1.call-update) | async-done | bytes 524304 | tf_op jit(solution)/shard_map/reduce_scatter | solution.py:395
  282.6 24.9 %shard_map.85.g_ref = f32[64,64]{1,0:T(8,128)} custom-call(f32[64,64]{1,0:T(8,128)} %fusion.34.refs_0_), custom_call_target="tpu_custom_call" | custom-call | tf_op jit(solution)/shard_map/pallas_call | solution.py:251
  307.6 6.7 %shard_map.86 = f32[64,128]{1,0:T(8,128)} custom-call(f32[64,64]{1,0:T(8,128)} %shard_map.85.g_ref), custom_call_target="tpu_custom_call" | custom-call | tf_op jit(solution)/shard_map/pallas_call | solution.py:136
  314.3 2.4 all-gather.5.cloned.1.call-done
  316.7 3.6 convolution_subtract_fusion
  320.3 3.6 multiply_convert_fusion
  323.9 8.2 %shard_map.87 = f32[64,4096]{1,0:T(8,128)} custom-call(s32[128]{0:T(128)} %bitcast.59, s32[128]{0:T(128)} %bitcast.64, f32[128]{0:T(128)} %bitcast.53, bf16[128,128,128]{2,1,0:T(8,128)(2,1)} %bitcast.46, bf16[64,8192]{1,0:T(8,128)(2,1)} %get-tuple-element.15.operand_ref), custom_call_target="tpu_custom_call" | custom-call | flops 268435456 | bytes 6291456 | tf_op jit(solution)/shard_map/pallas_call | solution.py:71
  332.1 2.8 reshape.52
  334.9 2.9 copy.12
  337.8 2.6 reshape_reshape.3.x_ref
  340.4 45.8 %shard_map.88 = f32[32,128]{1,0:T(8,128)} custom-call(f32[2048,128]{1,0:T(8,128)} %reshape_reshape.3.x_ref), custom_call_target="tpu_custom_call" | custom-call | tf_op jit(solution)/shard_map/pallas_call | solution.py:340
  388.9 24.2 %shard_map.89.g_ref = f32[64,64]{1,0:T(8,128)} custom-call(f32[64,64]{1,0:T(8,128)} %fusion.35.refs_0_), custom_call_target="tpu_custom_call" | custom-call | tf_op jit(solution)/shard_map/pallas_call | solution.py:251
  413.2 6.7 %shard_map.90 = f32[64,128]{1,0:T(8,128)} custom-call(f32[64,64]{1,0:T(8,128)} %shard_map.89.g_ref), custom_call_target="tpu_custom_call" | custom-call | tf_op jit(solution)/shard_map/pallas_call | solution.py:136
  422.2 1.9 dynamic-slice_bitcast_fusion
  (51 shorter events, 22.2 us)
Async XLA Ops:
  7.2 3.6 copy-start
  7.2 73.9 %reduce-scatter.3.cloned.1.call-start = ((), (), s32[]{:S(2)}) async-start(), calls=%async_computation.2 | async-start | bytes 2621440 | tf_op jit(solution)/shard_map/reduce_scatter | solution.py:395
  10.7 1.6 copy-start.7
  10.8 1.6 copy-start.8
  10.8 2.5 copy-start.9
  53.4 27.9 %copy-start.6 = (f32[64,128]{1,0:T(8,128)S(1)}, f32[64,128]{1,0:T(8,128)}, u32[]{:S(2)}) copy-start(f32[64,128]{1,0:T(8,128)} %get-tuple-element.6) | copy-start | bytes 98308
  53.5 64.9 %all-gather.3.cloned.1.call-start = ((), (), s32[]{:S(2)}) async-start(), calls=%async_computation.3 | async-start | bytes 2621440 | tf_op jit(solution)/shard_map/all_gather | solution.py:396
  81.1 198.6 %reduce-scatter.5.cloned.1.call-start = ((), (), s32[]{:S(2)}) async-start(), calls=%async_computation.4 | async-start | bytes 2621440 | tf_op jit(solution)/shard_map/reduce_scatter | solution.py:395
  212.3 1.6 copy-start.4
  237.1 1.0 copy-start.2
  247.9 31.9 %copy-start.3 = (f32[64,128]{1,0:T(8,128)S(1)}, f32[64,128]{1,0:T(8,128)}, u32[]{:S(2)}) copy-start(f32[64,128]{1,0:T(8,128)} %shard_map.83) | copy-start | bytes 98308
  247.9 31.9 %copy-start.1 = (f32[64,8192]{1,0:T(8,128)S(1)}, f32[64,8192]{1,0:T(8,128)}, u32[]{:S(2)}) copy-start(f32[64,8192]{1,0:T(8,128)} %get-tuple-element.14) | copy-start | bytes 6291460
  248.0 68.7 %all-gather.5.cloned.1.call-start = ((), (), s32[]{:S(2)}) async-start(), calls=%async_computation.5 | async-start | bytes 2621440 | tf_op jit(solution)/shard_map/all_gather | solution.py:396
  314.3 6.0 %copy-start.5 = (f32[64,128]{1,0:T(8,128)S(1)}, f32[64,128]{1,0:T(8,128)}, u32[]{:S(2)}) copy-start(f32[64,128]{1,0:T(8,128)} %shard_map.86) | copy-start | bytes 98308
Sparse Core Ops, SparseCore 0:
  53.6 27.4 reduce-scatter.2
  83.1 35.2 all-gather.2
  248.1 31.5 reduce-scatter.4
  281.4 35.2 all-gather.4

commit v11 on v10

--- a/solution.py
+++ b/solution.py
@@ -116,8 +116,12 @@
 
 
 def factor_kernel(g_ref, o_ref):
-    n = g_ref.shape[0]
-    o_ref[:, :n] = g_ref[...]
+    eliminate(g_ref[...], o_ref)
+
+
+def eliminate(gram, o_ref):
+    n = gram.shape[0]
+    o_ref[:, :n] = gram
     rows = lax.broadcasted_iota(jnp.int32, (n, 2 * n), 0)
     cols = lax.broadcasted_iota(jnp.int32, (n, 2 * n), 1)
     o_ref[:, n:] = jnp.where(rows[:, n:] == cols[:, n:] - n, 1.0, 0.0).astype(o_ref.dtype)
@@ -170,9 +174,10 @@
     return plans
 
 
-def group_kernel(all_groups, *refs):
+def group_kernel(all_groups, factored, *refs):
     n = len(all_groups)
-    x_refs, o_refs, scratch = refs[:n], refs[n : 2 * n], refs[2 * n :]
+    x_refs, o_refs = refs[:n], refs[n : 2 * n]
+    f_refs, scratch = refs[2 * n : 2 * n + len(factored)], refs[2 * n + len(factored) :]
     coords = [lax.axis_index(name) for name in FINE]
     plans = [group_plan(groups, coords) for groups in all_groups]
     barrier = pltpu.get_barrier_semaphore()
@@ -226,9 +231,11 @@
             for j in range(1, count):
                 acc = acc + slots[g, j]
             o_ref[...] = acc
-
-
-def group_sums(values, all_groups, cid):
+    for a, f_ref in zip(factored, f_refs):
+        eliminate(o_refs[a][...], f_ref)
+
+
+def group_sums(values, all_groups, cid, factored=()):
     specs, flats, scratch = [], [], []
     for value, groups in zip(values, all_groups):
         spec = []
@@ -248,19 +255,30 @@
             pltpu.SemaphoreType.DMA((len(spec), widest)),
             pltpu.SemaphoreType.DMA((len(spec), widest)),
         ]
+    out_shape = [jax.ShapeDtypeStruct(flat.shape, flat.dtype) for flat in flats]
+    out_shape += [jax.ShapeDtypeStruct((flats[a].shape[0], 2 * flats[a].shape[0]), jnp.float32) for a in factored]
     outs = pl.pallas_call(
-        functools.partial(group_kernel, tuple(specs)),
-        out_shape=[jax.ShapeDtypeStruct(flat.shape, flat.dtype) for flat in flats],
+        functools.partial(group_kernel, tuple(specs), tuple(factored)),
+        out_shape=out_shape,
         in_specs=[pl.BlockSpec(memory_space=pltpu.VMEM)] * len(flats),
-        out_specs=[pl.BlockSpec(memory_space=pltpu.VMEM)] * len(flats),
+        out_specs=[pl.BlockSpec(memory_space=pltpu.VMEM)] * len(out_shape),
         scratch_shapes=scratch,
         compiler_params=pltpu.CompilerParams(collective_id=cid, has_side_effects=True),
     )(*flats)
-    return [out.reshape(value.shape) for out, value in zip(outs, values)]
+    sums = [out.reshape(value.shape) for out, value in zip(outs, values)]
+    factors = []
+    for both in outs[len(flats) :]:
+        half = both.shape[0]
+        factors.append((both[:, :half], both[:, half:]))
+    return sums, factors
 
 
 def group_sum(value, groups, cid):
-    return group_sums([value], [groups], cid)[0]
+    return group_sums([value], [groups], cid)[0][0]
+
+
+def group_factor(value, groups, cid):
+    return group_sums([value], [groups], cid, factored=(0,))[1][0]
 
 
 ALL_GROUPS = (FEAT, ("z",), ("yh", "x"))
@@ -379,15 +397,15 @@
     own_cols = start_basis.shape[0] // claim_count
     own_first = lax.axis_index(CLAIM) * own_cols
     row_part, col_part = degree_local(tiles_here, scale_here, rows_here, cols_here, col_count)
-    col_total, row_total, start_total = group_sums(
-        [col_part, row_part, gram_of(start_basis)], [CLAIM_GROUPS, (FEAT,), (FEAT,)], 0
+    (col_total, row_total, _), (start_factor,) = group_sums(
+        [col_part, row_part, gram_of(start_basis)], [CLAIM_GROUPS, (FEAT,), (FEAT,)], 0, factored=(2,)
     )
     col_scale = lax.rsqrt(col_total + 1.0)
     row_scale_all = lax.rsqrt(row_total + 1.0)
     own_rows = row_part.shape[0] // lax.axis_size(FEAT)
     own_start = lax.axis_index(FEAT) * own_rows
     row_scale = lax.dynamic_slice_in_dim(row_scale_all, own_start, own_rows, 0)
-    first_basis, _ = orthonormal(start_basis, start_total)
+    first_basis = jnp.dot(start_basis, start_factor[1].T, precision=HIGH)
     first_operand = (col_scale[:, None] * first_basis).astype(jnp.bfloat16)
     first_partial = forward_local(tiles_here, scale_here, rows_here, cols_here, first_operand)
 
@@ -401,7 +419,7 @@
             block_t = block_t - jnp.dot(coupling, own_previous, precision=HIGH)
             wide_t = wide_t - jnp.dot(coupling, previous_t, precision=HIGH)
         gram = jnp.dot(block_t, block_t.T, precision=HIGH)
-        upper, inverse = factor_of(group_sum(gram, ALL_GROUPS, cid))
+        upper, inverse = group_factor(gram, ALL_GROUPS, cid)
         return jnp.dot(inverse, wide_t, precision=HIGH), upper
 
     def backward_partial(basis_t):
@@ -419,7 +437,8 @@
     own_scale = lax.dynamic_slice_in_dim(col_scale, own_first, own_cols, 0)
     own_second = lax.dynamic_slice_in_dim(v_second, own_first, own_cols, 0)
     q_second = own_scale[:, None] * own_sums - jnp.dot(own_second, b_second.T, precision=HIGH)
-    v_output, a_third = orthonormal(q_second, group_sum(gram_of(q_second), ALL_GROUPS, 3))
+    a_third, third_inverse = group_factor(gram_of(q_second), ALL_GROUPS, 3)
+    v_output = jnp.dot(q_second, third_inverse.T, precision=HIGH)
     bidiagonal = jnp.stack([b_first, a_second, b_second, a_third])
     u_output = lax.dynamic_slice_in_dim(u_second, own_start, own_rows, 1).T
     return (u_output, v_output, bidiagonal)

time: 434 us -> 431 us (level)
  Pallas kernels: 284 us -> 278 us
    pallas_call x5 -> x1, Pallas kernels: 33.4 us -> 6.68 us  [factor_of(): pl.pallas_call(factor_kernel, out_shape=jax.ShapeDtypeStruct((n, 2 * n),...]
    pallas_call x4, Pallas kernels: 94.1 us -> 115 us  [group_sums(): pl.pallas_call(functools.partial(group_kernel, tuple(specs), tuple(factor...]
    dot_general x0 -> x2, matrix products: none -> 4.57 us  [the longest x1 2.94 us: per_device(): first_basis = jnp.dot(start_basis, start_factor[1].T, precision=HIGH)]
    dot_general x3 -> x1, matrix products: 6.38 us -> 1.81 us  [orthonormal(): basis = jnp.dot(block, inverse.T, precision=HIGH)]
  transfers between devices with their start and end apart: 4 -> 4, of which waited for: 4 -> 4; matrix products, arithmetic and copies ran while one was open for 1% -> 1% of each run, Pallas kernels for 15% -> 14%
where the time goes in v11:
time: 431 us; the launch traced here: 429 us
  Pallas kernels  278 us (65%)
  waiting for transfers between devices  67.1 us (16%)
  matrix products  32.9 us (8%)
  local copies, waits for them, and re-layouts  19.2 us (4%)
  between operations  14 us (3%)
  blocking collectives  11.2 us (3%)
  other arithmetic  5.77 us (1%)
    pallas_call x2, Pallas kernels, claim_halving(): pl.pallas_call(functools.partial(halving_kernel, stages, gather), out_sha...  122 us
    pallas_call x4, Pallas kernels, group_sums(): pl.pallas_call(functools.partial(group_kernel, tuple(specs), tuple(factor...  115 us
    reduce_scatter x2, waiting for transfers between devices, row_step(): sums_t = lax.psum_scatter(partial_t, FEAT, scatter_dimension=1, tiled=True)  59 us
    pallas_call x4, Pallas kernels, block_product(): pl.pallas_call(kernel, grid_spec=grid_spec, out_shape=jax.ShapeDtypeStruc...  34.2 us
    psum x1, blocking collectives, per_device(): v_second, a_second = orthonormal(update, lax.psum(gram_of(update), FEAT))  11.2 us
    dot_general x2, matrix products, row_step(): return (jnp.dot(inverse, wide_t, precision=HIGH), upper)  8.82 us
  transfers between devices with their start and end apart: 4, of which 4 were waited for; matrix products, arithmetic and copies ran while one was open for 1% of the time, Pallas kernels for 14%

profile of v11, /device:TPU:64, one launch (start us, length us, event | category | flops | bytes accessed | tf_op | source)
XLA Modules:
  0.0 428.6 jit_solution(7043866115017135603)
XLA Ops:
  7.2 3.5 convert_reduce_fusion
  14.1 25.3 %shard_map.76 = (f32[32,128]{1,0:T(8,128)}, f32[64,128]{1,0:T(8,128)}, f32[64,64]{1,0:T(8,128)}, f32[64,128]{1,0:T(8,128)}) custom-call(f32[32,128]{1,0:T(8,128)} %fusion.10.refs_0_, f32[64,128]{1,0:T(8,128)} %fusion.8.refs_1_, f32[64,64]{1,0:T(8,128)} %fusion.32.refs_2_), custom_call_target="tpu_custom_call" | custom-call | tf_op jit(solution)/shard_map/pallas_call | solution.py:260
  40.1 2.9 multiply_convert_fusion.3
  43.0 9.1 %shard_map.77 = f32[64,8192]{1,0:T(8,128)} custom-call(s32[128]{0:T(128)} %bitcast.56, s32[128]{0:T(128)} %bitcast.61, f32[128]{0:T(128)} %bitcast.50, bf16[128,128,128]{2,1,0:T(8,128)(2,1)} %bitcast.43, bf16[64,4096]{1,0:T(8,128)(2,1)} %get-tuple-element.17.operand_ref), custom_call_target="tpu_custom_call" | custom-call | flops 268435456 | bytes 6815744 | tf_op jit(solution)/shard_map/pallas_call | solution.py:71
  52.1 27.6 %reduce-scatter.3.cloned.1.call-done = f32[64,2048]{1,0:T(8,128)} async-done(((f32[64,8192]{1,0:T(8,128)}), f32[64,2048]{1,0:T(8,128)}) %reduce-scatter.3.cloned.1.call-update) | async-done | bytes 524304 | tf_op jit(solution)/shard_map/reduce_scatter | solution.py:413
  80.0 2.4 fusion.5.refs_0_
  82.5 30.3 %shard_map.78 = (f32[64,64]{1,0:T(8,128)}, f32[64,128]{1,0:T(8,128)}) custom-call(f32[64,64]{1,0:T(8,128)} %fusion.5.refs_0_), custom_call_target="tpu_custom_call" | custom-call | tf_op jit(solution)/shard_map/pallas_call | solution.py:260
  112.7 4.3 all-gather.3.cloned.1.call-done
  117.0 5.2 %multiply_convert_fusion.1 = (bf16[64,8192]{1,0:T(8,128)(2,1)}, f32[64,8192]{1,0:T(8,128)}) fusion(f32[8192]{0:T(1024)S(1)} %rsqrt_bitcast_fusion, f32[64,8192]{1,0:T(8,128)} %all-gather.3.cloned.1.call-done, f32[64,128]{1,0:T(8,128)} %get-tuple-element.12), kind=kOutput, calls=%fused_computation.6 | convolution fusion | flops 404226048 | bytes 5341184 | tf_op jit(solution)/shard_map/dot_general | solution.py:423
  122.2 7.9 %shard_map.79 = f32[64,4096]{1,0:T(8,128)} custom-call(s32[128]{0:T(128)} %bitcast.57, s32[128]{0:T(128)} %bitcast.62, f32[128]{0:T(128)} %bitcast.51, bf16[128,128,128]{2,1,0:T(8,128)(2,1)} %bitcast.44, bf16[64,8192]{1,0:T(8,128)(2,1)} %get-tuple-element.19.operand_ref), custom_call_target="tpu_custom_call" | custom-call | flops 268435456 | bytes 6291456 | tf_op jit(solution)/shard_map/pallas_call | solution.py:71
  130.1 1.8 copy.10
  133.3 76.3 %shard_map.80 = f32[2048,128]{1,0:T(8,128)} custom-call(f32[2048,128]{1,0:T(8,128)} %reshape.50.x_ref), custom_call_target="tpu_custom_call" | custom-call | tf_op jit(solution)/shard_map/pallas_call | solution.py:358
  209.5 1.6 reshape.51
  212.7 2.6 convolution_subtract_fusion.1
  216.3 11.2 %psum.7.g_ref = f32[64,64]{1,0:T(8,128)} all-reduce(f32[64,64]{1,0:T(8,128)S(1)} %fusion.33), channel_id=1, replica_groups=mesh['yh'=2,'x'=4,'z'=8,'yl'=2,'c'=2] {'yl','c'}, use_global_device_ids=true, to_apply=%region_3.0 | all-reduce | flops 4096 | bytes 32768 | tf_op jit(solution)/shard_map/psum | solution.py:432
  227.5 6.7 %shard_map.81 = f32[64,128]{1,0:T(8,128)} custom-call(f32[64,64]{1,0:T(8,128)} %psum.7.g_ref), custom_call_target="tpu_custom_call" | custom-call | tf_op jit(solution)/shard_map/pallas_call | solution.py:140
  234.2 1.8 fusion.12
  237.9 9.1 %shard_map.82 = f32[64,8192]{1,0:T(8,128)} custom-call(s32[128]{0:T(128)} %bitcast.58, s32[128]{0:T(128)} %bitcast.63, f32[128]{0:T(128)} %bitcast.52, bf16[128,128,128]{2,1,0:T(8,128)(2,1)} %bitcast.45, bf16[64,4096]{1,0:T(8,128)(2,1)} %fusion.3.operand_ref), custom_call_target="tpu_custom_call" | custom-call | flops 268435456 | bytes 6815744 | tf_op jit(solution)/shard_map/pallas_call | solution.py:71
  247.0 31.4 %reduce-scatter.5.cloned.1.call-done = f32[64,2048]{1,0:T(8,128)} async-done(((f32[64,8192]{1,0:T(8,128)}), f32[64,2048]{1,0:T(8,128)}) %reduce-scatter.5.cloned.1.call-update) | async-done | bytes 524304 | tf_op jit(solution)/shard_map/reduce_scatter | solution.py:413
  278.5 1.6 convolution_subtract_fusion.2
  281.3 30.2 %shard_map.83 = (f32[64,64]{1,0:T(8,128)}, f32[64,128]{1,0:T(8,128)}) custom-call(f32[64,64]{1,0:T(8,128)} %fusion.34.refs_0_), custom_call_target="tpu_custom_call" | custom-call | tf_op jit(solution)/shard_map/pallas_call | solution.py:260
  311.6 3.8 all-gather.5.cloned.1.call-done
  315.4 3.6 convolution_subtract_fusion
  319.0 3.6 multiply_convert_fusion
  322.7 8.2 %shard_map.84 = f32[64,4096]{1,0:T(8,128)} custom-call(s32[128]{0:T(128)} %bitcast.59, s32[128]{0:T(128)} %bitcast.64, f32[128]{0:T(128)} %bitcast.53, bf16[128,128,128]{2,1,0:T(8,128)(2,1)} %bitcast.46, bf16[64,8192]{1,0:T(8,128)(2,1)} %get-tuple-element.21.operand_ref), custom_call_target="tpu_custom_call" | custom-call | flops 268435456 | bytes 6291456 | tf_op jit(solution)/shard_map/pallas_call | solution.py:71
  330.9 2.8 reshape.52
  333.7 2.9 copy.12
  336.6 2.6 reshape_reshape.3.x_ref
  339.2 45.7 %shard_map.85 = f32[32,128]{1,0:T(8,128)} custom-call(f32[2048,128]{1,0:T(8,128)} %reshape_reshape.3.x_ref), custom_call_target="tpu_custom_call" | custom-call | tf_op jit(solution)/shard_map/pallas_call | solution.py:358
  387.7 29.5 %shard_map.86 = (f32[64,64]{1,0:T(8,128)}, f32[64,128]{1,0:T(8,128)}) custom-call(f32[64,64]{1,0:T(8,128)} %fusion.35.refs_0_), custom_call_target="tpu_custom_call" | custom-call | tf_op jit(solution)/shard_map/pallas_call | solution.py:260
  417.9 1.6 fusion.14
  419.6 1.9 dynamic-slice_bitcast_fusion
  (47 shorter events, 15.6 us)
Async XLA Ops:
  7.2 3.6 copy-start
  7.2 72.5 %reduce-scatter.3.cloned.1.call-start = ((), (), s32[]{:S(2)}) async-start(), calls=%async_computation.2 | async-start | bytes 2621440 | tf_op jit(solution)/shard_map/reduce_scatter | solution.py:413
  10.7 1.6 copy-start.7
  10.8 1.6 copy-start.8
  10.8 2.5 copy-start.9
  52.1 27.9 %copy-start.6 = (f32[64,128]{1,0:T(8,128)S(1)}, f32[64,128]{1,0:T(8,128)}, u32[]{:S(2)}) copy-start(f32[64,128]{1,0:T(8,128)} %get-tuple-element.9) | copy-start | bytes 98308
  52.1 64.9 %all-gather.3.cloned.1.call-start = ((), (), s32[]{:S(2)}) async-start(), calls=%async_computation.3 | async-start | bytes 2621440 | tf_op jit(solution)/shard_map/all_gather | solution.py:414
  79.8 198.6 %reduce-scatter.5.cloned.1.call-start = ((), (), s32[]{:S(2)}) async-start(), calls=%async_computation.4 | async-start | bytes 2621440 | tf_op jit(solution)/shard_map/reduce_scatter | solution.py:413
  211.1 1.6 copy-start.4
  236.0 1.0 copy-start.2
  246.9 31.6 %copy-start.3 = (f32[64,128]{1,0:T(8,128)S(1)}, f32[64,128]{1,0:T(8,128)}, u32[]{:S(2)}) copy-start(f32[64,128]{1,0:T(8,128)} %shard_map.81) | copy-start | bytes 98308
  246.9 31.6 %copy-start.1 = (f32[64,8192]{1,0:T(8,128)S(1)}, f32[64,8192]{1,0:T(8,128)}, u32[]{:S(2)}) copy-start(f32[64,8192]{1,0:T(8,128)} %get-tuple-element.20) | copy-start | bytes 6291460
  247.0 68.4 %all-gather.5.cloned.1.call-start = ((), (), s32[]{:S(2)}) async-start(), calls=%async_computation.5 | async-start | bytes 2621440 | tf_op jit(solution)/shard_map/all_gather | solution.py:414
  311.6 7.5 %copy-start.5 = (f32[64,128]{1,0:T(8,128)S(1)}, f32[64,128]{1,0:T(8,128)}, u32[]{:S(2)}) copy-start(f32[64,128]{1,0:T(8,128)} %get-tuple-element.13) | copy-start | bytes 98308
Sparse Core Ops, SparseCore 0:
  52.2 27.4 reduce-scatter.2
  81.7 35.2 all-gather.2
  247.1 31.2 reduce-scatter.4
  280.1 35.2 all-gather.4

commit v12 on v11

--- a/solution.py
+++ b/solution.py
@@ -429,7 +429,8 @@
     u_first, b_first = row_step(first_partial, None, None, 1)
     summed = claim_halving(backward_partial(u_first), True, 4).reshape(-1, first_basis.shape[-1])
     update = col_scale[:, None] * summed - jnp.dot(first_basis, b_first.T, precision=HIGH)
-    v_second, a_second = orthonormal(update, lax.psum(gram_of(update), FEAT))
+    a_second, second_inverse = group_factor(gram_of(update), (FEAT,), 6)
+    v_second = jnp.dot(update, second_inverse.T, precision=HIGH)
     scaled = (col_scale[:, None] * v_second).astype(jnp.bfloat16)
     second_partial = forward_local(tiles_here, scale_here, rows_here, cols_here, scaled)
     u_second, b_second = row_step(second_partial, u_first, a_second, 2)

time: 431 us -> 425 us (0.986)
  blocking collectives: 11.2 us -> 0 us
    psum x1 -> x0, blocking collectives: 11.2 us -> none  [per_device(): v_second, a_second = orthonormal(update, lax.psum(gram_of(update), FEAT))]
    pallas_call x4 -> x5, Pallas kernels: 115 us -> 126 us  [group_sums(): pl.pallas_call(functools.partial(group_kernel, tuple(specs), tuple(factor...]
    pallas_call x1 -> x0, Pallas kernels: 6.68 us -> none  [factor_of(): pl.pallas_call(factor_kernel, out_shape=jax.ShapeDtypeStruct((n, 2 * n),...]
where the time goes in v12:
time: 425 us; the launch traced here: 422 us
  Pallas kernels  282 us (66%)
  waiting for transfers between devices  67.1 us (16%)
  matrix products  33.5 us (8%)
  local copies, waits for them, and re-layouts  19.1 us (4%)
  between operations  14 us (3%)
  other arithmetic  5.77 us (1%)
    pallas_call x5, Pallas kernels, group_sums(): pl.pallas_call(functools.partial(group_kernel, tuple(specs), tuple(factor...  126 us
    pallas_call x2, Pallas kernels, claim_halving(): pl.pallas_call(functools.partial(halving_kernel, stages, gather), out_sha...  122 us
    reduce_scatter x2, waiting for transfers between devices, row_step(): sums_t = lax.psum_scatter(partial_t, FEAT, scatter_dimension=1, tiled=True)  58.8 us
    pallas_call x4, Pallas kernels, block_product(): pl.pallas_call(kernel, grid_spec=grid_spec, out_shape=jax.ShapeDtypeStruc...  34.3 us
    dot_general x2, matrix products, row_step(): return (jnp.dot(inverse, wide_t, precision=HIGH), upper)  8.81 us
  transfers between devices with their start and end apart: 4, of which 4 were waited for; matrix products, arithmetic and copies ran while one was open for 1% of the time, Pallas kernels for 14%

profile of v12, /device:TPU:64, one launch (start us, length us, event | category | flops | bytes accessed | tf_op | source)
XLA Modules:
  0.0 422.3 jit_solution(17309729056656965380)
XLA Ops:
  7.2 3.5 convert_reduce_fusion
  14.1 25.3 %shard_map.76 = (f32[32,128]{1,0:T(8,128)}, f32[64,128]{1,0:T(8,128)}, f32[64,64]{1,0:T(8,128)}, f32[64,128]{1,0:T(8,128)}) custom-call(f32[32,128]{1,0:T(8,128)} %fusion.10.refs_0_, f32[64,128]{1,0:T(8,128)} %fusion.8.refs_1_, f32[64,64]{1,0:T(8,128)} %fusion.32.refs_2_), custom_call_target="tpu_custom_call" | custom-call | tf_op jit(solution)/shard_map/pallas_call | solution.py:260
  40.1 3.0 multiply_convert_fusion.3
  43.0 9.1 %shard_map.77 = f32[64,8192]{1,0:T(8,128)} custom-call(s32[128]{0:T(128)} %bitcast.56, s32[128]{0:T(128)} %bitcast.61, f32[128]{0:T(128)} %bitcast.50, bf16[128,128,128]{2,1,0:T(8,128)(2,1)} %bitcast.43, bf16[64,4096]{1,0:T(8,128)(2,1)} %get-tuple-element.19.operand_ref), custom_call_target="tpu_custom_call" | custom-call | flops 268435456 | bytes 6815744 | tf_op jit(solution)/shard_map/pallas_call | solution.py:71
  52.2 27.6 %reduce-scatter.3.cloned.1.call-done = f32[64,2048]{1,0:T(8,128)} async-done(((f32[64,8192]{1,0:T(8,128)}), f32[64,2048]{1,0:T(8,128)}) %reduce-scatter.3.cloned.1.call-update) | async-done | bytes 524304 | tf_op jit(solution)/shard_map/reduce_scatter | solution.py:413
  79.9 2.4 fusion.5.refs_0_
  82.3 30.3 %shard_map.78 = (f32[64,64]{1,0:T(8,128)}, f32[64,128]{1,0:T(8,128)}) custom-call(f32[64,64]{1,0:T(8,128)} %fusion.5.refs_0_), custom_call_target="tpu_custom_call" | custom-call | tf_op jit(solution)/shard_map/pallas_call | solution.py:260
  112.5 4.5 %all-gather.3.cloned.1.call-done = f32[64,8192]{1,0:T(8,128)} async-done(((f32[64,2048]{1,0:T(8,128)}), f32[64,8192]{1,0:T(8,128)}) %all-gather.3.cloned.1.call-update) | async-done | bytes 2097168 | tf_op jit(solution)/shard_map/all_gather | solution.py:414
  117.0 5.2 %multiply_convert_fusion.1 = (bf16[64,8192]{1,0:T(8,128)(2,1)}, f32[64,8192]{1,0:T(8,128)}) fusion(f32[8192]{0:T(1024)S(1)} %rsqrt_bitcast_fusion, f32[64,8192]{1,0:T(8,128)} %all-gather.3.cloned.1.call-done, f32[64,128]{1,0:T(8,128)} %get-tuple-element.13), kind=kOutput, calls=%fused_computation.6 | convolution fusion | flops 404226048 | bytes 5341184 | tf_op jit(solution)/shard_map/dot_general | solution.py:423
  122.2 8.1 %shard_map.79 = f32[64,4096]{1,0:T(8,128)} custom-call(s32[128]{0:T(128)} %bitcast.57, s32[128]{0:T(128)} %bitcast.62, f32[128]{0:T(128)} %bitcast.51, bf16[128,128,128]{2,1,0:T(8,128)(2,1)} %bitcast.44, bf16[64,8192]{1,0:T(8,128)(2,1)} %get-tuple-element.21.operand_ref), custom_call_target="tpu_custom_call" | custom-call | flops 268435456 | bytes 6291456 | tf_op jit(solution)/shard_map/pallas_call | solution.py:71
  130.3 1.8 copy.10
  133.4 76.2 %shard_map.80 = f32[2048,128]{1,0:T(8,128)} custom-call(f32[2048,128]{1,0:T(8,128)} %reshape.50.x_ref), custom_call_target="tpu_custom_call" | custom-call | tf_op jit(solution)/shard_map/pallas_call | solution.py:358
  209.6 1.6 reshape.51
  212.8 2.6 convolution_subtract_fusion.1
  215.4 1.6 fusion.33.refs_0_
  217.0 10.8 %shard_map.81 = (f32[64,64]{1,0:T(8,128)}, f32[64,128]{1,0:T(8,128)}) custom-call(f32[64,64]{1,0:T(8,128)} %fusion.33.refs_0_), custom_call_target="tpu_custom_call" | custom-call | tf_op jit(solution)/shard_map/pallas_call | solution.py:260
  227.8 1.8 fusion.17
  231.5 9.0 %shard_map.82 = f32[64,8192]{1,0:T(8,128)} custom-call(s32[128]{0:T(128)} %bitcast.58, s32[128]{0:T(128)} %bitcast.63, f32[128]{0:T(128)} %bitcast.52, bf16[128,128,128]{2,1,0:T(8,128)(2,1)} %bitcast.45, bf16[64,4096]{1,0:T(8,128)(2,1)} %fusion.3.operand_ref), custom_call_target="tpu_custom_call" | custom-call | flops 268435456 | bytes 6815744 | tf_op jit(solution)/shard_map/pallas_call | solution.py:71
  240.8 31.2 %reduce-scatter.5.cloned.1.call-done = f32[64,2048]{1,0:T(8,128)} async-done(((f32[64,8192]{1,0:T(8,128)}), f32[64,2048]{1,0:T(8,128)}) %reduce-scatter.5.cloned.1.call-update) | async-done | bytes 524304 | tf_op jit(solution)/shard_map/reduce_scatter | solution.py:413
  272.2 1.6 convolution_subtract_fusion.2
  275.0 30.2 %shard_map.83 = (f32[64,64]{1,0:T(8,128)}, f32[64,128]{1,0:T(8,128)}) custom-call(f32[64,64]{1,0:T(8,128)} %fusion.34.refs_0_), custom_call_target="tpu_custom_call" | custom-call | tf_op jit(solution)/shard_map/pallas_call | solution.py:260
  305.3 3.8 all-gather.5.cloned.1.call-done
  309.1 3.6 convolution_subtract_fusion
  312.7 3.6 multiply_convert_fusion
  316.3 8.2 %shard_map.84 = f32[64,4096]{1,0:T(8,128)} custom-call(s32[128]{0:T(128)} %bitcast.59, s32[128]{0:T(128)} %bitcast.64, f32[128]{0:T(128)} %bitcast.53, bf16[128,128,128]{2,1,0:T(8,128)(2,1)} %bitcast.46, bf16[64,8192]{1,0:T(8,128)(2,1)} %get-tuple-element.23.operand_ref), custom_call_target="tpu_custom_call" | custom-call | flops 268435456 | bytes 6291456 | tf_op jit(solution)/shard_map/pallas_call | solution.py:71
  324.5 2.8 reshape.52
  327.3 2.9 copy.12
  330.2 2.6 reshape_reshape.3.x_ref
  332.8 45.7 %shard_map.85 = f32[32,128]{1,0:T(8,128)} custom-call(f32[2048,128]{1,0:T(8,128)} %reshape_reshape.3.x_ref), custom_call_target="tpu_custom_call" | custom-call | tf_op jit(solution)/shard_map/pallas_call | solution.py:358
  381.2 29.6 %shard_map.86 = (f32[64,64]{1,0:T(8,128)}, f32[64,128]{1,0:T(8,128)}) custom-call(f32[64,64]{1,0:T(8,128)} %fusion.35.refs_0_), custom_call_target="tpu_custom_call" | custom-call | tf_op jit(solution)/shard_map/pallas_call | solution.py:260
  411.6 1.6 fusion.12
  413.3 1.9 dynamic-slice_bitcast_fusion
  (45 shorter events, 14.6 us)
Async XLA Ops:
  7.2 3.6 copy-start
  7.2 72.6 %reduce-scatter.3.cloned.1.call-start = ((), (), s32[]{:S(2)}) async-start(), calls=%async_computation.2 | async-start | bytes 2621440 | tf_op jit(solution)/shard_map/reduce_scatter | solution.py:413
  10.7 1.6 copy-start.7
  10.8 1.6 copy-start.8
  10.8 2.5 copy-start.9
  52.1 27.7 %copy-start.6 = (f32[64,128]{1,0:T(8,128)S(1)}, f32[64,128]{1,0:T(8,128)}, u32[]{:S(2)}) copy-start(f32[64,128]{1,0:T(8,128)} %get-tuple-element.10) | copy-start | bytes 98308
  52.1 64.9 %all-gather.3.cloned.1.call-start = ((), (), s32[]{:S(2)}) async-start(), calls=%async_computation.3 | async-start | bytes 2621440 | tf_op jit(solution)/shard_map/all_gather | solution.py:414
  79.8 192.3 %reduce-scatter.5.cloned.1.call-start = ((), (), s32[]{:S(2)}) async-start(), calls=%async_computation.4 | async-start | bytes 2621440 | tf_op jit(solution)/shard_map/reduce_scatter | solution.py:413
  211.2 1.6 copy-start.4
  229.7 1.0 copy-start.2
  240.5 31.7 %copy-start.3 = (f32[64,128]{1,0:T(8,128)S(1)}, f32[64,128]{1,0:T(8,128)}, u32[]{:S(2)}) copy-start(f32[64,128]{1,0:T(8,128)} %get-tuple-element.14) | copy-start | bytes 98308
  240.5 31.7 %copy-start.1 = (f32[64,8192]{1,0:T(8,128)S(1)}, f32[64,8192]{1,0:T(8,128)}, u32[]{:S(2)}) copy-start(f32[64,8192]{1,0:T(8,128)} %get-tuple-element.22) | copy-start | bytes 6291460
  240.6 68.5 %all-gather.5.cloned.1.call-start = ((), (), s32[]{:S(2)}) async-start(), calls=%async_computation.5 | async-start | bytes 2621440 | tf_op jit(solution)/shard_map/all_gather | solution.py:414
  305.3 7.5 %copy-start.5 = (f32[64,128]{1,0:T(8,128)S(1)}, f32[64,128]{1,0:T(8,128)}, u32[]{:S(2)}) copy-start(f32[64,128]{1,0:T(8,128)} %get-tuple-element.15) | copy-start | bytes 98308
Sparse Core Ops, SparseCore 0:
  52.2 27.4 reduce-scatter.2
  81.7 35.2 all-gather.2
  240.7 31.3 reduce-scatter.4
  273.7 35.2 all-gather.4

commit v13 on v12

--- a/solution.py
+++ b/solution.py
@@ -285,19 +285,22 @@
 CLAIM_GROUPS = (("z",), ("yh", "x"))
 
 
-def halving_kernel(stages, gather, x_ref, o_ref, *scratch):
+def halving_kernel(stages, alternate, gather, x_ref, o_ref, *scratch):
     if gather:
         work, recv, back, rs_send, rs_recv, ag_send, ag_recv = o_ref, *scratch
     else:
         work, recv, rs_send, rs_recv = scratch
     coords = [lax.axis_index(name) for name in FINE]
+    second = coords[FINE.index("c")]
     partners, bits = [], []
-    for axis, step in stages:
-        place = coords[axis]
-        bit = (place // step) % 2
-        flip = place + step * (1 - 2 * bit)
-        partners.append(tuple(flip if i == axis else c for i, c in enumerate(coords)))
-        bits.append(bit)
+    for (axis, step), (other, other_step) in zip(stages, alternate):
+        bit = (coords[axis] // step) % 2
+        other_bit = (coords[other] // other_step) % 2
+        place = list(coords)
+        place[axis] = place[axis] + (1 - second) * step * (1 - 2 * bit)
+        place[other] = place[other] + second * other_step * (1 - 2 * other_bit)
+        partners.append(tuple(place))
+        bits.append(bit + second * (other_bit - bit))
     barrier = pltpu.get_barrier_semaphore()
     for partner in partners:
         pl.semaphore_signal(barrier, inc=1, device_id=partner, device_id_type=pl.DeviceIdType.MESH)
@@ -344,10 +347,12 @@
 
 
 CLAIM_STAGES = (("z", 1), ("x", 1), ("z", 2), ("x", 2), ("yh", 1), ("z", 4))
-
-
-def claim_halving(value, gather, cid):
+SWAPPED_STAGES = (("x", 1), ("z", 1), ("x", 2), ("z", 2), ("yh", 1), ("z", 4))
+
+
+def claim_halving(value, gather, cid, alternate_order=None):
     stages = tuple((FINE.index(name), step) for name, step in CLAIM_STAGES)
+    alternate = tuple((FINE.index(name), step) for name, step in (alternate_order or CLAIM_STAGES))
     count = len(stages)
     flat = value.reshape(-1, 128)
     rows = flat.shape[0]
@@ -356,7 +361,7 @@
     scratch += [pltpu.VMEM(flat.shape, flat.dtype)] * (2 if gather else 1)
     scratch += [pltpu.SemaphoreType.DMA((count,))] * (4 if gather else 2)
     out = pl.pallas_call(
-        functools.partial(halving_kernel, stages, gather),
+        functools.partial(halving_kernel, stages, alternate, gather),
         out_shape=jax.ShapeDtypeStruct((out_rows, 128), flat.dtype),
         in_specs=[pl.BlockSpec(memory_space=pltpu.VMEM)],
         out_specs=pl.BlockSpec(memory_space=pltpu.VMEM),
@@ -427,7 +432,7 @@
         return backward_local(tiles_here, scale_here, rows_here, cols_here, operand_t, col_count)
 
     u_first, b_first = row_step(first_partial, None, None, 1)
-    summed = claim_halving(backward_partial(u_first), True, 4).reshape(-1, first_basis.shape[-1])
+    summed = claim_halving(backward_partial(u_first), True, 4, SWAPPED_STAGES).reshape(-1, first_basis.shape[-1])
     update = col_scale[:, None] * summed - jnp.dot(first_basis, b_first.T, precision=HIGH)
     a_second, second_inverse = group_factor(gram_of(update), (FEAT,), 6)
     v_second = jnp.dot(update, second_inverse.T, precision=HIGH)

time: 425 us -> 418 us (0.984)
  Pallas kernels: 282 us -> 277 us
    pallas_call x2, Pallas kernels: 122 us -> 116 us  [claim_halving(): pl.pallas_call(functools.partial(halving_kernel, stages, alternate, gathe...]
  transfers between devices with their start and end apart: 4 -> 4, of which waited for: 4 -> 4; matrix products, arithmetic and copies ran while one was open for 1% -> 1% of each run, Pallas kernels for 14% -> 15%
where the time goes in v13:
time: 418 us; the launch traced here: 416 us
  Pallas kernels  277 us (66%)
  waiting for transfers between devices  66 us (16%)
  matrix products  33.5 us (8%)
  local copies, waits for them, and re-layouts  19.1 us (5%)
  between operations  14 us (3%)
  other arithmetic  5.77 us (1%)
    pallas_call x5, Pallas kernels, group_sums(): pl.pallas_call(functools.partial(group_kernel, tuple(specs), tuple(factor...  126 us
    pallas_call x2, Pallas kernels, claim_halving(): pl.pallas_call(functools.partial(halving_kernel, stages, alternate, gathe...  116 us
    reduce_scatter x2, waiting for transfers between devices, row_step(): sums_t = lax.psum_scatter(partial_t, FEAT, scatter_dimension=1, tiled=True)  57.8 us
    pallas_call x4, Pallas kernels, block_product(): pl.pallas_call(kernel, grid_spec=grid_spec, out_shape=jax.ShapeDtypeStruc...  34.3 us
    dot_general x2, matrix products, row_step(): return (jnp.dot(inverse, wide_t, precision=HIGH), upper)  8.81 us
  transfers between devices with their start and end apart: 4, of which 4 were waited for; matrix products, arithmetic and copies ran while one was open for 1% of the time, Pallas kernels for 15%

profile of v13, /device:TPU:64, one launch (start us, length us, event | category | flops | bytes accessed | tf_op | source)
XLA Modules:
  0.0 415.7 jit_solution(15691571504449849338)
XLA Ops:
  7.2 3.5 convert_reduce_fusion
  14.1 25.3 %shard_map.76 = (f32[32,128]{1,0:T(8,128)}, f32[64,128]{1,0:T(8,128)}, f32[64,64]{1,0:T(8,128)}, f32[64,128]{1,0:T(8,128)}) custom-call(f32[32,128]{1,0:T(8,128)} %fusion.10.refs_0_, f32[64,128]{1,0:T(8,128)} %fusion.8.refs_1_, f32[64,64]{1,0:T(8,128)} %fusion.32.refs_2_), custom_call_target="tpu_custom_call" | custom-call | tf_op jit(solution)/shard_map/pallas_call | solution.py:260
  40.1 3.0 multiply_convert_fusion.3
  43.0 9.1 %shard_map.77 = f32[64,8192]{1,0:T(8,128)} custom-call(s32[128]{0:T(128)} %bitcast.56, s32[128]{0:T(128)} %bitcast.61, f32[128]{0:T(128)} %bitcast.50, bf16[128,128,128]{2,1,0:T(8,128)(2,1)} %bitcast.43, bf16[64,4096]{1,0:T(8,128)(2,1)} %get-tuple-element.19.operand_ref), custom_call_target="tpu_custom_call" | custom-call | flops 268435456 | bytes 6815744 | tf_op jit(solution)/shard_map/pallas_call | solution.py:71
  52.1 27.6 %reduce-scatter.3.cloned.1.call-done = f32[64,2048]{1,0:T(8,128)} async-done(((f32[64,8192]{1,0:T(8,128)}), f32[64,2048]{1,0:T(8,128)}) %reduce-scatter.3.cloned.1.call-update) | async-done | bytes 524304 | tf_op jit(solution)/shard_map/reduce_scatter | solution.py:418
  79.9 2.4 fusion.5.refs_0_
  82.3 30.3 %shard_map.78 = (f32[64,64]{1,0:T(8,128)}, f32[64,128]{1,0:T(8,128)}) custom-call(f32[64,64]{1,0:T(8,128)} %fusion.5.refs_0_), custom_call_target="tpu_custom_call" | custom-call | tf_op jit(solution)/shard_map/pallas_call | solution.py:260
  112.5 4.4 %all-gather.3.cloned.1.call-done = f32[64,8192]{1,0:T(8,128)} async-done(((f32[64,2048]{1,0:T(8,128)}), f32[64,8192]{1,0:T(8,128)}) %all-gather.3.cloned.1.call-update) | async-done | bytes 2097168 | tf_op jit(solution)/shard_map/all_gather | solution.py:419
  117.0 5.2 %multiply_convert_fusion.1 = (bf16[64,8192]{1,0:T(8,128)(2,1)}, f32[64,8192]{1,0:T(8,128)}) fusion(f32[8192]{0:T(1024)S(1)} %rsqrt_bitcast_fusion, f32[64,8192]{1,0:T(8,128)} %all-gather.3.cloned.1.call-done, f32[64,128]{1,0:T(8,128)} %get-tuple-element.13), kind=kOutput, calls=%fused_computation.6 | convolution fusion | flops 404226048 | bytes 5341184 | tf_op jit(solution)/shard_map/dot_general | solution.py:428
  122.2 8.1 %shard_map.79 = f32[64,4096]{1,0:T(8,128)} custom-call(s32[128]{0:T(128)} %bitcast.57, s32[128]{0:T(128)} %bitcast.62, f32[128]{0:T(128)} %bitcast.51, bf16[128,128,128]{2,1,0:T(8,128)(2,1)} %bitcast.44, bf16[64,8192]{1,0:T(8,128)(2,1)} %get-tuple-element.21.operand_ref), custom_call_target="tpu_custom_call" | custom-call | flops 268435456 | bytes 6291456 | tf_op jit(solution)/shard_map/pallas_call | solution.py:71
  130.3 1.8 copy.10
  133.4 70.7 %shard_map.80 = f32[2048,128]{1,0:T(8,128)} custom-call(f32[2048,128]{1,0:T(8,128)} %reshape.50.x_ref), custom_call_target="tpu_custom_call" | custom-call | tf_op jit(solution)/shard_map/pallas_call | solution.py:363
  204.1 1.6 reshape.51
  207.3 2.6 convolution_subtract_fusion.1
  209.9 1.6 fusion.33.refs_0_
  211.5 10.8 %shard_map.81 = (f32[64,64]{1,0:T(8,128)}, f32[64,128]{1,0:T(8,128)}) custom-call(f32[64,64]{1,0:T(8,128)} %fusion.33.refs_0_), custom_call_target="tpu_custom_call" | custom-call | tf_op jit(solution)/shard_map/pallas_call | solution.py:260
  222.4 1.8 fusion.17
  226.0 9.0 %shard_map.82 = f32[64,8192]{1,0:T(8,128)} custom-call(s32[128]{0:T(128)} %bitcast.58, s32[128]{0:T(128)} %bitcast.63, f32[128]{0:T(128)} %bitcast.52, bf16[128,128,128]{2,1,0:T(8,128)(2,1)} %bitcast.45, bf16[64,4096]{1,0:T(8,128)(2,1)} %fusion.3.operand_ref), custom_call_target="tpu_custom_call" | custom-call | flops 268435456 | bytes 6815744 | tf_op jit(solution)/shard_map/pallas_call | solution.py:71
  235.3 30.2 %reduce-scatter.5.cloned.1.call-done = f32[64,2048]{1,0:T(8,128)} async-done(((f32[64,8192]{1,0:T(8,128)}), f32[64,2048]{1,0:T(8,128)}) %reduce-scatter.5.cloned.1.call-update) | async-done | bytes 524304 | tf_op jit(solution)/shard_map/reduce_scatter | solution.py:418
  265.7 1.6 convolution_subtract_fusion.2
  268.5 30.2 %shard_map.83 = (f32[64,64]{1,0:T(8,128)}, f32[64,128]{1,0:T(8,128)}) custom-call(f32[64,64]{1,0:T(8,128)} %fusion.34.refs_0_), custom_call_target="tpu_custom_call" | custom-call | tf_op jit(solution)/shard_map/pallas_call | solution.py:260
  298.7 3.8 all-gather.5.cloned.1.call-done
  302.5 3.7 convolution_subtract_fusion
  306.2 3.6 multiply_convert_fusion
  309.8 8.2 %shard_map.84 = f32[64,4096]{1,0:T(8,128)} custom-call(s32[128]{0:T(128)} %bitcast.59, s32[128]{0:T(128)} %bitcast.64, f32[128]{0:T(128)} %bitcast.53, bf16[128,128,128]{2,1,0:T(8,128)(2,1)} %bitcast.46, bf16[64,8192]{1,0:T(8,128)(2,1)} %get-tuple-element.23.operand_ref), custom_call_target="tpu_custom_call" | custom-call | flops 268435456 | bytes 6291456 | tf_op jit(solution)/shard_map/pallas_call | solution.py:71
  318.0 2.8 reshape.52
  320.8 2.9 copy.12
  323.7 2.6 reshape_reshape.3.x_ref
  326.2 45.7 %shard_map.85 = f32[32,128]{1,0:T(8,128)} custom-call(f32[2048,128]{1,0:T(8,128)} %reshape_reshape.3.x_ref), custom_call_target="tpu_custom_call" | custom-call | tf_op jit(solution)/shard_map/pallas_call | solution.py:363
  374.7 29.5 %shard_map.86 = (f32[64,64]{1,0:T(8,128)}, f32[64,128]{1,0:T(8,128)}) custom-call(f32[64,64]{1,0:T(8,128)} %fusion.35.refs_0_), custom_call_target="tpu_custom_call" | custom-call | tf_op jit(solution)/shard_map/pallas_call | solution.py:260
  405.0 1.6 fusion.12
  406.6 1.9 dynamic-slice_bitcast_fusion
  (45 shorter events, 14.6 us)
Async XLA Ops:
  7.2 3.6 copy-start
  7.2 72.5 %reduce-scatter.3.cloned.1.call-start = ((), (), s32[]{:S(2)}) async-start(), calls=%async_computation.2 | async-start | bytes 2621440 | tf_op jit(solution)/shard_map/reduce_scatter | solution.py:418
  10.7 1.6 copy-start.7
  10.8 1.6 copy-start.8
  10.8 2.5 copy-start.9
  52.1 27.7 %copy-start.6 = (f32[64,128]{1,0:T(8,128)S(1)}, f32[64,128]{1,0:T(8,128)}, u32[]{:S(2)}) copy-start(f32[64,128]{1,0:T(8,128)} %get-tuple-element.10) | copy-start | bytes 98308
  52.1 64.9 %all-gather.3.cloned.1.call-start = ((), (), s32[]{:S(2)}) async-start(), calls=%async_computation.3 | async-start | bytes 2621440 | tf_op jit(solution)/shard_map/all_gather | solution.py:419
  79.7 185.8 %reduce-scatter.5.cloned.1.call-start = ((), (), s32[]{:S(2)}) async-start(), calls=%async_computation.4 | async-start | bytes 2621440 | tf_op jit(solution)/shard_map/reduce_scatter | solution.py:418
  205.7 1.6 copy-start.4
  224.2 1.0 copy-start.2
  235.1 30.6 %copy-start.3 = (f32[64,128]{1,0:T(8,128)S(1)}, f32[64,128]{1,0:T(8,128)}, u32[]{:S(2)}) copy-start(f32[64,128]{1,0:T(8,128)} %get-tuple-element.14) | copy-start | bytes 98308
  235.1 30.6 %copy-start.1 = (f32[64,8192]{1,0:T(8,128)S(1)}, f32[64,8192]{1,0:T(8,128)}, u32[]{:S(2)}) copy-start(f32[64,8192]{1,0:T(8,128)} %get-tuple-element.22) | copy-start | bytes 6291460
  235.1 67.4 %all-gather.5.cloned.1.call-start = ((), (), s32[]{:S(2)}) async-start(), calls=%async_computation.5 | async-start | bytes 2621440 | tf_op jit(solution)/shard_map/all_gather | solution.py:419
  298.7 7.5 %copy-start.5 = (f32[64,128]{1,0:T(8,128)S(1)}, f32[64,128]{1,0:T(8,128)}, u32[]{:S(2)}) copy-start(f32[64,128]{1,0:T(8,128)} %get-tuple-element.15) | copy-start | bytes 98308
Sparse Core Ops, SparseCore 0:
  52.2 27.4 reduce-scatter.2
  81.7 35.2 all-gather.2
  235.2 30.2 reduce-scatter.4
  267.2 35.2 all-gather.4

commit v14 on v13

--- a/solution.py
+++ b/solution.py
@@ -285,7 +285,7 @@
 CLAIM_GROUPS = (("z",), ("yh", "x"))
 
 
-def halving_kernel(stages, alternate, gather, x_ref, o_ref, *scratch):
+def halving_kernel(stages, alternate, gather, interleaved, x_ref, o_ref, *scratch):
     if gather:
         work, recv, back, rs_send, rs_recv, ag_send, ag_recv = o_ref, *scratch
     else:
@@ -309,12 +309,41 @@
     total = work.shape[0]
     base = 0
     pieces = []
+    quarter = total // 4
     for s, partner in enumerate(partners):
         size = total >> s
         half = size // 2
         keep = base + bits[s] * half
         give = base + (1 - bits[s]) * half
         slot = pl.ds(total - size, half)
+        if interleaved and s == 0:
+            gap = (1 - second) * quarter + second * 2 * quarter
+            give = (1 - second) * (1 - bits[0]) * 2 * quarter + second * (1 - bits[0]) * quarter
+            keep = (1 - second) * bits[0] * 2 * quarter + second * bits[0] * quarter
+            copies = []
+            for part in range(2):
+                copy = pltpu.make_async_remote_copy(
+                    src_ref=work.at[pl.ds(give + part * gap, quarter)],
+                    dst_ref=recv.at[pl.ds(part * quarter, quarter)],
+                    send_sem=rs_send.at[len(partners) * part],
+                    recv_sem=rs_recv.at[len(partners) * part],
+                    device_id=partner,
+                    device_id_type=pl.DeviceIdType.MESH,
+                )
+                copy.start()
+                copies.append(copy)
+            for copy in copies:
+                copy.wait()
+            for part in range(2):
+                rows = pl.ds(keep + part * gap, quarter)
+                work[rows, :] = work[rows, :] + recv[pl.ds(part * quarter, quarter), :]
+            continue
+        if interleaved and s == 1:
+            first, now = bits[0], bits[1]
+            keep = (1 - second) * (first * 2 * quarter + now * quarter) + second * (now * 2 * quarter + first * quarter)
+            give = (1 - second) * (first * 2 * quarter + (1 - now) * quarter) + second * (
+                (1 - now) * 2 * quarter + first * quarter
+            )
         copy = pltpu.make_async_remote_copy(
             src_ref=work.at[pl.ds(give, half)],
             dst_ref=recv.at[slot],
@@ -348,20 +377,22 @@
 
 CLAIM_STAGES = (("z", 1), ("x", 1), ("z", 2), ("x", 2), ("yh", 1), ("z", 4))
 SWAPPED_STAGES = (("x", 1), ("z", 1), ("x", 2), ("z", 2), ("yh", 1), ("z", 4))
+SWAPPED_FIRST = (("x", 1), ("z", 1), ("z", 2), ("x", 2), ("yh", 1), ("z", 4))
 
 
 def claim_halving(value, gather, cid, alternate_order=None):
     stages = tuple((FINE.index(name), step) for name, step in CLAIM_STAGES)
     alternate = tuple((FINE.index(name), step) for name, step in (alternate_order or CLAIM_STAGES))
+    interleaved = (not gather) and alternate != stages
     count = len(stages)
     flat = value.reshape(-1, 128)
     rows = flat.shape[0]
     out_rows = rows if gather else rows >> count
     scratch = [] if gather else [pltpu.VMEM(flat.shape, flat.dtype)]
     scratch += [pltpu.VMEM(flat.shape, flat.dtype)] * (2 if gather else 1)
-    scratch += [pltpu.SemaphoreType.DMA((count,))] * (4 if gather else 2)
+    scratch += [pltpu.SemaphoreType.DMA((count + 1,))] * (4 if gather else 2)
     out = pl.pallas_call(
-        functools.partial(halving_kernel, stages, alternate, gather),
+        functools.partial(halving_kernel, stages, alternate, gather, interleaved),
         out_shape=jax.ShapeDtypeStruct((out_rows, 128), flat.dtype),
         in_specs=[pl.BlockSpec(memory_space=pltpu.VMEM)],
         out_specs=pl.BlockSpec(memory_space=pltpu.VMEM),
@@ -388,7 +419,7 @@
     rows = value.shape[0] // lax.axis_size(CLAIM)
     bits = value.reshape(2, 2, 2, 2, 2, 2, rows, width)
     ordered = bits.transpose(5, 2, 4, 1, 0, 3, 6, 7).reshape(value.shape)
-    return claim_halving(ordered, False, 5).reshape(rows, width)
+    return claim_halving(ordered, False, 5, SWAPPED_FIRST).reshape(rows, width)
 
 
 def per_device(block_tiles, block_scale, row_index, col_index, start_basis):

time: 418 us -> 411 us (0.983)
  Pallas kernels: 277 us -> 271 us
    pallas_call x2, Pallas kernels: 116 us -> 110 us  [claim_halving(): pl.pallas_call(functools.partial(halving_kernel, stages, alternate, gathe...]
where the time goes in v14:
time: 411 us; the launch traced here: 409 us
  Pallas kernels  271 us (66%)
  waiting for transfers between devices  66.1 us (16%)
  matrix products  33.5 us (8%)
  local copies, waits for them, and re-layouts  19.1 us (5%)
  between operations  14 us (3%)
  other arithmetic  5.77 us (1%)
    pallas_call x5, Pallas kernels, group_sums(): pl.pallas_call(functools.partial(group_kernel, tuple(specs), tuple(factor...  127 us
    pallas_call x2, Pallas kernels, claim_halving(): pl.pallas_call(functools.partial(halving_kernel, stages, alternate, gathe...  110 us
    reduce_scatter x2, waiting for transfers between devices, row_step(): sums_t = lax.psum_scatter(partial_t, FEAT, scatter_dimension=1, tiled=True)  57.8 us
    pallas_call x4, Pallas kernels, block_product(): pl.pallas_call(kernel, grid_spec=grid_spec, out_shape=jax.ShapeDtypeStruc...  34.3 us
    dot_general x2, matrix products, row_step(): return (jnp.dot(inverse, wide_t, precision=HIGH), upper)  8.81 us
    all_gather x2, waiting for transfers between devices, row_step(): all_t = lax.all_gather(sums_t, FEAT, axis=1, tiled=True)  8.28 us
  transfers between devices with their start and end apart: 4, of which 4 were waited for; matrix products, arithmetic and copies ran while one was open for 1% of the time, Pallas kernels for 15%

profile of v14, /device:TPU:64, one launch (start us, length us, event | category | flops | bytes accessed | tf_op | source)
XLA Modules:
  0.0 409.5 jit_solution(1739450466213078894)
XLA Ops:
  7.2 3.5 convert_reduce_fusion
  10.8 1.6 fusion.32.refs_2_
  14.1 25.3 %shard_map.76 = (f32[32,128]{1,0:T(8,128)}, f32[64,128]{1,0:T(8,128)}, f32[64,64]{1,0:T(8,128)}, f32[64,128]{1,0:T(8,128)}) custom-call(f32[32,128]{1,0:T(8,128)} %fusion.10.refs_0_, f32[64,128]{1,0:T(8,128)} %fusion.8.refs_1_, f32[64,64]{1,0:T(8,128)} %fusion.32.refs_2_), custom_call_target="tpu_custom_call" | custom-call | tf_op jit(solution)/shard_map/pallas_call | solution.py:260
  40.1 3.0 multiply_convert_fusion.3
  43.0 9.1 %shard_map.77 = f32[64,8192]{1,0:T(8,128)} custom-call(s32[128]{0:T(128)} %bitcast.56, s32[128]{0:T(128)} %bitcast.61, f32[128]{0:T(128)} %bitcast.50, bf16[128,128,128]{2,1,0:T(8,128)(2,1)} %bitcast.43, bf16[64,4096]{1,0:T(8,128)(2,1)} %get-tuple-element.19.operand_ref), custom_call_target="tpu_custom_call" | custom-call | flops 268435456 | bytes 6815744 | tf_op jit(solution)/shard_map/pallas_call | solution.py:71
  52.1 27.6 %reduce-scatter.3.cloned.1.call-done = f32[64,2048]{1,0:T(8,128)} async-done(((f32[64,8192]{1,0:T(8,128)}), f32[64,2048]{1,0:T(8,128)}) %reduce-scatter.3.cloned.1.call-update) | async-done | bytes 524304 | tf_op jit(solution)/shard_map/reduce_scatter | solution.py:449
  79.9 2.4 fusion.5.refs_0_
  82.3 30.2 %shard_map.78 = (f32[64,64]{1,0:T(8,128)}, f32[64,128]{1,0:T(8,128)}) custom-call(f32[64,64]{1,0:T(8,128)} %fusion.5.refs_0_), custom_call_target="tpu_custom_call" | custom-call | tf_op jit(solution)/shard_map/pallas_call | solution.py:260
  112.5 4.5 %all-gather.3.cloned.1.call-done = f32[64,8192]{1,0:T(8,128)} async-done(((f32[64,2048]{1,0:T(8,128)}), f32[64,8192]{1,0:T(8,128)}) %all-gather.3.cloned.1.call-update) | async-done | bytes 2097168 | tf_op jit(solution)/shard_map/all_gather | solution.py:450
  117.0 5.2 %multiply_convert_fusion.1 = (bf16[64,8192]{1,0:T(8,128)(2,1)}, f32[64,8192]{1,0:T(8,128)}) fusion(f32[8192]{0:T(1024)S(1)} %rsqrt_bitcast_fusion, f32[64,8192]{1,0:T(8,128)} %all-gather.3.cloned.1.call-done, f32[64,128]{1,0:T(8,128)} %get-tuple-element.13), kind=kOutput, calls=%fused_computation.6 | convolution fusion | flops 404226048 | bytes 5341184 | tf_op jit(solution)/shard_map/dot_general | solution.py:459
  122.2 8.1 %shard_map.79 = f32[64,4096]{1,0:T(8,128)} custom-call(s32[128]{0:T(128)} %bitcast.57, s32[128]{0:T(128)} %bitcast.62, f32[128]{0:T(128)} %bitcast.51, bf16[128,128,128]{2,1,0:T(8,128)(2,1)} %bitcast.44, bf16[64,8192]{1,0:T(8,128)(2,1)} %get-tuple-element.21.operand_ref), custom_call_target="tpu_custom_call" | custom-call | flops 268435456 | bytes 6291456 | tf_op jit(solution)/shard_map/pallas_call | solution.py:71
  130.3 1.8 copy.10
  133.5 70.7 %shard_map.80 = f32[2048,128]{1,0:T(8,128)} custom-call(f32[2048,128]{1,0:T(8,128)} %reshape.50.x_ref), custom_call_target="tpu_custom_call" | custom-call | tf_op jit(solution)/shard_map/pallas_call | solution.py:394
  204.2 1.6 reshape.51
  207.3 2.6 convolution_subtract_fusion.1
  211.5 10.8 %shard_map.81 = (f32[64,64]{1,0:T(8,128)}, f32[64,128]{1,0:T(8,128)}) custom-call(f32[64,64]{1,0:T(8,128)} %fusion.33.refs_0_), custom_call_target="tpu_custom_call" | custom-call | tf_op jit(solution)/shard_map/pallas_call | solution.py:260
  222.4 1.8 fusion.17
  226.1 9.0 %shard_map.82 = f32[64,8192]{1,0:T(8,128)} custom-call(s32[128]{0:T(128)} %bitcast.58, s32[128]{0:T(128)} %bitcast.63, f32[128]{0:T(128)} %bitcast.52, bf16[128,128,128]{2,1,0:T(8,128)(2,1)} %bitcast.45, bf16[64,4096]{1,0:T(8,128)(2,1)} %fusion.3.operand_ref), custom_call_target="tpu_custom_call" | custom-call | flops 268435456 | bytes 6815744 | tf_op jit(solution)/shard_map/pallas_call | solution.py:71
  235.4 30.2 %reduce-scatter.5.cloned.1.call-done = f32[64,2048]{1,0:T(8,128)} async-done(((f32[64,8192]{1,0:T(8,128)}), f32[64,2048]{1,0:T(8,128)}) %reduce-scatter.5.cloned.1.call-update) | async-done | bytes 524304 | tf_op jit(solution)/shard_map/reduce_scatter | solution.py:449
  265.7 1.6 convolution_subtract_fusion.2
  268.5 30.3 %shard_map.83 = (f32[64,64]{1,0:T(8,128)}, f32[64,128]{1,0:T(8,128)}) custom-call(f32[64,64]{1,0:T(8,128)} %fusion.34.refs_0_), custom_call_target="tpu_custom_call" | custom-call | tf_op jit(solution)/shard_map/pallas_call | solution.py:260
  298.8 3.8 all-gather.5.cloned.1.call-done
  302.6 3.7 convolution_subtract_fusion
  306.3 3.6 multiply_convert_fusion
  309.9 8.2 %shard_map.84 = f32[64,4096]{1,0:T(8,128)} custom-call(s32[128]{0:T(128)} %bitcast.59, s32[128]{0:T(128)} %bitcast.64, f32[128]{0:T(128)} %bitcast.53, bf16[128,128,128]{2,1,0:T(8,128)(2,1)} %bitcast.46, bf16[64,8192]{1,0:T(8,128)(2,1)} %get-tuple-element.23.operand_ref), custom_call_target="tpu_custom_call" | custom-call | flops 268435456 | bytes 6291456 | tf_op jit(solution)/shard_map/pallas_call | solution.py:71
  318.0 2.8 reshape.52
  320.8 2.9 copy.12
  323.7 2.6 reshape_reshape.3.x_ref
  326.3 38.8 %shard_map.85 = f32[32,128]{1,0:T(8,128)} custom-call(f32[2048,128]{1,0:T(8,128)} %reshape_reshape.3.x_ref), custom_call_target="tpu_custom_call" | custom-call | tf_op jit(solution)/shard_map/pallas_call | solution.py:394
  367.9 30.1 %shard_map.86 = (f32[64,64]{1,0:T(8,128)}, f32[64,128]{1,0:T(8,128)}) custom-call(f32[64,64]{1,0:T(8,128)} %fusion.35.refs_0_), custom_call_target="tpu_custom_call" | custom-call | tf_op jit(solution)/shard_map/pallas_call | solution.py:260
  398.8 1.6 fusion.12
  400.4 1.9 dynamic-slice_bitcast_fusion
  (45 shorter events, 14.6 us)
Async XLA Ops:
  7.2 3.6 copy-start
  7.2 72.5 %reduce-scatter.3.cloned.1.call-start = ((), (), s32[]{:S(2)}) async-start(), calls=%async_computation.2 | async-start | bytes 2621440 | tf_op jit(solution)/shard_map/reduce_scatter | solution.py:449
  10.7 1.6 copy-start.7
  10.8 1.6 copy-start.8
  10.8 2.5 copy-start.9
  52.1 27.7 %copy-start.6 = (f32[64,128]{1,0:T(8,128)S(1)}, f32[64,128]{1,0:T(8,128)}, u32[]{:S(2)}) copy-start(f32[64,128]{1,0:T(8,128)} %get-tuple-element.10) | copy-start | bytes 98308
  52.1 64.9 %all-gather.3.cloned.1.call-start = ((), (), s32[]{:S(2)}) async-start(), calls=%async_computation.3 | async-start | bytes 2621440 | tf_op jit(solution)/shard_map/all_gather | solution.py:450
  79.7 185.8 %reduce-scatter.5.cloned.1.call-start = ((), (), s32[]{:S(2)}) async-start(), calls=%async_computation.4 | async-start | bytes 2621440 | tf_op jit(solution)/shard_map/reduce_scatter | solution.py:449
  205.8 1.6 copy-start.4
  224.2 1.0 copy-start.2
  235.1 30.6 %copy-start.3 = (f32[64,128]{1,0:T(8,128)S(1)}, f32[64,128]{1,0:T(8,128)}, u32[]{:S(2)}) copy-start(f32[64,128]{1,0:T(8,128)} %get-tuple-element.14) | copy-start | bytes 98308
  235.1 30.6 %copy-start.1 = (f32[64,8192]{1,0:T(8,128)S(1)}, f32[64,8192]{1,0:T(8,128)}, u32[]{:S(2)}) copy-start(f32[64,8192]{1,0:T(8,128)} %get-tuple-element.22) | copy-start | bytes 6291460
  235.1 67.5 %all-gather.5.cloned.1.call-start = ((), (), s32[]{:S(2)}) async-start(), calls=%async_computation.5 | async-start | bytes 2621440 | tf_op jit(solution)/shard_map/all_gather | solution.py:450
  298.8 7.4 %copy-start.5 = (f32[64,128]{1,0:T(8,128)S(1)}, f32[64,128]{1,0:T(8,128)}, u32[]{:S(2)}) copy-start(f32[64,128]{1,0:T(8,128)} %get-tuple-element.15) | copy-start | bytes 98308
Sparse Core Ops, SparseCore 0:
  52.2 27.4 reduce-scatter.2
  81.7 35.2 all-gather.2
  235.2 30.3 reduce-scatter.4
  267.3 35.2 all-gather.4

commit v15 on v14

--- a/solution.py
+++ b/solution.py
@@ -17,7 +17,7 @@
 FEAT = ("yl", "c")
 
 
-TILES_PER_STEP = 16
+TILES_PER_STEP = 32
 
 
 def forward_kernel(rows_ref, cols_ref, scale_ref, tiles_ref, operand_ref, out_ref):
@@ -28,7 +28,7 @@
     def _():
         out_ref[...] = jnp.zeros_like(out_ref)
 
-    for t in range(tiles_ref.shape[0]):
+    def tile(t, carry):
         b = step * tiles_ref.shape[0] + t
         picked = operand_ref[:, pl.ds(pl.multiple_of(cols_ref[b] * edge, edge), edge)]
         product = lax.dot_general(
@@ -36,6 +36,9 @@
         )
         target = pl.ds(pl.multiple_of(rows_ref[b] * edge, edge), edge)
         out_ref[:, target] = out_ref[:, target] + product * scale_ref[b]
+        return carry
+
+    lax.fori_loop(0, tiles_ref.shape[0], tile, 0, unroll=8)
 
 
 def backward_kernel(rows_ref, cols_ref, scale_ref, tiles_ref, operand_ref, out_ref):
@@ -46,12 +49,15 @@
     def _():
         out_ref[...] = jnp.zeros_like(out_ref)
 
-    for t in range(tiles_ref.shape[0]):
+    def tile(t, carry):
         b = step * tiles_ref.shape[0] + t
         picked = operand_ref[:, pl.ds(pl.multiple_of(rows_ref[b] * edge, edge), edge)]
         product = jnp.dot(picked, tiles_ref[t], preferred_element_type=jnp.float32) * scale_ref[b]
         target = pl.ds(pl.multiple_of(cols_ref[b] * edge, edge), edge)
         out_ref[:, target] = out_ref[:, target] + product
+        return carry
+
+    lax.fori_loop(0, tiles_ref.shape[0], tile, 0, unroll=8)
 
 
 def block_product(kernel, block_tiles, block_scale, row_index, col_index, operand, out_shape):

time: 411 us -> 408 us (level)
  no operation moved by 1% of the time
where the time goes in v15:
time: 408 us; the launch traced here: 405 us
  Pallas kernels  268 us (66%)
  waiting for transfers between devices  64.9 us (16%)
  matrix products  33.5 us (8%)
  local copies, waits for them, and re-layouts  19.1 us (5%)
  between operations  14 us (3%)
  other arithmetic  5.77 us (1%)
    pallas_call x5, Pallas kernels, group_sums(): pl.pallas_call(functools.partial(group_kernel, tuple(specs), tuple(factor...  127 us
    pallas_call x2, Pallas kernels, claim_halving(): pl.pallas_call(functools.partial(halving_kernel, stages, alternate, gathe...  110 us
    reduce_scatter x2, waiting for transfers between devices, row_step(): sums_t = lax.psum_scatter(partial_t, FEAT, scatter_dimension=1, tiled=True)  56.7 us
    pallas_call x4, Pallas kernels, block_product(): pl.pallas_call(kernel, grid_spec=grid_spec, out_shape=jax.ShapeDtypeStruc...  31.3 us
    dot_general x2, matrix products, row_step(): return (jnp.dot(inverse, wide_t, precision=HIGH), upper)  8.81 us
  transfers between devices with their start and end apart: 4, of which 4 were waited for; matrix products, arithmetic and copies ran while one was open for 1% of the time, Pallas kernels for 15%

profile of v15, /device:TPU:64, one launch (start us, length us, event | category | flops | bytes accessed | tf_op | source)
XLA Modules:
  0.0 405.4 jit_solution(16342047599525520789)
XLA Ops:
  7.2 3.5 convert_reduce_fusion
  14.1 25.3 %shard_map.76 = (f32[32,128]{1,0:T(8,128)}, f32[64,128]{1,0:T(8,128)}, f32[64,64]{1,0:T(8,128)}, f32[64,128]{1,0:T(8,128)}) custom-call(f32[32,128]{1,0:T(8,128)} %fusion.10.refs_0_, f32[64,128]{1,0:T(8,128)} %fusion.8.refs_1_, f32[64,64]{1,0:T(8,128)} %fusion.32.refs_2_), custom_call_target="tpu_custom_call" | custom-call | tf_op jit(solution)/shard_map/pallas_call | solution.py:266
  40.1 3.0 multiply_convert_fusion.3
  43.0 8.3 %shard_map.77 = f32[64,8192]{1,0:T(8,128)} custom-call(s32[128]{0:T(128)} %bitcast.56, s32[128]{0:T(128)} %bitcast.61, f32[128]{0:T(128)} %bitcast.50, bf16[128,128,128]{2,1,0:T(8,128)(2,1)} %bitcast.43, bf16[64,4096]{1,0:T(8,128)(2,1)} %get-tuple-element.19.operand_ref), custom_call_target="tpu_custom_call" | custom-call | flops 268435456 | bytes 6815744 | tf_op jit(solution)/shard_map/pallas_call | solution.py:77
  51.4 27.6 %reduce-scatter.3.cloned.1.call-done = f32[64,2048]{1,0:T(8,128)} async-done(((f32[64,8192]{1,0:T(8,128)}), f32[64,2048]{1,0:T(8,128)}) %reduce-scatter.3.cloned.1.call-update) | async-done | bytes 524304 | tf_op jit(solution)/shard_map/reduce_scatter | solution.py:455
  79.3 2.4 fusion.5.refs_0_
  81.7 30.2 %shard_map.78 = (f32[64,64]{1,0:T(8,128)}, f32[64,128]{1,0:T(8,128)}) custom-call(f32[64,64]{1,0:T(8,128)} %fusion.5.refs_0_), custom_call_target="tpu_custom_call" | custom-call | tf_op jit(solution)/shard_map/pallas_call | solution.py:266
  111.9 4.3 %all-gather.3.cloned.1.call-done = f32[64,8192]{1,0:T(8,128)} async-done(((f32[64,2048]{1,0:T(8,128)}), f32[64,8192]{1,0:T(8,128)}) %all-gather.3.cloned.1.call-update) | async-done | bytes 2097168 | tf_op jit(solution)/shard_map/all_gather | solution.py:456
  116.3 5.2 %multiply_convert_fusion.1 = (bf16[64,8192]{1,0:T(8,128)(2,1)}, f32[64,8192]{1,0:T(8,128)}) fusion(f32[8192]{0:T(1024)S(1)} %rsqrt_bitcast_fusion, f32[64,8192]{1,0:T(8,128)} %all-gather.3.cloned.1.call-done, f32[64,128]{1,0:T(8,128)} %get-tuple-element.13), kind=kOutput, calls=%fused_computation.6 | convolution fusion | flops 404226048 | bytes 5341184 | tf_op jit(solution)/shard_map/dot_general | solution.py:465
  121.5 7.2 %shard_map.79 = f32[64,4096]{1,0:T(8,128)} custom-call(s32[128]{0:T(128)} %bitcast.57, s32[128]{0:T(128)} %bitcast.62, f32[128]{0:T(128)} %bitcast.51, bf16[128,128,128]{2,1,0:T(8,128)(2,1)} %bitcast.44, bf16[64,8192]{1,0:T(8,128)(2,1)} %get-tuple-element.21.operand_ref), custom_call_target="tpu_custom_call" | custom-call | flops 268435456 | bytes 6291456 | tf_op jit(solution)/shard_map/pallas_call | solution.py:77
  128.7 1.8 copy.10
  131.9 70.7 %shard_map.80 = f32[2048,128]{1,0:T(8,128)} custom-call(f32[2048,128]{1,0:T(8,128)} %reshape.50.x_ref), custom_call_target="tpu_custom_call" | custom-call | tf_op jit(solution)/shard_map/pallas_call | solution.py:400
  202.6 1.6 reshape.51
  205.8 2.6 convolution_subtract_fusion.1
  208.4 1.6 fusion.33.refs_0_
  210.0 10.8 %shard_map.81 = (f32[64,64]{1,0:T(8,128)}, f32[64,128]{1,0:T(8,128)}) custom-call(f32[64,64]{1,0:T(8,128)} %fusion.33.refs_0_), custom_call_target="tpu_custom_call" | custom-call | tf_op jit(solution)/shard_map/pallas_call | solution.py:266
  220.8 1.8 fusion.17
  224.5 8.3 %shard_map.82 = f32[64,8192]{1,0:T(8,128)} custom-call(s32[128]{0:T(128)} %bitcast.58, s32[128]{0:T(128)} %bitcast.63, f32[128]{0:T(128)} %bitcast.52, bf16[128,128,128]{2,1,0:T(8,128)(2,1)} %bitcast.45, bf16[64,4096]{1,0:T(8,128)(2,1)} %fusion.3.operand_ref), custom_call_target="tpu_custom_call" | custom-call | flops 268435456 | bytes 6815744 | tf_op jit(solution)/shard_map/pallas_call | solution.py:77
  233.1 29.1 %reduce-scatter.5.cloned.1.call-done = f32[64,2048]{1,0:T(8,128)} async-done(((f32[64,8192]{1,0:T(8,128)}), f32[64,2048]{1,0:T(8,128)}) %reduce-scatter.5.cloned.1.call-update) | async-done | bytes 524304 | tf_op jit(solution)/shard_map/reduce_scatter | solution.py:455
  262.3 1.6 convolution_subtract_fusion.2
  265.1 30.2 %shard_map.83 = (f32[64,64]{1,0:T(8,128)}, f32[64,128]{1,0:T(8,128)}) custom-call(f32[64,64]{1,0:T(8,128)} %fusion.34.refs_0_), custom_call_target="tpu_custom_call" | custom-call | tf_op jit(solution)/shard_map/pallas_call | solution.py:266
  295.4 3.8 all-gather.5.cloned.1.call-done
  299.2 3.6 convolution_subtract_fusion
  302.8 3.6 multiply_convert_fusion
  306.4 7.5 %shard_map.84 = f32[64,4096]{1,0:T(8,128)} custom-call(s32[128]{0:T(128)} %bitcast.59, s32[128]{0:T(128)} %bitcast.64, f32[128]{0:T(128)} %bitcast.53, bf16[128,128,128]{2,1,0:T(8,128)(2,1)} %bitcast.46, bf16[64,8192]{1,0:T(8,128)(2,1)} %get-tuple-element.23.operand_ref), custom_call_target="tpu_custom_call" | custom-call | flops 268435456 | bytes 6291456 | tf_op jit(solution)/shard_map/pallas_call | solution.py:77
  313.9 2.8 reshape.52
  316.7 2.9 copy.12
  319.6 2.6 reshape_reshape.3.x_ref
  322.2 38.8 %shard_map.85 = f32[32,128]{1,0:T(8,128)} custom-call(f32[2048,128]{1,0:T(8,128)} %reshape_reshape.3.x_ref), custom_call_target="tpu_custom_call" | custom-call | tf_op jit(solution)/shard_map/pallas_call | solution.py:400
  363.8 30.1 %shard_map.86 = (f32[64,64]{1,0:T(8,128)}, f32[64,128]{1,0:T(8,128)}) custom-call(f32[64,64]{1,0:T(8,128)} %fusion.35.refs_0_), custom_call_target="tpu_custom_call" | custom-call | tf_op jit(solution)/shard_map/pallas_call | solution.py:266
  394.7 1.6 fusion.12
  396.3 1.9 dynamic-slice_bitcast_fusion
  (45 shorter events, 14.8 us)
Async XLA Ops:
  7.2 3.6 copy-start
  7.2 71.8 %reduce-scatter.3.cloned.1.call-start = ((), (), s32[]{:S(2)}) async-start(), calls=%async_computation.2 | async-start | bytes 2621440 | tf_op jit(solution)/shard_map/reduce_scatter | solution.py:455
  10.7 1.6 copy-start.7
  10.8 1.6 copy-start.8
  10.8 2.5 copy-start.9
  51.3 27.9 %copy-start.6 = (f32[64,128]{1,0:T(8,128)S(1)}, f32[64,128]{1,0:T(8,128)}, u32[]{:S(2)}) copy-start(f32[64,128]{1,0:T(8,128)} %get-tuple-element.10) | copy-start | bytes 98308
  51.4 64.9 %all-gather.3.cloned.1.call-start = ((), (), s32[]{:S(2)}) async-start(), calls=%async_computation.3 | async-start | bytes 2621440 | tf_op jit(solution)/shard_map/all_gather | solution.py:456
  79.0 183.1 %reduce-scatter.5.cloned.1.call-start = ((), (), s32[]{:S(2)}) async-start(), calls=%async_computation.4 | async-start | bytes 2621440 | tf_op jit(solution)/shard_map/reduce_scatter | solution.py:455
  204.2 1.6 copy-start.4
  222.6 1.0 copy-start.2
  232.8 29.5 %copy-start.3 = (f32[64,128]{1,0:T(8,128)S(1)}, f32[64,128]{1,0:T(8,128)}, u32[]{:S(2)}) copy-start(f32[64,128]{1,0:T(8,128)} %get-tuple-element.14) | copy-start | bytes 98308
  232.8 29.5 %copy-start.1 = (f32[64,8192]{1,0:T(8,128)S(1)}, f32[64,8192]{1,0:T(8,128)}, u32[]{:S(2)}) copy-start(f32[64,8192]{1,0:T(8,128)} %get-tuple-element.22) | copy-start | bytes 6291460
  232.8 66.4 %all-gather.5.cloned.1.call-start = ((), (), s32[]{:S(2)}) async-start(), calls=%async_computation.5 | async-start | bytes 2621440 | tf_op jit(solution)/shard_map/all_gather | solution.py:456
  295.3 7.5 %copy-start.5 = (f32[64,128]{1,0:T(8,128)S(1)}, f32[64,128]{1,0:T(8,128)}, u32[]{:S(2)}) copy-start(f32[64,128]{1,0:T(8,128)} %get-tuple-element.15) | copy-start | bytes 98308
Sparse Core Ops, SparseCore 0:
  51.5 27.4 reduce-scatter.2
  80.9 35.2 all-gather.2
  232.9 29.1 reduce-scatter.4
  263.8 35.3 all-gather.4
